TPU v7x, 32 devices: a whole 2x2x4 slice. The times are simulated.
32 devices in a mesh: mem: 2 (over y), col: 16 (over z, x, core).
Axes of the slice: x: 2, y: 2, z: 4, core: 2. Of those that a mesh axis runs over, the one named last changes fastest.
Arguments:
- perturbations: bfloat16 [4, 256, 256, 256], P(None, 'mem', 'col'), may hold values from -4 to 4
- loc_weights: float32 [7], replicated, may hold values from 0.3 to 1
- offsets: int32 [7, 2], replicated, may hold values from -4 to 4, as said below
- obs_x: int32 [32768], P('col'), may hold values from 0 to 255, as said below
- obs_y: int32 [32768], P('col'), may hold values from 0 to 255
- obs_t: int32 [32768], P('col'), may hold values from 0 to 3
- innovations: float32 [32768], P('col'), may hold values from -6 to 6
- obs_rinv: float32 [32768], P('col'), may hold values from 0.5 to 6
Outputs:
- control: float32 [256, 256, 256], P('mem', 'col')
- increment: float32 [4, 256, 256], P(None, 'col')
Inputs may be any that keep to these rules, and one draw needn't show every extreme that they name: `obs_x`: observation o lies in the columns (o // 2048) * 16 to (o // 2048) * 16 + 15. `offsets`: column 0 gives the offset along the first grid dimension, column 1 along the second; along the first both -4 and 4 occur.
All inputs are finite; a program needn't handle non-finite values.
Results may differ from a plain program's by a relative error of at most 0.00035.
Values may be sent and summed in bfloat16 or wider, within the bound.
No kernel may reach another device: no remote copies, remote signals or barrier semaphores. Data moves between devices by JAX's collectives and lax.ppermute only.
A program may use at most 64 MiB of HBM per device.

v0:
```python
import jax
import jax.numpy as jnp
from jax import lax
from jax.sharding import PartitionSpec as P

TAPS = 7
RADIUS = 4
ITERS = 3


def with_halo(block, sides, width):
    for axis, dim in sides:
        count = lax.axis_size(axis)
        forward = [(i, i + 1) for i in range(count - 1)]
        backward = [(target, source) for source, target in forward]
        low = lax.ppermute(
            lax.slice_in_dim(block, block.shape[dim] - width, None, axis=dim), axis, forward
        )
        high = lax.ppermute(lax.slice_in_dim(block, 0, width, axis=dim), axis, backward)
        block = jnp.concatenate([low, block, high], axis=dim)
    return block


def apply_taps(padded, loc_weights, offsets, mirror):
    length = padded.shape[1] - 2 * RADIUS
    summed = jnp.zeros((padded.shape[0], length, padded.shape[2]), jnp.float32)
    for tap_index in range(TAPS):
        along = offsets[tap_index, 0]
        across = offsets[tap_index, 1]
        if mirror:
            along = -along
            across = -across
        moved = lax.dynamic_slice_in_dim(padded, RADIUS + along, length, 1)
        summed = summed + loc_weights[tap_index] * jnp.roll(moved, -across, axis=2)
    return summed


def per_device(perturbations, loc_weights, offsets, obs_x, obs_y, obs_t, innovations, obs_rinv):
    levels, members, col_width, row_depth = perturbations.shape
    first_column = lax.axis_index("col") * col_width
    flat_index = (obs_t * col_width + (obs_x - first_column)) * row_depth + obs_y

    def spread(values):
        flat = jnp.zeros((levels * col_width * row_depth,), jnp.float32).at[flat_index].add(values)
        return flat.reshape(levels, col_width, row_depth)

    def combine(coeffs):
        return jnp.stack(
            [
                jnp.sum(perturbations[level].astype(jnp.float32) * coeffs, axis=0)
                for level in range(levels)
            ]
        )

    def forward(control):
        padded = with_halo(control, (("col", 1),), RADIUS)
        return combine(apply_taps(padded, loc_weights, offsets, False))

    def adjoint(values):
        weighted = spread(values)
        products = perturbations[0].astype(jnp.float32) * weighted[0][None]
        for level in range(1, levels):
            products = products + perturbations[level].astype(jnp.float32) * weighted[level][None]
        padded = with_halo(products, (("col", 1),), RADIUS)
        return apply_taps(padded, loc_weights, offsets, True)

    def squares(source):
        return lax.psum(jnp.sum(source * source), ("mem", "col"))

    gradient = adjoint(obs_rinv * innovations)
    control = jnp.zeros_like(gradient)
    residual = gradient
    direction = gradient
    norm_now = squares(residual)
    for turn_index in range(ITERS):
        final_turn = turn_index + 1 == ITERS
        partial_value = forward(direction).reshape(-1)[flat_index]
        inner_direction = direction
        observed, own_norm = lax.psum(
            (partial_value, jnp.sum(inner_direction * inner_direction)), "mem"
        )
        curvature = lax.psum(jnp.sum(obs_rinv * observed * observed) + own_norm, "col")
        if not final_turn:
            image = direction + adjoint(obs_rinv * observed)
        step_size = norm_now / curvature
        control = control + step_size * direction
        if not final_turn:
            residual = residual - step_size * image
            norm_next = squares(residual)
            direction = residual + norm_next / norm_now * direction
            norm_now = norm_next
    increment = lax.psum(forward(control), "mem")
    return (control, increment)


def solution(mesh):
    in_specs = (
        P(None, "mem", "col", None),
        P(),
        P(),
        P("col"),
        P("col"),
        P("col"),
        P("col"),
        P("col"),
    )
    out_specs = (P("mem", "col", None), P(None, "col", None))
    return jax.shard_map(
        per_device, mesh=mesh, in_specs=in_specs, out_specs=out_specs, check_vma=False
    )
```

profile of v0, /device:TPU:0, one launch (start us, length us, event | category | flops | bytes accessed | tf_op | source)
XLA Modules:
  0.0 647.9 jit_solution(5231806114973662985)
XLA Ops:
  8.7 11.3 %scatter_custom_fusion = f32[16384]{0:T(1024)S(1)} fusion(s32[2048]{0:T(1024)S(1)} %get-tuple-element.42, f32[2048]{0:T(1024)S(1)} %mul.452, f32[]{:T(128)} %constant.72.clone.1), kind=kCustom, calls=%fused_computation.379 | custom fusion | flops 2048 | bytes 65540 | tf_op jit(solution)/shard_map/scatter-add | solution.py:44
  20.0 2.4 fusion.181
  22.5 1.5 fusion.148
  24.5 1.2 copy-done.18
  25.8 2.4 collective-permute-start
  28.2 1.3 collective-permute-start.1
  49.0 2.1 pad_maximum_fusion
  51.1 5.4 constant_dynamic-slice_fusion.48
  56.5 16.9 %multiply_reduce_fusion.4 = (f32[]{:T(128)}, f32[128,16,256]{2,0,1:T(8,128)S(1)}) fusion(s32[]{:T(128)S(6)} %select_n.219, f32[128,16,256]{2,0,1:T(8,128)} %get-tuple-element.90, f32[]{:T(128)} %bitcast.28, s32[]{:T(128)S(6)} %select_n.217, f32[128,16,256]{2,0,1:T(8,128)} %get-tuple-element.91, f32[]{:T(128)} %bitcast.24, s32[]{:T(128)S(6)} %select_n.215, ...), kind=kLoop, calls=%fused_computation.317 | loop fusion | flops 11534335 | bytes 16777276 | tf_op jit(solution)/shard_map/reduce_sum | solution.py:68
  73.4 1.3 copy-done.10
  74.8 5.1 collective-permute-start.2
  79.9 1.5 collective-permute-start.3
  95.6 2.1 pad_maximum_fusion.1
  97.7 5.3 constant_dynamic-slice_fusion.41
  103.0 17.0 %fusion.149 = (f32[16,256]{1,0:T(8,128)S(1)}, f32[16,256]{1,0:T(8,128)S(1)}, f32[16,256]{1,0:T(8,128)S(1)}, f32[16,256]{1,0:T(8,128)S(1)}) fusion(bf16[1,128,16,256]{3,2,1,0:T(8,128)(2,1)} %copy-done.9, bf16[1,128,16,256]{3,2,1,0:T(8,128)(2,1)} %copy-done, bf16[1,128,16,256]{3,2,1,0:T(8,128)(2,1)} %copy-done.3, bf16[1,128,16,256]{3,2,1,0:T(8,128)(2,1)} %copy-done.6, ...), kind=kLoop, calls=%fused_computation.288 | loop fusion | flops 16760832 | bytes 18939960 | tf_op jit(solution)/shard_map/reduce_sum | solution.py:50
  120.1 11.8 %gather_fusion = f32[2048]{0:T(1024)S(1)} fusion(f32[16384]{0:T(1024)S(1)} %bitcast.132, s32[2048]{0:T(1024)S(1)} %get-tuple-element.41), kind=kCustom, calls=%fused_computation | custom fusion | bytes 24576 | tf_op jit(solution)/shard_map/gather | solution.py:77
  131.9 5.6 all-reduce.2
  138.2 11.3 %scatter_custom_fusion.1 = f32[16384]{0:T(1024)S(1)} fusion(s32[2048]{0:T(1024)S(1)} %get-tuple-element.42, f32[2048]{0:T(1024)S(1)} %get-tuple-element.38, f32[]{:T(128)} %constant.72.clone.1), kind=kCustom, calls=%fused_computation.377 | custom fusion | flops 2048 | bytes 65540 | tf_op jit(solution)/shard_map/scatter-add | solution.py:44
  149.6 2.7 fusion.152
  152.3 1.3 copy-done.19
  153.7 3.1 collective-permute-start.4
  156.8 1.3 collective-permute-start.5
  159.4 50.1 %psum.91 = f32[]{:T(128)} all-reduce(f32[]{:T(128)} %get-tuple-element.39), channel_id=1, replica_groups=mesh['mem'=2,'col'=16] {'mem','col'}, use_global_device_ids=true, to_apply=%region_2.4 | all-reduce | flops 1 | bytes 8 | tf_op jit(solution)/shard_map/psum | solution.py:68
  209.5 31.5 %psum.94 = f32[]{:T(128)} all-reduce(f32[]{:T(128)S(6)} %add.574), channel_id=1, replica_groups=mesh['mem'=2,'col'=16] {'col'}, use_global_device_ids=true, to_apply=%region_10.12 | all-reduce | flops 1 | bytes 8 | tf_op jit(solution)/shard_map/psum | solution.py:82
  243.1 2.1 pad_maximum_fusion.2
  245.2 5.4 constant_dynamic-slice_fusion.34
  250.7 18.1 %multiply_reduce_fusion.3 = (f32[]{:T(128)}, f32[128,16,256]{2,0,1:T(8,128)}) fusion(f32[128,16,256]{2,0,1:T(8,128)} %copy-done.10, s32[]{:T(128)S(6)} %select_n.219, f32[128,16,256]{2,0,1:T(8,128)} %get-tuple-element.76, f32[]{:T(128)} %bitcast.28, s32[]{:T(128)S(6)} %select_n.217, f32[128,16,256]{2,0,1:T(8,128)} %get-tuple-element.77, f32[]{:T(128)} %bitcast.24, ...), kind=kLoop, calls=%fused_computation.316 | loop fusion | flops 13107199 | bytes 18874432 | tf_op jit(solution)/shard_map/reduce_sum | solution.py:68
  268.7 37.0 %psum.95 = f32[]{:T(128)} all-reduce(f32[]{:T(128)} %get-tuple-element.35), channel_id=1, replica_groups=mesh['mem'=2,'col'=16] {'mem','col'}, use_global_device_ids=true, to_apply=%region_13.15 | all-reduce | flops 1 | bytes 8 | tf_op jit(solution)/shard_map/psum | solution.py:68
  307.0 2.7 multiply_reduce_fusion.2
  309.9 1.3 collective-permute-start.6
  311.2 1.5 collective-permute-start.7
  312.7 4.8 collective-permute-done.7
  317.8 5.5 constant_dynamic-slice_fusion.27
  323.2 17.1 %fusion.153 = (f32[16,256]{1,0:T(8,128)S(1)}, f32[16,256]{1,0:T(8,128)S(1)}, f32[16,256]{1,0:T(8,128)S(1)}, f32[16,256]{1,0:T(8,128)S(1)}) fusion(bf16[1,128,16,256]{3,2,1,0:T(8,128)(2,1)} %copy-done.9, bf16[1,128,16,256]{3,2,1,0:T(8,128)(2,1)} %copy-done, bf16[1,128,16,256]{3,2,1,0:T(8,128)(2,1)} %copy-done.3, bf16[1,128,16,256]{3,2,1,0:T(8,128)(2,1)} %copy-done.6, ...), kind=kLoop, calls=%fused_computation.292 | loop fusion | flops 16760832 | bytes 18939960 | tf_op jit(solution)/shard_map/reduce_sum | solution.py:50
  340.4 11.8 %gather_fusion.1 = f32[2048]{0:T(1024)S(1)} fusion(f32[16384]{0:T(1024)S(1)} %bitcast.134, s32[2048]{0:T(1024)S(1)} %get-tuple-element.41), kind=kCustom, calls=%fused_computation.1 | custom fusion | bytes 24576 | tf_op jit(solution)/shard_map/gather | solution.py:77
  352.2 5.7 all-reduce.1
  358.6 11.3 %scatter_custom_fusion.2 = f32[16384]{0:T(1024)S(1)} fusion(s32[2048]{0:T(1024)S(1)} %get-tuple-element.42, f32[2048]{0:T(1024)S(1)} %get-tuple-element.32, f32[]{:T(128)} %constant.72.clone.1), kind=kCustom, calls=%fused_computation.375 | custom fusion | flops 2048 | bytes 65540 | tf_op jit(solution)/shard_map/scatter-add | solution.py:44
  370.0 2.7 fusion.156
  372.7 1.3 copy-done.20
  374.1 9.2 %collective-permute-start.8 = (f32[128,4,256]{2,0,1:T(8,128)S(1)}, f32[128,4,256]{2,0,1:T(8,128)S(1)}, u32[]{:S(2)}, u32[]{:S(2)}) collective-permute-start(f32[128,4,256]{2,0,1:T(8,128)S(1)} %get-tuple-element.100), channel_id=1, source_target_pairs={{0,1},{1,2},{2,3},{3,4},{4,5},{5,6},{6,7},{7,8},{8,9},{9,10},{10,1... | collective-permute-start | bytes 1572872 | tf_op jit(solution)/shard_map/ppermute | solution.py:16
  383.3 1.3 collective-permute-start.9
  385.9 35.6 %psum.98 = f32[]{:T(128)} all-reduce(f32[]{:T(128)S(6)} %add.592), channel_id=1, replica_groups=mesh['mem'=2,'col'=16] {'col'}, use_global_device_ids=true, to_apply=%region_22.24 | all-reduce | flops 1 | bytes 8 | tf_op jit(solution)/shard_map/psum | solution.py:82
  423.7 2.1 pad_maximum_fusion.4
  425.8 5.4 constant_dynamic-slice_fusion.20
  431.2 18.5 %multiply_reduce_fusion.1 = (f32[]{:T(128)}, f32[128,16,256]{2,0,1:T(8,128)}) fusion(f32[128,16,256]{2,0,1:T(8,128)} %get-tuple-element.36, f32[128,16,256]{2,0,1:T(8,128)} %copy-done.13, s32[]{:T(128)S(6)} %select_n.219, f32[128,16,256]{2,0,1:T(8,128)} %get-tuple-element.62, f32[]{:T(128)} %bitcast.28, s32[]{:T(128)S(6)} %select_n.217, ...), kind=kLoop, calls=%fused_computation.313 | loop fusion | flops 13107199 | bytes 20971584 | tf_op jit(solution)/shard_map/reduce_sum | solution.py:68
  449.7 37.1 %psum.99 = f32[]{:T(128)} all-reduce(f32[]{:T(128)} %get-tuple-element.29), channel_id=1, replica_groups=mesh['mem'=2,'col'=16] {'mem','col'}, use_global_device_ids=true, to_apply=%region_25.27 | all-reduce | flops 1 | bytes 8 | tf_op jit(solution)/shard_map/psum | solution.py:68
  488.1 2.8 multiply_reduce_fusion
  490.9 1.3 collective-permute-start.10
  492.3 1.5 collective-permute-start.11
  493.8 4.7 collective-permute-done.11
  498.8 5.5 constant_dynamic-slice_fusion.13
  504.3 17.1 %fusion.157 = (f32[16,256]{1,0:T(8,128)S(1)}, f32[16,256]{1,0:T(8,128)S(1)}, f32[16,256]{1,0:T(8,128)S(1)}, f32[16,256]{1,0:T(8,128)S(1)}) fusion(bf16[1,128,16,256]{3,2,1,0:T(8,128)(2,1)} %copy-done.9, bf16[1,128,16,256]{3,2,1,0:T(8,128)(2,1)} %copy-done, bf16[1,128,16,256]{3,2,1,0:T(8,128)(2,1)} %copy-done.3, bf16[1,128,16,256]{3,2,1,0:T(8,128)(2,1)} %copy-done.6, ...), kind=kLoop, calls=%fused_computation.296 | loop fusion | flops 16760832 | bytes 18939960 | tf_op jit(solution)/shard_map/reduce_sum | solution.py:50
  521.5 11.8 %gather_fusion.2 = f32[2048]{0:T(1024)S(1)} fusion(f32[16384]{0:T(1024)S(1)} %bitcast.133, s32[2048]{0:T(1024)S(1)} %get-tuple-element.41), kind=kCustom, calls=%fused_computation.2 | custom fusion | bytes 24576 | tf_op jit(solution)/shard_map/gather | solution.py:77
  533.3 5.7 all-reduce
  540.7 37.1 %psum.102 = f32[]{:T(128)} all-reduce(f32[]{:T(128)S(6)} %add.611), channel_id=1, replica_groups=mesh['mem'=2,'col'=16] {'col'}, use_global_device_ids=true, to_apply=%region_34.36 | all-reduce | flops 1 | bytes 8 | tf_op jit(solution)/shard_map/psum | solution.py:82
  579.1 2.7 multiply_add_fusion
  581.9 1.4 collective-permute-start.12
  583.4 1.6 collective-permute-start.13
  585.0 2.2 collective-permute-done.13
  587.4 5.3 constant_dynamic-slice_fusion.6
  592.8 17.1 %fusion.158 = (f32[16,256]{1,0:T(8,128)S(1)}, f32[16,256]{1,0:T(8,128)S(1)}, f32[16,256]{1,0:T(8,128)S(1)}, f32[16,256]{1,0:T(8,128)S(1)}) fusion(bf16[1,128,16,256]{3,2,1,0:T(8,128)(2,1)} %copy-done.9, bf16[1,128,16,256]{3,2,1,0:T(8,128)(2,1)} %copy-done, bf16[1,128,16,256]{3,2,1,0:T(8,128)(2,1)} %copy-done.3, bf16[1,128,16,256]{3,2,1,0:T(8,128)(2,1)} %copy-done.6, ...), kind=kLoop, calls=%fused_computation.297 | loop fusion | flops 16760832 | bytes 18939960 | tf_op jit(solution)/shard_map/reduce_sum | solution.py:50
  610.6 2.5 copy.14
  613.1 26.0 %all-reduce.5.cloned.1.call-done = f32[4,16,256]{2,1,0:T(8,128)} async-done(((f32[4,16,256]{2,1,0:T(8,128)}), f32[4,16,256]{2,1,0:T(8,128)}) %all-reduce.5.cloned.1.call-update) | async-done | bytes 65552 | tf_op jit(solution)/shard_map/psum | solution.py:92
  639.1 1.5 copy.83
  (104 shorter events, 10.8 us)
Async XLA Ops:
  7.2 631.9 %all-reduce.5.cloned.1.call-start = ((), (), s32[]{:S(2)}) async-start(), calls=%async_computation | async-start | bytes 131072 | tf_op jit(solution)/shard_map/psum | solution.py:92
  22.5 1.5 copy-start
  22.5 1.5 copy-start.3
  22.5 1.6 copy-start.6
  22.5 1.9 copy-start.9
  24.4 1.3 copy-start.18
  24.4 5.0 copy-start.26
  24.5 23.0 %copy-start.27 = (f32[7]{0:T(128)S(1)}, f32[7]{0:T(128)}, u32[]{:S(2)}) copy-start(f32[7]{0:T(128)} %param.11) | copy-start | bytes 88
  25.8 22.4 %collective-permute-start = (f32[128,4,256]{2,0,1:T(8,128)S(1)}, f32[128,4,256]{2,0,1:T(8,128)S(1)}, u32[]{:S(2)}, u32[]{:S(2)}) collective-permute-start(f32[128,4,256]{2,0,1:T(8,128)S(1)} %get-tuple-element.108), channel_id=1, source_target_pairs={{0,1},{1,2},{2,3},{3,4},{4,5},{5,6},{6,7},{7,8},{8,9},{9,10},{10,1... | collective-permute-start | bytes 1572872 | tf_op jit(solution)/shard_map/ppermute | solution.py:16
  28.2 20.8 %collective-permute-start.1 = (f32[128,4,256]{2,0,1:T(8,128)S(1)}, f32[128,4,256]{2,0,1:T(8,128)}, u32[]{:S(2)}, u32[]{:S(2)}) collective-permute-start(f32[128,4,256]{2,0,1:T(8,128)S(1)} %get-tuple-element.109), channel_id=1, source_target_pairs={{1,0},{2,1},{3,2},{4,3},{5,4},{6,5},{7,6},{8,7},{9,8},{10,9},{11,1... | collective-permute-start | bytes 1572872 | tf_op jit(solution)/shard_map/ppermute | solution.py:19
  48.2 0.8 copy-start.21
  73.4 1.3 copy-start.10
  74.8 20.0 %collective-permute-start.2 = (f32[128,4,256]{2,0,1:T(8,128)S(1)}, f32[128,4,256]{2,0,1:T(8,128)S(1)}, u32[]{:S(2)}, u32[]{:S(2)}) collective-permute-start(f32[128,4,256]{2,0,1:T(8,128)S(1)} %get-tuple-element.106), channel_id=1, source_target_pairs={{0,1},{1,2},{2,3},{3,4},{4,5},{5,6},{6,7},{7,8},{8,9},{9,10},{10,1... | collective-permute-start | bytes 1572872 | tf_op jit(solution)/shard_map/ppermute | solution.py:16
  79.9 15.7 %collective-permute-start.3 = (f32[128,4,256]{2,0,1:T(8,128)S(1)}, f32[128,4,256]{2,0,1:T(8,128)}, u32[]{:S(2)}, u32[]{:S(2)}) collective-permute-start(f32[128,4,256]{2,0,1:T(8,128)S(1)} %get-tuple-element.107), channel_id=1, source_target_pairs={{1,0},{2,1},{3,2},{4,3},{5,4},{6,5},{7,6},{8,7},{9,8},{10,9},{11,1... | collective-permute-start | bytes 1572872 | tf_op jit(solution)/shard_map/ppermute | solution.py:19
  94.8 0.8 copy-start.22
  120.1 17.4 %copy-start.25 = (f32[2048]{0:T(1024)S(1)}, f32[2048]{0:T(1024)}, u32[]{:S(2)}) copy-start(f32[2048]{0:T(1024)} %param.17) | copy-start | bytes 24580
  120.1 29.4 %copy-start.1 = (bf16[1,128,16,256]{3,2,1,0:T(8,128)(2,1)S(1)}, bf16[1,128,16,256]{3,2,1,0:T(8,128)(2,1)}, u32[]{:S(2)}) copy-start(bf16[1,128,16,256]{3,2,1,0:T(8,128)(2,1)} %copy-done) | copy-start | bytes 3145732
  120.1 29.4 %copy-start.4 = (bf16[1,128,16,256]{3,2,1,0:T(8,128)(2,1)S(1)}, bf16[1,128,16,256]{3,2,1,0:T(8,128)(2,1)}, u32[]{:S(2)}) copy-start(bf16[1,128,16,256]{3,2,1,0:T(8,128)(2,1)} %copy-done.3) | copy-start | bytes 3145732
  120.1 29.4 %copy-start.7 = (bf16[1,128,16,256]{3,2,1,0:T(8,128)(2,1)S(1)}, bf16[1,128,16,256]{3,2,1,0:T(8,128)(2,1)}, u32[]{:S(2)}) copy-start(bf16[1,128,16,256]{3,2,1,0:T(8,128)(2,1)} %copy-done.6) | copy-start | bytes 3145732
  152.3 1.4 copy-start.19
  153.7 88.6 %collective-permute-start.4 = (f32[128,4,256]{2,0,1:T(8,128)S(1)}, f32[128,4,256]{2,0,1:T(8,128)S(1)}, u32[]{:S(2)}, u32[]{:S(2)}) collective-permute-start(f32[128,4,256]{2,0,1:T(8,128)S(1)} %get-tuple-element.104), channel_id=1, source_target_pairs={{0,1},{1,2},{2,3},{3,4},{4,5},{5,6},{6,7},{7,8},{8,9},{9,10},{10,1... | collective-permute-start | bytes 1572872 | tf_op jit(solution)/shard_map/ppermute | solution.py:16
  156.8 86.3 %collective-permute-start.5 = (f32[128,4,256]{2,0,1:T(8,128)S(1)}, f32[128,4,256]{2,0,1:T(8,128)}, u32[]{:S(2)}, u32[]{:S(2)}) collective-permute-start(f32[128,4,256]{2,0,1:T(8,128)S(1)} %get-tuple-element.105), channel_id=1, source_target_pairs={{1,0},{2,1},{3,2},{4,3},{5,4},{6,5},{7,6},{8,7},{9,8},{10,9},{11,1... | collective-permute-start | bytes 1572872 | tf_op jit(solution)/shard_map/ppermute | solution.py:19
  242.3 0.8 copy-start.23
  250.7 56.4 %copy-start.11 = (f32[128,16,256]{2,0,1:T(8,128)S(1)}, f32[128,16,256]{2,0,1:T(8,128)}, u32[]{:S(2)}) copy-start(f32[128,16,256]{2,0,1:T(8,128)} %copy-done.10) | copy-start | bytes 6291460
  309.8 7.7 %copy-start.13 = (f32[128,16,256]{2,0,1:T(8,128)}, f32[128,16,256]{2,0,1:T(8,128)S(1)}, u32[]{:S(2)}) copy-start(f32[128,16,256]{2,0,1:T(8,128)S(1)} %get-tuple-element.34) | copy-start | bytes 6291460
  309.9 2.8 collective-permute-start.6
  311.2 6.3 collective-permute-start.7
  340.4 29.6 %copy-start.2 = (bf16[1,128,16,256]{3,2,1,0:T(8,128)(2,1)S(1)}, bf16[1,128,16,256]{3,2,1,0:T(8,128)(2,1)}, u32[]{:S(2)}) copy-start(bf16[1,128,16,256]{3,2,1,0:T(8,128)(2,1)} %copy-done) | copy-start | bytes 3145732
  340.4 29.6 %copy-start.5 = (bf16[1,128,16,256]{3,2,1,0:T(8,128)(2,1)S(1)}, bf16[1,128,16,256]{3,2,1,0:T(8,128)(2,1)}, u32[]{:S(2)}) copy-start(bf16[1,128,16,256]{3,2,1,0:T(8,128)(2,1)} %copy-done.3) | copy-start | bytes 3145732
  340.4 29.6 %copy-start.8 = (bf16[1,128,16,256]{3,2,1,0:T(8,128)(2,1)S(1)}, bf16[1,128,16,256]{3,2,1,0:T(8,128)(2,1)}, u32[]{:S(2)}) copy-start(bf16[1,128,16,256]{3,2,1,0:T(8,128)(2,1)} %copy-done.6) | copy-start | bytes 3145732
  372.7 1.3 copy-start.20
  374.1 48.8 %collective-permute-start.8 = (f32[128,4,256]{2,0,1:T(8,128)S(1)}, f32[128,4,256]{2,0,1:T(8,128)S(1)}, u32[]{:S(2)}, u32[]{:S(2)}) collective-permute-start(f32[128,4,256]{2,0,1:T(8,128)S(1)} %get-tuple-element.100), channel_id=1, source_target_pairs={{0,1},{1,2},{2,3},{3,4},{4,5},{5,6},{6,7},{7,8},{8,9},{9,10},{10,1... | collective-permute-start | bytes 1572872 | tf_op jit(solution)/shard_map/ppermute | solution.py:16
  383.3 40.4 %collective-permute-start.9 = (f32[128,4,256]{2,0,1:T(8,128)S(1)}, f32[128,4,256]{2,0,1:T(8,128)}, u32[]{:S(2)}, u32[]{:S(2)}) collective-permute-start(f32[128,4,256]{2,0,1:T(8,128)S(1)} %get-tuple-element.101), channel_id=1, source_target_pairs={{1,0},{2,1},{3,2},{4,3},{5,4},{6,5},{7,6},{8,7},{9,8},{10,9},{11,1... | collective-permute-start | bytes 1572872 | tf_op jit(solution)/shard_map/ppermute | solution.py:19
  422.9 0.8 copy-start.24
  431.2 56.9 %copy-start.14 = (f32[128,16,256]{2,0,1:T(8,128)S(1)}, f32[128,16,256]{2,0,1:T(8,128)}, u32[]{:S(2)}) copy-start(f32[128,16,256]{2,0,1:T(8,128)} %copy-done.13) | copy-start | bytes 6291460
  490.8 7.7 %copy-start.17 = (f32[128,16,256]{2,0,1:T(8,128)}, f32[128,16,256]{2,0,1:T(8,128)S(1)}, u32[]{:S(2)}) copy-start(f32[128,16,256]{2,0,1:T(8,128)S(1)} %get-tuple-element.28) | copy-start | bytes 6291460
  490.9 2.9 collective-permute-start.10
  492.3 6.3 collective-permute-start.11
  521.5 57.7 %copy-start.12 = (f32[128,16,256]{2,0,1:T(8,128)S(1)}, f32[128,16,256]{2,0,1:T(8,128)}, u32[]{:S(2)}) copy-start(f32[128,16,256]{2,0,1:T(8,128)} %copy-done.10) | copy-start | bytes 6291460
  581.8 5.4 copy-start.15
  581.9 3.0 collective-permute-start.12
  583.4 3.8 collective-permute-start.13
  592.8 17.8 %copy-start.16 = (f32[128,16,256]{2,0,1:T(8,128)S(1)}, f32[128,16,256]{2,0,1:T(8,128)}, u32[]{:S(2)}) copy-start(f32[128,16,256]{2,0,1:T(8,128)} %copy-done.15) | copy-start | bytes 6291460
Sparse Core Ops, SparseCore 0:
  610.7 28.3 all-reduce.4
where the time goes:
time: 657 us; the launch traced here: 648 us
  blocking collectives  245 us (37%)
  other arithmetic  184 us (28%)
  local copies, waits for them, and re-layouts  90.8 us (14%)
  between operations  56.3 us (9%)
  waiting for transfers between devices  37.7 us (6%)
  starting transfers between devices  34 us (5%)
    psum x3, blocking collectives, squares(): return lax.psum(jnp.sum(source * source), ('mem', 'col'))  124 us
    psum x3, blocking collectives, per_device(): lax.psum(jnp.sum(obs_rinv * observed * observed) + own_norm, 'col')  104 us
    reduce_sum x4, other arithmetic, combine(): jnp.sum(perturbations[level].astype(jnp.float32) * coeffs, axis=0)  68.3 us
    reduce_sum x3, other arithmetic, squares(): return lax.psum(jnp.sum(source * source), ('mem', 'col'))  53.4 us
    dynamic_slice x7, local copies, waits for them, and re-layouts, apply_taps(): moved = lax.dynamic_slice_in_dim(padded, RADIUS + along, length, 1)  37.9 us
    gather x3, local copies, waits for them, and re-layouts, per_device(): partial_value = forward(direction).reshape(-1)[flat_index]  35.3 us
    scatter-add x3, other arithmetic, spread(): jnp.zeros((levels * col_width * row_depth,), jnp.float32).at[flat_index]  33.8 us
    psum x1, waiting for transfers between devices, per_device(): increment = lax.psum(forward(control), 'mem')  26 us
  transfers between devices with their start and end apart: 15, of which 4 were waited for; matrix products, arithmetic and copies ran while one was open for 1% of the time, Pallas kernels for 0%

commit v1 on v0

v1 whole, which is shorter than its diff:
```python
import functools

import jax
import jax.numpy as jnp
from jax import lax
from jax.experimental import pallas as pl
from jax.experimental.pallas import tpu as pltpu
from jax.sharding import PartitionSpec as P

RADIUS = 4
SCALE = 2.0**-12
TINY = 3e-8
GROUP = 4
LANES = 128
SMEM = pltpu.MemorySpace.SMEM
VMEM = pltpu.MemorySpace.VMEM


def split3(v):
    hi = v.astype(jnp.bfloat16)
    rest = v - hi.astype(jnp.float32)
    mid = rest.astype(jnp.bfloat16)
    low = (rest - mid.astype(jnp.float32)).astype(jnp.bfloat16)
    return hi, mid, low


def obs_kernel(place_ref, ox_ref, oy_ref, ot_ref, inno_ref, rinv_ref, field_ref, a_ref, b_ref):
    _, levels, width, depth = field_ref.shape
    cells = levels * width
    count = ox_ref.shape[1]
    first, parity = place_ref[0], place_ref[1]
    row = ot_ref[...] * width + ox_ref[...] - first
    hit = lax.broadcasted_iota(jnp.int32, (cells, count), 0) == row
    rinv = rinv_ref[...]
    pieces = split3(rinv) + split3(rinv * inno_ref[...])
    left = jnp.concatenate(
        [jnp.where(hit, piece.astype(jnp.float32), 0.0).astype(jnp.bfloat16) for piece in pieces], axis=0
    )
    right = (lax.broadcasted_iota(jnp.int32, (depth, count), 0) == oy_ref[...]).astype(jnp.float32)
    out = lax.dot_general(
        left, right.astype(jnp.bfloat16), (((1,), (1,)), ((), ())), preferred_element_type=jnp.float32
    )
    for field in range(2):
        base = 3 * field * cells
        total = out[base : base + cells] + (
            out[base + cells : base + 2 * cells] + out[base + 2 * cells : base + 3 * cells]
        )
        field_ref[field] = total.reshape(levels, width, depth)
    low = field_ref[:, :, 0:RADIUS, :]
    high = field_ref[:, :, width - RADIUS :, :]
    even = parity == 0
    a_ref[...] = jnp.where(even, high, low)
    b_ref[...] = jnp.where(even, low, high)


def mid_kernel(place_ref, f_ref, r_ref, m_ref, a_ref, b_ref):
    even = place_ref[1] == 0
    width = f_ref.shape[1] - 2 * RADIUS
    total = f_ref[...] + r_ref[...]
    m_ref[...] = total
    right = total[:, width - RADIUS : width + RADIUS]
    left = jnp.concatenate([total[:, width + RADIUS :], total[:, :RADIUS]], axis=1)
    a_ref[...] = jnp.where(even, right, left)
    b_ref[...] = jnp.where(even, left, right)


def finish_field(even, total, from_a, from_b):
    width = total.shape[1] - 2 * RADIUS
    right = jnp.where(even, from_a, from_b)
    left = jnp.where(even, from_b, from_a)
    rest = jnp.zeros((total.shape[0], width - 2 * RADIUS, total.shape[2]), jnp.float32)
    return total + jnp.concatenate([left[:, RADIUS:], rest, right, left[:, :RADIUS]], axis=1)


def fold(values):
    levels, width, depth = values.shape
    total = jnp.zeros((8, LANES), jnp.float32)
    for level in range(levels):
        for row in range(0, width, 8):
            for lane in range(0, depth, LANES):
                total = total + values[level, row : row + 8, lane : lane + LANES]
    return total


def apply_core(weight_ref, offset_ref, p_ref, h_ref, w_ref, t_ref, f_ref, prod_ref, mid_ref):
    levels, block, width, depth = p_ref.shape
    taps = weight_ref.shape[0]
    halves = [slice(i * LANES, (i + 1) * LANES) for i in range(2)]
    ext = width + 2 * RADIUS
    lane = lax.broadcasted_iota(jnp.int32, (8, LANES), 1)

    def shifted(ref, slot, start, rows, across):
        shift = across & (LANES - 1)
        swap = (across < 0).astype(jnp.int32)
        first = pltpu.roll(ref[slot, swap, pl.ds(start, rows), :], shift, 1)
        second = pltpu.roll(ref[slot, 1 - swap, pl.ds(start, rows), :], shift, 1)
        wrap = jnp.broadcast_to((lane < shift)[None], (rows // 8, 8, LANES)).reshape(rows, LANES)
        return jnp.where(wrap, second, first), jnp.where(wrap, first, second)

    def group(step, carry):
        base = step * GROUP
        for slot in range(GROUP):
            k = base + slot
            for i, half in enumerate(halves):
                own = sum(p_ref[l, k, :, half].astype(jnp.float32) * w_ref[l, 0:width, half] for l in range(levels))
                edge = sum(h_ref[l, k, :, half].astype(jnp.float32) * w_ref[l, width:ext, half] for l in range(levels))
                prod_ref[slot, i, 0:8, :] = edge
                prod_ref[slot, i, 8 : 8 + width, :] = own
                prod_ref[slot, i, 8 + width : 16 + width, :] = edge
        for slot in range(GROUP):
            k = base + slot
            total = [jnp.zeros((width, LANES), jnp.float32)] * 2
            for s in range(taps):
                got = shifted(prod_ref, slot, 8 - offset_ref[s, 0], width, offset_ref[s, 1])
                total = [old + weight_ref[s] * new for old, new in zip(total, got)]
            for i, half in enumerate(halves):
                t_ref[k, :, half] = total[i]
                mid_ref[slot, i, 8 : 8 + width, :] = total[i]
                mid_ref[slot, i, 16 + width : 24 + width, :] = total[i][0:8]
        moved = []
        for slot in range(GROUP):
            total = [jnp.zeros((ext, LANES), jnp.float32)] * 2
            for s in range(taps):
                got = shifted(mid_ref, slot, 8 + offset_ref[s, 0], ext, -offset_ref[s, 1])
                total = [old + weight_ref[s] * new for old, new in zip(total, got)]
            moved.append(total)
        for l in range(levels):
            for i, half in enumerate(halves):
                f_ref[l, 0:width, half] += sum(
                    p_ref[l, base + slot, :, half].astype(jnp.float32) * moved[slot][i][0:width]
                    for slot in range(GROUP)
                )
                f_ref[l, width:ext, half] += sum(
                    h_ref[l, base + slot, :, half].astype(jnp.float32) * moved[slot][i][width:]
                    for slot in range(GROUP)
                )
        return carry

    lax.fori_loop(0, block // GROUP, group, 0)


def first_kernel(
    weight_ref, offset_ref, p_ref, h_ref, w_ref, t_ref, f_ref, prod_ref, mid_ref
):
    @pl.when(pl.program_id(0) == 0)
    def _():
        f_ref[...] = jnp.zeros_like(f_ref)
        mid_ref[...] = jnp.zeros_like(mid_ref)

    apply_core(weight_ref, offset_ref, p_ref, h_ref, w_ref, t_ref, f_ref, prod_ref, mid_ref)


def next_kernel(
    weight_ref, offset_ref, place_ref, p_ref, h_ref, m_ref, a_ref, b_ref, d_ref, old_ref,
    t_ref, f_ref, done_ref, w_ref, moment_ref, prod_ref, mid_ref,
):
    @pl.when(pl.program_id(0) == 0)
    def _():
        f_ref[...] = jnp.zeros_like(f_ref)
        mid_ref[...] = jnp.zeros_like(mid_ref)
        finish(place_ref, m_ref, a_ref, b_ref, d_ref, old_ref, done_ref, w_ref, moment_ref)

    apply_core(weight_ref, offset_ref, p_ref, h_ref, w_ref, t_ref, f_ref, prod_ref, mid_ref)


def finish(place_ref, m_ref, a_ref, b_ref, d_ref, old_ref, done_ref, w_ref, moment_ref):
    width = done_ref.shape[1]
    field = finish_field(place_ref[1] == 0, m_ref[...], a_ref[...], b_ref[...])
    fresh = field * d_ref[...] * SCALE
    w_ref[...] = fresh
    done_ref[...] = field[:, :width]
    moment_ref[0] = fold(field[:, :width] * old_ref[:, :width, :])
    moment_ref[1] = fold(field[:, :width] * fresh[:, :width])


def last_kernel(place_ref, m_ref, a_ref, b_ref, d_ref, old_ref, m0_ref, m1_ref, done_ref, moment_ref):
    width = done_ref.shape[1]
    field = finish_field(place_ref[1] == 0, m_ref[...], a_ref[...], b_ref[...])[:, :width]
    fresh = field * d_ref[:, :width, :] * SCALE
    done_ref[...] = field
    tiles = [m0_ref[0], m0_ref[1], m1_ref[0], m1_ref[1], fold(field * old_ref[:, :width, :]), fold(field * fresh)]
    rows = [jnp.sum(tile, axis=0, keepdims=True) for tile in tiles]
    moment_ref[...] = jnp.concatenate(rows + [jnp.zeros((2, LANES), jnp.float32)], axis=0)


def coefficients(m):
    m0, m1, m2, m3, m4, m5 = m
    zero, one = jnp.zeros_like(m0), jnp.ones_like(m0)
    a0 = m1 / m0
    s2 = m2 - a0 * m1
    s3 = m3 - a0 * m2
    s4 = m4 - a0 * m3
    s5 = m5 - a0 * m4
    ok1 = s2 > TINY * m2
    s2k = jnp.where(ok1, s2, one)
    b1 = jnp.where(ok1, s2 / m0, zero)
    a1 = jnp.where(ok1, s3 / s2k - a0, a0)
    v2 = s4 - a1 * s3 - b1 * m2
    v3 = s5 - a1 * s4 - b1 * m3
    ok2 = jnp.logical_and(ok1, v2 > TINY * m4)
    v2k = jnp.where(ok2, v2, one)
    b2 = jnp.where(ok2, v2 / s2k, zero)
    a2 = jnp.where(ok2, v3 / v2k - s3 / s2k, a0)
    return a0, b1, a1, b2, a2, ok1, ok2


def final_kernel(moment_ref, t0_ref, t1_ref, t2_ref, f0_ref, f1_ref, f2_ref, c_ref, e_ref, coef_ref):
    @pl.when(pl.program_id(0) == 0)
    def _():
        sums = jnp.sum(moment_ref[...], axis=1, keepdims=True)
        m = [sums[n : n + 1] for n in range(6)]
        a0, b1, a1, b2, a2, ok1, ok2 = coefficients(m)
        scale = SCALE
        zero = jnp.zeros_like(a0)
        d0 = scale + a0
        d1 = scale + a1 - b1 / d0
        d2 = scale + a2 - b2 / d1
        z0 = scale / d0
        z1 = jnp.where(ok1, -z0 / d1, zero)
        z2 = jnp.where(ok2, -z1 / d2, zero)
        e1 = b1 / d0
        e2 = b2 / d1
        g2 = z2
        g1 = z1 - e2 * z2
        g0 = z0 - e1 * g1
        c2 = g2
        c1 = g1 - (a0 + a1) * g2
        c0 = g0 - a0 * g1 + (a0 * a1 - b1) * g2
        for n, value in enumerate((c0, c1, c2)):
            coef_ref[n] = jnp.broadcast_to(value, coef_ref.shape[1:])
        e_ref[...] = f0_ref[...] * c0[None] + f1_ref[...] * c1[None] + f2_ref[...] * c2[None]

    c = [coef_ref[n][0:1, 0:1][None] for n in range(3)]
    c_ref[...] = t0_ref[...] * c[0] + t1_ref[...] * c[1] + t2_ref[...] * c[2]


def per_device(perturbations, loc_weights, offsets, obs_x, obs_y, obs_t, innovations, obs_rinv):
    levels, members, width, depth = perturbations.shape
    columns = lax.axis_size("col")
    halves = lax.axis_size("mem")
    ext = width + 2 * RADIUS
    block = min(16, members)
    grid = members // block
    me = lax.axis_index("col")
    parity = me % 2
    place = jnp.stack([me * width, parity]).astype(jnp.int32)
    even = parity == 0
    pair_a = [(i, i ^ 1) for i in range(columns)]
    pair_b = [(i, i + 1) for i in range(1, columns - 1, 2)]
    pair_b = pair_b + [(target, source) for source, target in pair_b]

    def swap(a, b):
        return lax.ppermute(b, "col", pair_b), lax.ppermute(a, "col", pair_a)

    def edges(a, b, dim):
        return jnp.where(even, jnp.concatenate([a, b], axis=dim), jnp.concatenate([b, a], axis=dim))

    smem = pl.BlockSpec(memory_space=SMEM)
    vmem = pl.BlockSpec(memory_space=VMEM)

    def shape(*dims, dtype=jnp.float32):
        return jax.ShapeDtypeStruct(dims, dtype)

    high = width - RADIUS
    send_a = lax.dynamic_slice_in_dim(perturbations, jnp.where(even, high, 0), RADIUS, 2)
    send_b = lax.dynamic_slice_in_dim(perturbations, jnp.where(even, 0, high), RADIUS, 2)
    got_b, got_a = swap(send_a, send_b)
    halo = edges(got_a, got_b, 2)

    row = lambda v: v.reshape(1, -1)
    fields, obs_a, obs_b = pl.pallas_call(
        obs_kernel,
        out_shape=(
            shape(2, levels, width, depth),
            shape(2, levels, RADIUS, depth),
            shape(2, levels, RADIUS, depth),
        ),
        in_specs=[smem] + [vmem] * 5,
        out_specs=(vmem, vmem, vmem),
        name="obs",
    )(place, row(obs_x), row(obs_y), row(obs_t), row(innovations), row(obs_rinv))
    side_b, side_a = swap(obs_a, obs_b)
    fields = jnp.concatenate([fields, edges(side_a, side_b, 2)], axis=2)
    diagonal, weighted = fields[0], fields[1]

    p_spec = pl.BlockSpec((levels, block, width, depth), lambda i: (0, i, 0, 0))
    h_spec = pl.BlockSpec((levels, block, 2 * RADIUS, depth), lambda i: (0, i, 0, 0))
    t_spec = pl.BlockSpec((block, width, depth), lambda i: (i, 0, 0))
    t_shape = shape(members, width, depth)
    scratch = [
        pltpu.VMEM((GROUP, 2, width + 16, LANES), jnp.float32),
        pltpu.VMEM((GROUP, 2, width + 24, LANES), jnp.float32),
    ]
    cost = pl.CostEstimate(
        flops=2 * 30 * members * width * depth, bytes_accessed=10 * members * width * depth, transcendentals=0
    )

    def whole(*dims):
        return pl.BlockSpec(dims, lambda i: (0,) * len(dims))

    f_spec, f_shape = whole(levels, ext, depth), shape(levels, ext, depth)
    own_spec, own_shape = whole(levels, width, depth), shape(levels, width, depth)
    b_spec = whole(levels, 2 * RADIUS, depth)
    m_spec, m_shape = whole(2, 8, LANES), shape(2, 8, LANES)

    def exchange(field):
        if halves == 2:
            partner = lax.ppermute(field, "mem", [(0, 1), (1, 0)])
        else:
            field, partner = lax.psum(field, "mem"), jnp.zeros_like(field)
        total, a, b = pl.pallas_call(
            mid_kernel,
            out_shape=(f_shape, shape(levels, 2 * RADIUS, depth), shape(levels, 2 * RADIUS, depth)),
            in_specs=[smem, vmem, vmem],
            out_specs=(vmem, vmem, vmem),
            name="mid",
        )(place, field, partner)
        from_b, from_a = swap(a, b)
        return total, from_a, from_b

    t0, f0 = pl.pallas_call(
        first_kernel,
        out_shape=(t_shape, f_shape),
        grid=(grid,),
        in_specs=[smem, smem, p_spec, h_spec, f_spec],
        out_specs=(t_spec, f_spec),
        scratch_shapes=scratch,
        cost_estimate=cost,
        name="first",
    )(loc_weights, offsets, perturbations, halo, weighted)

    def following(pieces, old):
        return pl.pallas_call(
            next_kernel,
            out_shape=(t_shape, f_shape, own_shape, f_shape, m_shape),
            grid=(grid,),
            in_specs=[smem, smem, smem, p_spec, h_spec, f_spec, b_spec, b_spec, f_spec, f_spec],
            out_specs=(t_spec, f_spec, own_spec, f_spec, m_spec),
            scratch_shapes=scratch,
            cost_estimate=cost,
            name="next",
        )(loc_weights, offsets, place, perturbations, halo, *pieces, diagonal, old)

    t1, f1, e0, w1, moment0 = following(exchange(f0), weighted)
    t2, f2, e1, w2, moment1 = following(exchange(f1), w1)
    e2, moments = pl.pallas_call(
        last_kernel,
        out_shape=(own_shape, shape(8, LANES)),
        in_specs=[smem] + [vmem] * 7,
        out_specs=(vmem, vmem),
        name="last",
    )(place, *exchange(f2), diagonal, w2, moment0, moment1)
    step = 1
    while step < columns:
        moments = moments + lax.ppermute(moments, "col", [(i, i ^ step) for i in range(columns)])
        step *= 2
    control, increment = pl.pallas_call(
        final_kernel,
        out_shape=(t_shape, own_shape),
        grid=(grid,),
        in_specs=[whole(8, LANES)] + [t_spec] * 3 + [own_spec] * 3,
        out_specs=(t_spec, own_spec),
        scratch_shapes=[pltpu.VMEM((3, 8, LANES), jnp.float32)],
        name="final",
    )(moments, t0, t1, t2, e0, e1, e2)
    return control, increment


def solution(mesh):
    in_specs = (P(None, "mem", "col", None), P(), P(), P("col"), P("col"), P("col"), P("col"), P("col"))
    out_specs = (P("mem", "col", None), P(None, "col", None))
    return jax.shard_map(per_device, mesh=mesh, in_specs=in_specs, out_specs=out_specs, check_vma=False)
```

time: 657 us -> 162 us (0.25); the launches traced: 648 us -> 161 us
  blocking collectives: 245 us -> 0 us
  other arithmetic: 184 us -> 8.45 us
  local copies, waits for them, and re-layouts: 90.8 us -> 7.77 us
  Pallas kernels: 0 us -> 71.5 us
  between operations: 56.3 us -> 0.74 us
  starting transfers between devices: 34 us -> 55.1 us
  waiting for transfers between devices: 37.7 us -> 17.2 us
    psum x9 -> x0, blocking collectives: 245 us -> none  [the longest x3 124 us: squares(): return lax.psum(jnp.sum(source * source), ('mem', 'col'))]
    reduce_sum x12 -> x0, other arithmetic: 129 us -> none  [the longest x4 68.3 us: combine(): jnp.sum(perturbations[level].astype(jnp.float32) * coeffs, axis=0)]
    pallas_call x0 -> x9, Pallas kernels: none -> 71.5 us  [the longest x2 37.5 us: following(): pl.pallas_call(next_kernel, out_shape=(t_shape, f_shape, own_shape, f_sha...]
    gather x3 -> x0, local copies, waits for them, and re-layouts: 35.3 us -> none  [per_device(): partial_value = forward(direction).reshape(-1)[flat_index]]
    dynamic_slice x7 -> x1, local copies, waits for them, and re-layouts: 37.9 us -> 3.31 us  [per_device(): lax.dynamic_slice_in_dim(perturbations, jnp.where(even, high, 0), RADIUS, 2)]
    scatter-add x3 -> x0, other arithmetic: 33.8 us -> none  [spread(): jnp.zeros((levels * col_width * row_depth,), jnp.float32).at[flat_index]]
    psum x1 -> x0, waiting for transfers between devices: 26 us -> none  [per_device(): increment = lax.psum(forward(control), 'mem')]
    ppermute x14 -> x17, starting transfers between devices: 33.9 us -> 55.1 us  [the longest x10 36.4 us: swap(): return (lax.ppermute(b, 'col', pair_b), lax.ppermute(a, 'col', pair_a))]
  transfers between devices with their start and end apart: 15 -> 17, of which waited for: 4 -> 10; matrix products, arithmetic and copies ran while one was open for 1% -> 2% of each run, Pallas kernels for 0% -> 1%
where the time goes in v1:
time: 162 us; the launch traced here: 161 us
  Pallas kernels  71.5 us (44%)
  starting transfers between devices  55.1 us (34%)
  waiting for transfers between devices  17.2 us (11%)
  other arithmetic  8.45 us (5%)
  local copies, waits for them, and re-layouts  7.77 us (5%)
    pallas_call x2, Pallas kernels, following(): pl.pallas_call(next_kernel, out_shape=(t_shape, f_shape, own_shape, f_sha...  37.5 us
    ppermute x10, starting transfers between devices, swap(): return (lax.ppermute(b, 'col', pair_b), lax.ppermute(a, 'col', pair_a))  36.4 us
    pallas_call x1, Pallas kernels, per_device(): pl.pallas_call(first_kernel, out_shape=(t_shape, f_shape), grid=(grid,),...  18.4 us
    ppermute x4, starting transfers between devices, per_device(): lax.ppermute(moments, 'col', [(i, i ^ step) for i in range(columns)])  14.1 us
    ppermute x3, waiting for transfers between devices, exchange(): partner = lax.ppermute(field, 'mem', [(0, 1), (1, 0)])  9.92 us
    pallas_call x1, Pallas kernels, per_device(): pl.pallas_call(final_kernel, out_shape=(t_shape, own_shape), grid=(grid,)...  6.98 us
    ppermute x4, waiting for transfers between devices, per_device(): lax.ppermute(moments, 'col', [(i, i ^ step) for i in range(columns)])  6.06 us
    select_n x2, other arithmetic, edges(): jnp.where(even, jnp.concatenate([a, b], axis=dim), jnp.concatenate([b, a]...  4.94 us
  transfers between devices with their start and end apart: 17, of which 10 were waited for; matrix products, arithmetic and copies ran while one was open for 2% of the time, Pallas kernels for 1%

profile of v1, /device:TPU:0, one launch (start us, length us, event | category | flops | bytes accessed | tf_op | source)
XLA Modules:
  0.0 160.8 jit_solution(11806027154372247817)
XLA Ops:
  0.6 0.0 copy-start.9
  0.7 3.3 %constant_dynamic-slice_fusion.1 = (bf16[4,128,4,256]{3,2,1,0:T(4,128)(2,1)S(1)}, bf16[4,128,4,256]{3,2,1,0:T(4,128)(2,1)S(1)}) fusion(bf16[4,128,16,256]{3,2,1,0:T(8,128)(2,1)} %p_ref.5, s32[]{:T(128)S(6)} %select_n.34, s32[]{:T(128)S(6)} %select_n.35), kind=kLoop, calls=%fused_computation.10 | loop fusion | bytes 4194312 | tf_op jit(solution)/shard_map/dynamic_slice | solution.py:265
  4.0 0.6 collective-permute-start
  4.5 1.6 %collective-permute-start.1 = (bf16[4,128,4,256]{3,2,1,0:T(4,128)(2,1)S(1)}, bf16[4,128,4,256]{3,2,1,0:T(4,128)(2,1)}, u32[]{:S(2)}, u32[]{:S(2)}) collective-permute-start(bf16[4,128,4,256]{3,2,1,0:T(4,128)(2,1)S(1)} %get-tuple-element.55), channel_id=1, source_target_pairs={{1,2},{3,4},{5,6},{7,8},{9,10},{11,12},{13,14},{2,1},{4,3},{6,5},{... | collective-permute-start | bytes 3145736 | tf_op jit(solution)/shard_map/ppermute | solution.py:253
  6.2 0.7 pad_add_fusion.place_ref
  6.8 2.1 %obs.1 = (f32[2,4,16,256]{3,2,1,0:T(8,128)}, f32[2,4,4,256]{3,2,1,0:T(4,128)}, f32[2,4,4,256]{3,2,1,0:T(4,128)}) custom-call(s32[2]{0:T(128)} %pad_add_fusion.place_ref, s32[1,2048]{1,0:T(1,128)} %bitcast.11, s32[1,2048]{1,0:T(1,128)} %bitcast.12, s32[1,2048]{1,0:T(1,128)} %bitcast.13, f32[1,2048]{1,0:T(1,128)} %bitcast.14, f32[1,2048]{1,0:T(1,128)} %bitcast.15), custom_call_target="tpu_custom_call" | custom-call | tf_op jit(solution)/shard_map/obs/pallas_call | solution.py:271
  8.9 2.9 %collective-permute-start.2 = (f32[2,4,4,256]{3,2,1,0:T(4,128)}, f32[2,4,4,256]{3,2,1,0:T(4,128)S(1)}, u32[]{:S(2)}, u32[]{:S(2)}) collective-permute-start(f32[2,4,4,256]{3,2,1,0:T(4,128)} %get-tuple-element.29), channel_id=1, source_target_pairs={{0,1},{1,0},{2,3},{3,2},{4,5},{5,4},{6,7},{7,6},{8,9},{9,8},{10,11... | collective-permute-start | bytes 98312 | tf_op jit(solution)/shard_map/ppermute | solution.py:253
  11.8 0.7 collective-permute-start.3
  12.5 0.0 copy-done.9
  12.5 0.7 copy.12.offset_ref
  13.1 0.0 collective-permute-done.2
  13.2 0.0 collective-permute-done.3
  13.2 1.6 fusion.2
  14.8 0.0 collective-permute-done
  14.8 0.0 collective-permute-done.1
  14.8 4.9 %maximum_select_fusion.h_ref = bf16[4,128,8,256]{3,2,1,0:T(8,128)(2,1)} fusion(bf16[4,128,4,256]{3,2,1,0:T(4,128)(2,1)} %collective-permute-done.1, bf16[4,128,4,256]{3,2,1,0:T(4,128)(2,1)S(1)} %collective-permute-done, pred[]{:T(512)S(6)} %eq.5), kind=kLoop, calls=%fused_computation | loop fusion | flops 9437184 | bytes 4194305 | tf_op jit(solution)/shard_map/jit(_where)/select_n | solution.py:256
  19.7 18.4 %first.1 = (f32[128,16,256]{2,1,0:T(8,128)}, f32[4,24,256]{2,1,0:T(8,128)}) custom-call(f32[7]{0:T(128)} %weight_ref.5, s32[7,2]{1,0:T(8,128)} %copy.12.offset_ref, bf16[4,128,16,256]{3,2,1,0:T(8,128)(2,1)} %p_ref.5, bf16[4,128,8,256]{3,2,1,0:T(8,128)(2,1)} %maximum_select_fusion.h_ref, f32[4,24,256]{2,1,0:T(8,128)} %get-tuple-element.57.w_ref.old_ref), custom_call_target="tpu_custom_call" | custom-call | flops 31457280 | bytes 5242880 | tf_op jit(solution)/shard_map/first/pallas_call | solution.py:321
  38.1 1.5 collective-permute-start.4
  39.6 3.3 %collective-permute-done.4.r_ref = f32[4,24,256]{2,1,0:T(8,128)S(1)} collective-permute-done((f32[4,24,256]{2,1,0:T(8,128)}, f32[4,24,256]{2,1,0:T(8,128)S(1)}, u32[]{:S(2)}, u32[]{:S(2)}) %collective-permute-start.4) | collective-permute-done | bytes 98336 | tf_op jit(solution)/shard_map/ppermute | solution.py:308
  42.9 0.0 copy-start
  42.9 0.6 copy-done
  43.5 1.6 %mid.3 = (f32[4,24,256]{2,1,0:T(8,128)}, f32[4,8,256]{2,1,0:T(8,128)}, f32[4,8,256]{2,1,0:T(8,128)}) custom-call(s32[2]{0:T(128)} %pad_add_fusion.place_ref, f32[4,24,256]{2,1,0:T(8,128)} %get-tuple-element.31.f_ref, f32[4,24,256]{2,1,0:T(8,128)} %copy-done), custom_call_target="tpu_custom_call" | custom-call | tf_op jit(solution)/shard_map/mid/pallas_call | solution.py:311
  45.2 18.5 %collective-permute-start.5 = (f32[4,8,256]{2,1,0:T(8,128)}, f32[4,8,256]{2,1,0:T(8,128)S(1)}, u32[]{:S(2)}, u32[]{:S(2)}) collective-permute-start(f32[4,8,256]{2,1,0:T(8,128)} %get-tuple-element.33), channel_id=1, source_target_pairs={{0,1},{1,0},{2,3},{3,2},{4,5},{5,4},{6,7},{7,6},{8,9},{9,8},{10,11... | collective-permute-start | bytes 98312 | tf_op jit(solution)/shard_map/ppermute | solution.py:253
  63.7 0.7 collective-permute-start.6
  64.3 0.4 collective-permute-done.5.a_ref
  64.7 0.0 copy-start.4
  64.7 0.0 collective-permute-done.6.b_ref
  64.8 0.0 copy-start.6
  64.8 0.6 copy-done.4
  65.4 0.0 copy-done.6
  65.4 18.7 %next.2 = (f32[128,16,256]{2,1,0:T(8,128)}, f32[4,24,256]{2,1,0:T(8,128)}, f32[4,16,256]{2,1,0:T(8,128)}, f32[4,24,256]{2,1,0:T(8,128)}, f32[2,8,128]{2,1,0:T(8,128)}) custom-call(f32[7]{0:T(128)} %weight_ref.5, s32[7,2]{1,0:T(8,128)} %copy.12.offset_ref, s32[2]{0:T(128)} %pad_add_fusion.place_ref, bf16[4,128,16,256]{3,2,1,0:T(8,128)(2,1)} %p_ref.5, ...), custom_call_target="tpu_custom_call" | custom-call | flops 31457280 | bytes 5242880 | tf_op jit(solution)/shard_map/next/pallas_call | solution.py:333
  84.1 1.6 collective-permute-start.7
  85.7 3.3 %collective-permute-done.7.r_ref = f32[4,24,256]{2,1,0:T(8,128)S(1)} collective-permute-done((f32[4,24,256]{2,1,0:T(8,128)}, f32[4,24,256]{2,1,0:T(8,128)S(1)}, u32[]{:S(2)}, u32[]{:S(2)}) %collective-permute-start.7) | collective-permute-done | bytes 98336 | tf_op jit(solution)/shard_map/ppermute | solution.py:308
  89.0 0.6 copy-done.1
  89.6 1.6 %mid.4 = (f32[4,24,256]{2,1,0:T(8,128)}, f32[4,8,256]{2,1,0:T(8,128)}, f32[4,8,256]{2,1,0:T(8,128)}) custom-call(s32[2]{0:T(128)} %pad_add_fusion.place_ref, f32[4,24,256]{2,1,0:T(8,128)} %get-tuple-element.35.f_ref, f32[4,24,256]{2,1,0:T(8,128)} %copy-done.1), custom_call_target="tpu_custom_call" | custom-call | tf_op jit(solution)/shard_map/mid/pallas_call | solution.py:311
  91.2 5.0 %collective-permute-start.8 = (f32[4,8,256]{2,1,0:T(8,128)}, f32[4,8,256]{2,1,0:T(8,128)S(1)}, u32[]{:S(2)}, u32[]{:S(2)}) collective-permute-start(f32[4,8,256]{2,1,0:T(8,128)} %get-tuple-element.37), channel_id=1, source_target_pairs={{0,1},{1,0},{2,3},{3,2},{4,5},{5,4},{6,7},{7,6},{8,9},{9,8},{10,11... | collective-permute-start | bytes 98312 | tf_op jit(solution)/shard_map/ppermute | solution.py:253
  96.2 0.7 collective-permute-start.9
  96.9 0.4 collective-permute-done.8.a_ref
  97.3 0.0 collective-permute-done.9.b_ref
  97.3 0.6 copy-done.3
  97.9 0.0 copy-done.5
  97.9 18.8 %next.3 = (f32[128,16,256]{2,1,0:T(8,128)}, f32[4,24,256]{2,1,0:T(8,128)}, f32[4,16,256]{2,1,0:T(8,128)}, f32[4,24,256]{2,1,0:T(8,128)}, f32[2,8,128]{2,1,0:T(8,128)}) custom-call(f32[7]{0:T(128)} %weight_ref.5, s32[7,2]{1,0:T(8,128)} %copy.12.offset_ref, s32[2]{0:T(128)} %pad_add_fusion.place_ref, bf16[4,128,16,256]{3,2,1,0:T(8,128)(2,1)} %p_ref.5, ...), custom_call_target="tpu_custom_call" | custom-call | flops 31457280 | bytes 5242880 | tf_op jit(solution)/shard_map/next/pallas_call | solution.py:333
  116.7 1.6 collective-permute-start.10
  118.3 3.3 %collective-permute-done.10.r_ref = f32[4,24,256]{2,1,0:T(8,128)S(1)} collective-permute-done((f32[4,24,256]{2,1,0:T(8,128)}, f32[4,24,256]{2,1,0:T(8,128)S(1)}, u32[]{:S(2)}, u32[]{:S(2)}) %collective-permute-start.10) | collective-permute-done | bytes 98336 | tf_op jit(solution)/shard_map/ppermute | solution.py:308
  121.6 0.6 copy-done.2
  122.2 1.6 %mid.5 = (f32[4,24,256]{2,1,0:T(8,128)}, f32[4,8,256]{2,1,0:T(8,128)}, f32[4,8,256]{2,1,0:T(8,128)}) custom-call(s32[2]{0:T(128)} %pad_add_fusion.place_ref, f32[4,24,256]{2,1,0:T(8,128)} %get-tuple-element.40.f_ref, f32[4,24,256]{2,1,0:T(8,128)} %copy-done.2), custom_call_target="tpu_custom_call" | custom-call | tf_op jit(solution)/shard_map/mid/pallas_call | solution.py:311
  123.8 5.2 %collective-permute-start.11 = (f32[4,8,256]{2,1,0:T(8,128)}, f32[4,8,256]{2,1,0:T(8,128)S(1)}, u32[]{:S(2)}, u32[]{:S(2)}) collective-permute-start(f32[4,8,256]{2,1,0:T(8,128)} %get-tuple-element.42), channel_id=1, source_target_pairs={{0,1},{1,0},{2,3},{3,2},{4,5},{5,4},{6,7},{7,6},{8,9},{9,8},{10,11... | collective-permute-start | bytes 98312 | tf_op jit(solution)/shard_map/ppermute | solution.py:253
  129.0 0.7 collective-permute-start.12
  129.7 0.4 collective-permute-done.11.a_ref
  130.1 0.0 collective-permute-done.12.b_ref
  130.1 0.6 copy-done.7
  130.7 0.0 copy-done.8
  130.7 1.7 %last.1 = (f32[4,16,256]{2,1,0:T(8,128)}, f32[8,128]{1,0:T(8,128)}) custom-call(s32[2]{0:T(128)} %pad_add_fusion.place_ref, f32[4,24,256]{2,1,0:T(8,128)} %get-tuple-element.41.m_ref, f32[4,8,256]{2,1,0:T(8,128)} %copy-done.7, f32[4,8,256]{2,1,0:T(8,128)} %copy-done.8, f32[4,24,256]{2,1,0:T(8,128)} %get-tuple-element.56.d_ref, ...), custom_call_target="tpu_custom_call" | custom-call | tf_op jit(solution)/shard_map/last/pallas_call | solution.py:346
  132.4 6.5 %collective-permute-start.13 = (f32[8,128]{1,0:T(8,128)}, f32[8,128]{1,0:T(8,128)S(1)}, u32[]{:S(2)}, u32[]{:S(2)}) collective-permute-start(f32[8,128]{1,0:T(8,128)} %get-tuple-element.47), channel_id=1, source_target_pairs={{0,1},{1,0},{2,3},{3,2},{4,5},{5,4},{6,7},{7,6},{8,9},{9,8},{10,11... | collective-permute-start | bytes 12296 | tf_op jit(solution)/shard_map/ppermute | solution.py:355
  138.9 1.0 collective-permute-done.13
  139.9 0.7 add.19
  140.6 2.9 %collective-permute-start.14 = (f32[8,128]{1,0:T(8,128)S(1)}, f32[8,128]{1,0:T(8,128)S(1)}, u32[]{:S(2)}, u32[]{:S(2)}) collective-permute-start(f32[8,128]{1,0:T(8,128)S(1)} %add.19), channel_id=1, source_target_pairs={{0,2},{1,3},{2,0},{3,1},{4,6},{5,7},{6,4},{7,5},{8,10},{9,11},{10,... | collective-permute-start | bytes 12296 | tf_op jit(solution)/shard_map/ppermute | solution.py:355
  143.5 1.6 collective-permute-done.14
  145.1 1.8 %collective-permute-start.15 = (f32[8,128]{1,0:T(8,128)S(1)}, f32[8,128]{1,0:T(8,128)S(1)}, u32[]{:S(2)}, u32[]{:S(2)}) collective-permute-start(f32[8,128]{1,0:T(8,128)S(1)} %add.20), channel_id=1, source_target_pairs={{0,4},{1,5},{2,6},{3,7},{4,0},{5,1},{6,2},{7,3},{8,12},{9,13},{10,... | collective-permute-start | bytes 12296 | tf_op jit(solution)/shard_map/ppermute | solution.py:355
  147.0 1.8 %collective-permute-done.15 = f32[8,128]{1,0:T(8,128)S(1)} collective-permute-done((f32[8,128]{1,0:T(8,128)S(1)}, f32[8,128]{1,0:T(8,128)S(1)}, u32[]{:S(2)}, u32[]{:S(2)}) %collective-permute-start.15) | collective-permute-done | bytes 4128 | tf_op jit(solution)/shard_map/ppermute | solution.py:355
  148.7 2.8 %collective-permute-start.16 = (f32[8,128]{1,0:T(8,128)S(1)}, f32[8,128]{1,0:T(8,128)S(1)}, u32[]{:S(2)}, u32[]{:S(2)}) collective-permute-start(f32[8,128]{1,0:T(8,128)S(1)} %add.21), channel_id=1, source_target_pairs={{0,8},{1,9},{2,10},{3,11},{4,12},{5,13},{6,14},{7,15},{8,0},{9,1},... | collective-permute-start | bytes 12296 | tf_op jit(solution)/shard_map/ppermute | solution.py:355
  151.6 1.7 %collective-permute-done.16 = f32[8,128]{1,0:T(8,128)S(1)} collective-permute-done((f32[8,128]{1,0:T(8,128)S(1)}, f32[8,128]{1,0:T(8,128)S(1)}, u32[]{:S(2)}, u32[]{:S(2)}) %collective-permute-start.16) | collective-permute-done | bytes 4128 | tf_op jit(solution)/shard_map/ppermute | solution.py:355
  153.2 0.6 add.22.moment_ref
  153.8 7.0 %final.1 = (f32[128,16,256]{2,1,0:T(8,128)}, f32[4,16,256]{2,1,0:T(8,128)}) custom-call(f32[8,128]{1,0:T(8,128)} %add.22.moment_ref, f32[128,16,256]{2,1,0:T(8,128)} %get-tuple-element.48.t0_ref, f32[128,16,256]{2,1,0:T(8,128)} %get-tuple-element.49.t1_ref, f32[128,16,256]{2,1,0:T(8,128)} %get-tuple-element.50.t2_ref, ...), custom_call_target="tpu_custom_call" | custom-call | tf_op jit(solution)/shard_map/final/pallas_call | solution.py:357
  (9 shorter events, 0.0 us)
Async XLA Ops:
  0.6 11.8 %copy-start.9 = (s32[7,2]{0,1:T(2,128)S(1)}, s32[7,2]{0,1:T(2,128)}, u32[]{:S(2)}) copy-start(s32[7,2]{0,1:T(2,128)} %param.10) | copy-start | bytes 172
  4.0 10.8 %collective-permute-start = (bf16[4,128,4,256]{3,2,1,0:T(4,128)(2,1)S(1)}, bf16[4,128,4,256]{3,2,1,0:T(4,128)(2,1)S(1)}, u32[]{:S(2)}, u32[]{:S(2)}) collective-permute-start(bf16[4,128,4,256]{3,2,1,0:T(4,128)(2,1)S(1)} %get-tuple-element.54), channel_id=1, source_target_pairs={{0,1},{1,0},{2,3},{3,2},{4,5},{5,4},{6,7},{7,6},{8,9},{9,8},{10,11... | collective-permute-start | bytes 3145736 | tf_op jit(solution)/shard_map/ppermute | solution.py:253
  4.5 10.2 %collective-permute-start.1 = (bf16[4,128,4,256]{3,2,1,0:T(4,128)(2,1)S(1)}, bf16[4,128,4,256]{3,2,1,0:T(4,128)(2,1)}, u32[]{:S(2)}, u32[]{:S(2)}) collective-permute-start(bf16[4,128,4,256]{3,2,1,0:T(4,128)(2,1)S(1)} %get-tuple-element.55), channel_id=1, source_target_pairs={{1,2},{3,4},{5,6},{7,8},{9,10},{11,12},{13,14},{2,1},{4,3},{6,5},{... | collective-permute-start | bytes 3145736 | tf_op jit(solution)/shard_map/ppermute | solution.py:253
  8.9 4.2 %collective-permute-start.2 = (f32[2,4,4,256]{3,2,1,0:T(4,128)}, f32[2,4,4,256]{3,2,1,0:T(4,128)S(1)}, u32[]{:S(2)}, u32[]{:S(2)}) collective-permute-start(f32[2,4,4,256]{3,2,1,0:T(4,128)} %get-tuple-element.29), channel_id=1, source_target_pairs={{0,1},{1,0},{2,3},{3,2},{4,5},{5,4},{6,7},{7,6},{8,9},{9,8},{10,11... | collective-permute-start | bytes 98312 | tf_op jit(solution)/shard_map/ppermute | solution.py:253
  11.8 1.3 collective-permute-start.3
  38.1 4.8 %collective-permute-start.4 = (f32[4,24,256]{2,1,0:T(8,128)}, f32[4,24,256]{2,1,0:T(8,128)S(1)}, u32[]{:S(2)}, u32[]{:S(2)}) collective-permute-start(f32[4,24,256]{2,1,0:T(8,128)} %get-tuple-element.31.f_ref), channel_id=1, source_target_pairs={{0,16},{16,0},{1,17},{17,1},{2,18},{18,2},{3,19},{19,3},{4,20},{20... | collective-permute-start | bytes 294920 | tf_op jit(solution)/shard_map/ppermute | solution.py:308
  42.9 0.6 copy-start
  45.2 19.6 %collective-permute-start.5 = (f32[4,8,256]{2,1,0:T(8,128)}, f32[4,8,256]{2,1,0:T(8,128)S(1)}, u32[]{:S(2)}, u32[]{:S(2)}) collective-permute-start(f32[4,8,256]{2,1,0:T(8,128)} %get-tuple-element.33), channel_id=1, source_target_pairs={{0,1},{1,0},{2,3},{3,2},{4,5},{5,4},{6,7},{7,6},{8,9},{9,8},{10,11... | collective-permute-start | bytes 98312 | tf_op jit(solution)/shard_map/ppermute | solution.py:253
  63.7 1.1 collective-permute-start.6
  64.7 0.6 copy-start.4
  64.8 0.6 copy-start.6
  84.1 4.9 %collective-permute-start.7 = (f32[4,24,256]{2,1,0:T(8,128)}, f32[4,24,256]{2,1,0:T(8,128)S(1)}, u32[]{:S(2)}, u32[]{:S(2)}) collective-permute-start(f32[4,24,256]{2,1,0:T(8,128)} %get-tuple-element.35.f_ref), channel_id=1, source_target_pairs={{0,16},{16,0},{1,17},{17,1},{2,18},{18,2},{3,19},{19,3},{4,20},{20... | collective-permute-start | bytes 294920 | tf_op jit(solution)/shard_map/ppermute | solution.py:308
  89.0 0.6 copy-start.1
  91.2 6.0 %collective-permute-start.8 = (f32[4,8,256]{2,1,0:T(8,128)}, f32[4,8,256]{2,1,0:T(8,128)S(1)}, u32[]{:S(2)}, u32[]{:S(2)}) collective-permute-start(f32[4,8,256]{2,1,0:T(8,128)} %get-tuple-element.37), channel_id=1, source_target_pairs={{0,1},{1,0},{2,3},{3,2},{4,5},{5,4},{6,7},{7,6},{8,9},{9,8},{10,11... | collective-permute-start | bytes 98312 | tf_op jit(solution)/shard_map/ppermute | solution.py:253
  96.2 1.1 collective-permute-start.9
  97.3 0.6 copy-start.3
  97.3 0.6 copy-start.5
  116.7 4.9 %collective-permute-start.10 = (f32[4,24,256]{2,1,0:T(8,128)}, f32[4,24,256]{2,1,0:T(8,128)S(1)}, u32[]{:S(2)}, u32[]{:S(2)}) collective-permute-start(f32[4,24,256]{2,1,0:T(8,128)} %get-tuple-element.40.f_ref), channel_id=1, source_target_pairs={{0,16},{16,0},{1,17},{17,1},{2,18},{18,2},{3,19},{19,3},{4,20},{20... | collective-permute-start | bytes 294920 | tf_op jit(solution)/shard_map/ppermute | solution.py:308
  121.6 0.6 copy-start.2
  123.8 6.3 %collective-permute-start.11 = (f32[4,8,256]{2,1,0:T(8,128)}, f32[4,8,256]{2,1,0:T(8,128)S(1)}, u32[]{:S(2)}, u32[]{:S(2)}) collective-permute-start(f32[4,8,256]{2,1,0:T(8,128)} %get-tuple-element.42), channel_id=1, source_target_pairs={{0,1},{1,0},{2,3},{3,2},{4,5},{5,4},{6,7},{7,6},{8,9},{9,8},{10,11... | collective-permute-start | bytes 98312 | tf_op jit(solution)/shard_map/ppermute | solution.py:253
  129.0 1.1 collective-permute-start.12
  130.1 0.6 copy-start.7
  130.1 0.6 copy-start.8
  132.4 7.5 %collective-permute-start.13 = (f32[8,128]{1,0:T(8,128)}, f32[8,128]{1,0:T(8,128)S(1)}, u32[]{:S(2)}, u32[]{:S(2)}) collective-permute-start(f32[8,128]{1,0:T(8,128)} %get-tuple-element.47), channel_id=1, source_target_pairs={{0,1},{1,0},{2,3},{3,2},{4,5},{5,4},{6,7},{7,6},{8,9},{9,8},{10,11... | collective-permute-start | bytes 12296 | tf_op jit(solution)/shard_map/ppermute | solution.py:355
  140.6 4.5 %collective-permute-start.14 = (f32[8,128]{1,0:T(8,128)S(1)}, f32[8,128]{1,0:T(8,128)S(1)}, u32[]{:S(2)}, u32[]{:S(2)}) collective-permute-start(f32[8,128]{1,0:T(8,128)S(1)} %add.19), channel_id=1, source_target_pairs={{0,2},{1,3},{2,0},{3,1},{4,6},{5,7},{6,4},{7,5},{8,10},{9,11},{10,... | collective-permute-start | bytes 12296 | tf_op jit(solution)/shard_map/ppermute | solution.py:355
  145.1 3.6 %collective-permute-start.15 = (f32[8,128]{1,0:T(8,128)S(1)}, f32[8,128]{1,0:T(8,128)S(1)}, u32[]{:S(2)}, u32[]{:S(2)}) collective-permute-start(f32[8,128]{1,0:T(8,128)S(1)} %add.20), channel_id=1, source_target_pairs={{0,4},{1,5},{2,6},{3,7},{4,0},{5,1},{6,2},{7,3},{8,12},{9,13},{10,... | collective-permute-start | bytes 12296 | tf_op jit(solution)/shard_map/ppermute | solution.py:355
  148.7 4.5 %collective-permute-start.16 = (f32[8,128]{1,0:T(8,128)S(1)}, f32[8,128]{1,0:T(8,128)S(1)}, u32[]{:S(2)}, u32[]{:S(2)}) collective-permute-start(f32[8,128]{1,0:T(8,128)S(1)} %add.21), channel_id=1, source_target_pairs={{0,8},{1,9},{2,10},{3,11},{4,12},{5,13},{6,14},{7,15},{8,0},{9,1},... | collective-permute-start | bytes 12296 | tf_op jit(solution)/shard_map/ppermute | solution.py:355

commit v2 on v1

--- a/solution.py
+++ b/solution.py
@@ -11,6 +11,8 @@
 SCALE = 2.0**-12
 TINY = 3e-8
 GROUP = 4
+LIMIT = 20 << 20
+AHEAD = 2
 LANES = 128
 SMEM = pltpu.MemorySpace.SMEM
 VMEM = pltpu.MemorySpace.VMEM
@@ -82,85 +84,181 @@
     return total
 
 
-def apply_core(weight_ref, offset_ref, p_ref, h_ref, w_ref, t_ref, f_ref, prod_ref, mid_ref):
+def apply_core(weight_ref, offset_ref, p_ref, h_ref, w_ref, t_ref, f_ref, work, chunk, enter, leave):
+    prod_refs, mid_refs, roll_refs = split(work)
     levels, block, width, depth = p_ref.shape
     taps = weight_ref.shape[0]
     halves = [slice(i * LANES, (i + 1) * LANES) for i in range(2)]
     ext = width + 2 * RADIUS
     lane = lax.broadcasted_iota(jnp.int32, (8, LANES), 1)
 
-    def shifted(ref, slot, start, rows, across):
-        shift = across & (LANES - 1)
-        swap = (across < 0).astype(jnp.int32)
-        first = pltpu.roll(ref[slot, swap, pl.ds(start, rows), :], shift, 1)
-        second = pltpu.roll(ref[slot, 1 - swap, pl.ds(start, rows), :], shift, 1)
+    def shifted(first, second, shift):
+        rows = first.shape[0]
+        first, second = pltpu.roll(first, shift, 1), pltpu.roll(second, shift, 1)
         wrap = jnp.broadcast_to((lane < shift)[None], (rows // 8, 8, LANES)).reshape(rows, LANES)
         return jnp.where(wrap, second, first), jnp.where(wrap, first, second)
 
-    def group(step, carry):
-        base = step * GROUP
+    def products(k, prod_ref):
+        for i, half in enumerate(halves):
+            own = sum(p_ref[l, k, :, half].astype(jnp.float32) * w_ref[l, 0:width, half] for l in range(levels))
+            edge = sum(h_ref[l, k, :, half].astype(jnp.float32) * w_ref[l, width:ext, half] for l in range(levels))
+            prod_ref[i, 0:8, :] = edge
+            prod_ref[i, 8 : 8 + width, :] = own
+            prod_ref[i, 8 + width : 16 + width, :] = edge
+
+    def transposed(k, prod_ref, mid_ref):
+        total = None
+        for s in range(taps):
+            across = offset_ref[s, 1]
+            swap = (across < 0).astype(jnp.int32)
+            start = pl.ds(8 - offset_ref[s, 0], width)
+            got = shifted(prod_ref[swap, start, :], prod_ref[1 - swap, start, :], across & (LANES - 1))
+            got = [weight_ref[s] * new for new in got]
+            total = got if total is None else [old + new for old, new in zip(total, got)]
+        for i, half in enumerate(halves):
+            t_ref[k, :, half] = total[i]
+            mid_ref[i] = total[i]
+
+    def rolled(mid_ref, roll_ref):
+        for s in range(taps):
+            across = -offset_ref[s, 1]
+            swap = (across < 0).astype(jnp.int32)
+            got = shifted(mid_ref[swap], mid_ref[1 - swap], across & (LANES - 1))
+            for i in range(2):
+                new = weight_ref[s] * got[i]
+                roll_ref[s, i, 8 : 8 + width, :] = new
+                roll_ref[s, i, 16 + width : 24 + width, :] = new[0:8]
+
+    def gather(base):
+        starts = [8 + offset_ref[s, 0] for s in range(taps)]
+        for i, half in enumerate(halves):
+            for row in range(0, ext, 8):
+                moved = [
+                    sum(roll_refs[slot][s, i, pl.ds(starts[s] + row, 8), :] for s in range(taps))
+                    for slot in range(GROUP)
+                ]
+                for l in range(levels):
+                    if row < width:
+                        values = [p_ref[l, base + slot, row : row + 8, half] for slot in range(GROUP)]
+                    else:
+                        values = [h_ref[l, base + slot, :, half] for slot in range(GROUP)]
+                    f_ref[l, row : row + 8, half] += sum(
+                        value.astype(jnp.float32) * new for value, new in zip(values, moved)
+                    )
+
+    def stage_one(base):
         for slot in range(GROUP):
-            k = base + slot
-            for i, half in enumerate(halves):
-                own = sum(p_ref[l, k, :, half].astype(jnp.float32) * w_ref[l, 0:width, half] for l in range(levels))
-                edge = sum(h_ref[l, k, :, half].astype(jnp.float32) * w_ref[l, width:ext, half] for l in range(levels))
-                prod_ref[slot, i, 0:8, :] = edge
-                prod_ref[slot, i, 8 : 8 + width, :] = own
-                prod_ref[slot, i, 8 + width : 16 + width, :] = edge
+            products(base + slot, prod_refs[slot])
+
+    def stage_two(base):
         for slot in range(GROUP):
-            k = base + slot
-            total = [jnp.zeros((width, LANES), jnp.float32)] * 2
-            for s in range(taps):
-                got = shifted(prod_ref, slot, 8 - offset_ref[s, 0], width, offset_ref[s, 1])
-                total = [old + weight_ref[s] * new for old, new in zip(total, got)]
-            for i, half in enumerate(halves):
-                t_ref[k, :, half] = total[i]
-                mid_ref[slot, i, 8 : 8 + width, :] = total[i]
-                mid_ref[slot, i, 16 + width : 24 + width, :] = total[i][0:8]
-        moved = []
+            transposed(base + slot, prod_refs[slot], mid_refs[slot])
+
+    def stage_three(base):
         for slot in range(GROUP):
-            total = [jnp.zeros((ext, LANES), jnp.float32)] * 2
-            for s in range(taps):
-                got = shifted(mid_ref, slot, 8 + offset_ref[s, 0], ext, -offset_ref[s, 1])
-                total = [old + weight_ref[s] * new for old, new in zip(total, got)]
-            moved.append(total)
+            rolled(mid_refs[slot], roll_refs[slot])
+
+    stages = (stage_one, stage_two, stage_three, gather)
+    lag = len(stages) - 1
+    span = chunk // GROUP
+    chunks = block // chunk
+
+    def run(step, active):
+        for n in reversed(range(len(stages))):
+            if active(n):
+                stages[n]((step - n) * GROUP)
+
+    def body(step, carry):
+        run(step, lambda n: True)
+        return carry
+
+    enter(0)
+    for step in range(min(lag, span)):
+        run(step, lambda n: n <= step)
+    lax.fori_loop(lag, span, body, 0)
+
+    def following(index, carry):
+        enter(index)
+        lax.fori_loop(index * span, (index + 1) * span, body, 0)
+        leave(index - 1)
+        return carry
+
+    lax.fori_loop(1, chunks, following, 0)
+    steps = chunks * span
+    for step in range(steps, steps + lag):
+        run(step, lambda n: 0 <= step - n < steps)
+    leave(chunks - 1)
+
+
+def split(work):
+    return [work[n * GROUP : (n + 1) * GROUP] for n in range(3)]
+
+
+def clear(work):
+    for ref in split(work)[2]:
+        ref[...] = jnp.zeros_like(ref)
+
+
+def ordered_kernel(
+    started, weight_ref, offset_ref, place_ref, p_ref, ha_ref, hb_ref, w_ref, *rest
+):
+    levels, block, width, depth = p_ref.shape
+    before_ref = rest[0]
+    f_ref, t_ref, h_ref, *work = rest[3:] if started else rest
+    f_ref[...] = before_ref[...] if started else jnp.zeros_like(f_ref)
+    clear(work)
+    even = place_ref[1] == 0
+
+    def join(k, carry):
         for l in range(levels):
-            for i, half in enumerate(halves):
-                f_ref[l, 0:width, half] += sum(
-                    p_ref[l, base + slot, :, half].astype(jnp.float32) * moved[slot][i][0:width]
-                    for slot in range(GROUP)
-                )
-                f_ref[l, width:ext, half] += sum(
-                    h_ref[l, base + slot, :, half].astype(jnp.float32) * moved[slot][i][width:]
-                    for slot in range(GROUP)
-                )
+            from_a, from_b = ha_ref[l, k].astype(jnp.float32), hb_ref[l, k].astype(jnp.float32)
+            both = jnp.concatenate([jnp.where(even, from_a, from_b), jnp.where(even, from_b, from_a)], axis=0)
+            h_ref[l, k] = both.astype(h_ref.dtype)
         return carry
 
-    lax.fori_loop(0, block // GROUP, group, 0)
-
-
-def first_kernel(
-    weight_ref, offset_ref, p_ref, h_ref, w_ref, t_ref, f_ref, prod_ref, mid_ref
+    lax.fori_loop(0, block, join, 0)
+    nothing = lambda index: None
+    apply_core(weight_ref, offset_ref, p_ref, h_ref, w_ref, t_ref, f_ref, work, block, nothing, nothing)
+
+
+def next_kernel(
+    weight_ref, offset_ref, place_ref, p_hbm, h_hbm, m_ref, a_ref, b_ref, d_ref, old_ref,
+    t_hbm, f_ref, done_ref, w_ref, moment_ref, p_ref, h_ref, t_ref, p_sem, h_sem, t_sem, *work
 ):
-    @pl.when(pl.program_id(0) == 0)
-    def _():
-        f_ref[...] = jnp.zeros_like(f_ref)
-        mid_ref[...] = jnp.zeros_like(mid_ref)
-
-    apply_core(weight_ref, offset_ref, p_ref, h_ref, w_ref, t_ref, f_ref, prod_ref, mid_ref)
-
-
-def next_kernel(
-    weight_ref, offset_ref, place_ref, p_ref, h_ref, m_ref, a_ref, b_ref, d_ref, old_ref,
-    t_ref, f_ref, done_ref, w_ref, moment_ref, prod_ref, mid_ref,
-):
-    @pl.when(pl.program_id(0) == 0)
-    def _():
-        f_ref[...] = jnp.zeros_like(f_ref)
-        mid_ref[...] = jnp.zeros_like(mid_ref)
-        finish(place_ref, m_ref, a_ref, b_ref, d_ref, old_ref, done_ref, w_ref, moment_ref)
-
-    apply_core(weight_ref, offset_ref, p_ref, h_ref, w_ref, t_ref, f_ref, prod_ref, mid_ref)
+    chunks = p_sem.shape[0]
+    chunk = p_ref.shape[1] // chunks
+
+    def part(index):
+        return pl.ds(index * chunk, chunk)
+
+    def fetch(index):
+        at = part(index)
+        return (
+            pltpu.make_async_copy(p_hbm.at[:, at], p_ref.at[:, at], p_sem.at[index]),
+            pltpu.make_async_copy(h_hbm.at[:, at], h_ref.at[:, at], h_sem.at[index]),
+        )
+
+    def put(index):
+        at = part(index)
+        return pltpu.make_async_copy(t_ref.at[at], t_hbm.at[at], t_sem.at[index])
+
+    for index in range(chunks):
+        for copy in fetch(index):
+            copy.start()
+    f_ref[...] = jnp.zeros_like(f_ref)
+    clear(work)
+    finish(place_ref, m_ref, a_ref, b_ref, d_ref, old_ref, done_ref, w_ref, moment_ref)
+
+    def enter(index):
+        for copy in fetch(index):
+            copy.wait()
+
+    def leave(index):
+        put(index).start()
+
+    apply_core(weight_ref, offset_ref, p_ref, h_ref, w_ref, t_ref, f_ref, work, chunk, enter, leave)
+    for index in range(chunks):
+        put(index).wait()
 
 
 def finish(place_ref, m_ref, a_ref, b_ref, d_ref, old_ref, done_ref, w_ref, moment_ref):
@@ -239,8 +337,11 @@
     columns = lax.axis_size("col")
     halves = lax.axis_size("mem")
     ext = width + 2 * RADIUS
+    parts = 4
+    part = members // parts
     block = min(16, members)
     grid = members // block
+    chunks = members // block
     me = lax.axis_index("col")
     parity = me % 2
     place = jnp.stack([me * width, parity]).astype(jnp.int32)
@@ -257,15 +358,22 @@
 
     smem = pl.BlockSpec(memory_space=SMEM)
     vmem = pl.BlockSpec(memory_space=VMEM)
+    hbm = pl.BlockSpec(memory_space=pl.ANY)
 
     def shape(*dims, dtype=jnp.float32):
         return jax.ShapeDtypeStruct(dims, dtype)
 
     high = width - RADIUS
-    send_a = lax.dynamic_slice_in_dim(perturbations, jnp.where(even, high, 0), RADIUS, 2)
-    send_b = lax.dynamic_slice_in_dim(perturbations, jnp.where(even, 0, high), RADIUS, 2)
-    got_b, got_a = swap(send_a, send_b)
-    halo = edges(got_a, got_b, 2)
+
+    def send(index, after=None):
+        own = lax.slice_in_dim(perturbations, index * part, (index + 1) * part, axis=1)
+        send_a = lax.dynamic_slice_in_dim(own, jnp.where(even, high, 0), RADIUS, 2)
+        send_b = lax.dynamic_slice_in_dim(own, jnp.where(even, 0, high), RADIUS, 2)
+        if after is not None:
+            send_a, send_b, after = lax.optimization_barrier((send_a, send_b, after))
+        return swap(send_a, send_b), after
+
+    pieces = [send(index)[0] for index in range(min(AHEAD, parts))]
 
     row = lambda v: v.reshape(1, -1)
     fields, obs_a, obs_b = pl.pallas_call(
@@ -278,19 +386,17 @@
         in_specs=[smem] + [vmem] * 5,
         out_specs=(vmem, vmem, vmem),
         name="obs",
+        compiler_params=pltpu.CompilerParams(vmem_limit_bytes=LIMIT),
     )(place, row(obs_x), row(obs_y), row(obs_t), row(innovations), row(obs_rinv))
     side_b, side_a = swap(obs_a, obs_b)
     fields = jnp.concatenate([fields, edges(side_a, side_b, 2)], axis=2)
     diagonal, weighted = fields[0], fields[1]
 
-    p_spec = pl.BlockSpec((levels, block, width, depth), lambda i: (0, i, 0, 0))
-    h_spec = pl.BlockSpec((levels, block, 2 * RADIUS, depth), lambda i: (0, i, 0, 0))
     t_spec = pl.BlockSpec((block, width, depth), lambda i: (i, 0, 0))
     t_shape = shape(members, width, depth)
-    scratch = [
-        pltpu.VMEM((GROUP, 2, width + 16, LANES), jnp.float32),
-        pltpu.VMEM((GROUP, 2, width + 24, LANES), jnp.float32),
-    ]
+    scratch = []
+    for dims in ((2, width + 16), (2, width), (loc_weights.shape[0], 2, width + 24)):
+        scratch += [pltpu.VMEM((*dims, LANES), jnp.float32)] * GROUP
     cost = pl.CostEstimate(
         flops=2 * 30 * members * width * depth, bytes_accessed=10 * members * width * depth, transcendentals=0
     )
@@ -300,8 +406,7 @@
 
     f_spec, f_shape = whole(levels, ext, depth), shape(levels, ext, depth)
     own_spec, own_shape = whole(levels, width, depth), shape(levels, width, depth)
-    b_spec = whole(levels, 2 * RADIUS, depth)
-    m_spec, m_shape = whole(2, 8, LANES), shape(2, 8, LANES)
+    m_shape = shape(2, 8, LANES)
 
     def exchange(field):
         if halves == 2:
@@ -314,31 +419,57 @@
             in_specs=[smem, vmem, vmem],
             out_specs=(vmem, vmem, vmem),
             name="mid",
+            compiler_params=pltpu.CompilerParams(vmem_limit_bytes=LIMIT),
         )(place, field, partner)
         from_b, from_a = swap(a, b)
         return total, from_a, from_b
 
-    t0, f0 = pl.pallas_call(
-        first_kernel,
-        out_shape=(t_shape, f_shape),
-        grid=(grid,),
-        in_specs=[smem, smem, p_spec, h_spec, f_spec],
-        out_specs=(t_spec, f_spec),
-        scratch_shapes=scratch,
-        cost_estimate=cost,
-        name="first",
-    )(loc_weights, offsets, perturbations, halo, weighted)
+    h_shape = jax.ShapeDtypeStruct((levels, members, 2 * RADIUS, depth), perturbations.dtype)
+    earlier = ()
+    for index in range(parts):
+
+        def at(*dims, axis, index=index):
+            return pl.BlockSpec(dims, lambda i: tuple(index if n == axis else 0 for n in range(len(dims))))
+
+        side = pl.BlockSpec((levels, part, RADIUS, depth), lambda i: (0, 0, 0, 0))
+        from_b, from_a = pieces[index]
+        f0, t0, halo = earlier = pl.pallas_call(
+            functools.partial(ordered_kernel, index > 0),
+            out_shape=(f_shape, t_shape, h_shape),
+            grid=(1,),
+            in_specs=[smem] * 3
+            + [at(levels, part, width, depth, axis=1), side, side, f_spec]
+            + [f_spec, hbm, hbm][: len(earlier)],
+            out_specs=(f_spec, at(part, width, depth, axis=0), at(levels, part, 2 * RADIUS, depth, axis=1)),
+            scratch_shapes=scratch,
+            input_output_aliases={7: 0, 8: 1, 9: 2} if earlier else {},
+            cost_estimate=cost,
+            name="first",
+            compiler_params=pltpu.CompilerParams(vmem_limit_bytes=LIMIT),
+        )(loc_weights, offsets, place, perturbations, from_a, from_b, weighted, *earlier)
+        if index + AHEAD < parts:
+            piece, f0 = send(index + AHEAD, f0)
+            pieces.append(piece)
+            earlier = (f0, t0, halo)
 
     def following(pieces, old):
         return pl.pallas_call(
             next_kernel,
             out_shape=(t_shape, f_shape, own_shape, f_shape, m_shape),
-            grid=(grid,),
-            in_specs=[smem, smem, smem, p_spec, h_spec, f_spec, b_spec, b_spec, f_spec, f_spec],
-            out_specs=(t_spec, f_spec, own_spec, f_spec, m_spec),
-            scratch_shapes=scratch,
+            in_specs=[smem] * 3 + [hbm] * 2 + [vmem] * 5,
+            out_specs=(hbm, vmem, vmem, vmem, vmem),
+            scratch_shapes=[
+                pltpu.VMEM(perturbations.shape, perturbations.dtype),
+                pltpu.VMEM(halo.shape, halo.dtype),
+                pltpu.VMEM((members, width, depth), jnp.float32),
+                pltpu.SemaphoreType.DMA((chunks,)),
+                pltpu.SemaphoreType.DMA((chunks,)),
+                pltpu.SemaphoreType.DMA((chunks,)),
+            ]
+            + scratch,
             cost_estimate=cost,
             name="next",
+            compiler_params=pltpu.CompilerParams(vmem_limit_bytes=LIMIT),
         )(loc_weights, offsets, place, perturbations, halo, *pieces, diagonal, old)
 
     t1, f1, e0, w1, moment0 = following(exchange(f0), weighted)
@@ -349,6 +480,7 @@
         in_specs=[smem] + [vmem] * 7,
         out_specs=(vmem, vmem),
         name="last",
+        compiler_params=pltpu.CompilerParams(vmem_limit_bytes=LIMIT),
     )(place, *exchange(f2), diagonal, w2, moment0, moment1)
     step = 1
     while step < columns:
@@ -362,6 +494,7 @@
         out_specs=(t_spec, own_spec),
         scratch_shapes=[pltpu.VMEM((3, 8, LANES), jnp.float32)],
         name="final",
+        compiler_params=pltpu.CompilerParams(vmem_limit_bytes=LIMIT),
     )(moments, t0, t1, t2, e0, e1, e2)
     return control, increment
 

time: 162 us -> 132 us (0.81)
  Pallas kernels: 71.5 us -> 47.9 us
  other arithmetic: 8.45 us -> 0.13 us
  starting transfers between devices: 55.1 us -> 57 us
  local copies, waits for them, and re-layouts: 7.77 us -> 9.5 us
    pallas_call x2, Pallas kernels: 37.5 us -> 25.5 us  [following(): pl.pallas_call(next_kernel, out_shape=(t_shape, f_shape, own_shape, f_sha...]
    select_n x2 -> x1, other arithmetic: 4.94 us -> 0.03 us  [edges(): jnp.where(even, jnp.concatenate([a, b], axis=dim), jnp.concatenate([b, a]...]
    pallas_call x1, Pallas kernels: 6.98 us -> 3.58 us  [per_device(): pl.pallas_call(final_kernel, out_shape=(t_shape, own_shape), grid=(grid,)...]
    pallas_call x3, Pallas kernels: 4.86 us -> 1.68 us  [exchange(): pl.pallas_call(mid_kernel, out_shape=(f_shape, shape(levels, 2 * RADIUS,...]
    pallas_call x1 -> x4, Pallas kernels: 18.4 us -> 15.4 us  [per_device(): pl.pallas_call(functools.partial(ordered_kernel, index > 0), out_shape=(f...]
    slice x0 -> x1, local copies, waits for them, and re-layouts: none -> 2.55 us  [send(): lax.slice_in_dim(perturbations, index * part, (index + 1) * part, axis=1)]
    dynamic_slice x1 -> x3, local copies, waits for them, and re-layouts: 3.31 us -> 1.18 us  [send(): send_b = lax.dynamic_slice_in_dim(own, jnp.where(even, 0, high), RADIUS, 2)]
    ppermute x10 -> x16, starting transfers between devices: 36.4 us -> 37.9 us  [swap(): return (lax.ppermute(b, 'col', pair_b), lax.ppermute(a, 'col', pair_a))]
  transfers between devices with their start and end apart: 17 -> 23, of which waited for: 10 -> 9; matrix products, arithmetic and copies ran while one was open for 2% -> 3% of each run, Pallas kernels for 1% -> 9%
where the time goes in v2:
time: 132 us; the launch traced here: 131 us
  starting transfers between devices  57 us (43%)
  Pallas kernels  47.9 us (36%)
  waiting for transfers between devices  15.6 us (12%)
  local copies, waits for them, and re-layouts  9.5 us (7%)
    ppermute x16, starting transfers between devices, swap(): return (lax.ppermute(b, 'col', pair_b), lax.ppermute(a, 'col', pair_a))  37.9 us
    pallas_call x2, Pallas kernels, following(): pl.pallas_call(next_kernel, out_shape=(t_shape, f_shape, own_shape, f_sha...  25.5 us
    pallas_call x4, Pallas kernels, per_device(): pl.pallas_call(functools.partial(ordered_kernel, index > 0), out_shape=(f...  15.4 us
    ppermute x4, starting transfers between devices, per_device(): lax.ppermute(moments, 'col', [(i, i ^ step) for i in range(columns)])  13.6 us
    ppermute x3, waiting for transfers between devices, exchange(): partner = lax.ppermute(field, 'mem', [(0, 1), (1, 0)])  8.81 us
    ppermute x4, waiting for transfers between devices, per_device(): lax.ppermute(moments, 'col', [(i, i ^ step) for i in range(columns)])  6.37 us
    unnamed x19, local copies, waits for them, and re-layouts  5.78 us
    ppermute x3, starting transfers between devices, exchange(): partner = lax.ppermute(field, 'mem', [(0, 1), (1, 0)])  5.54 us
  transfers between devices with their start and end apart: 23, of which 9 were waited for; matrix products, arithmetic and copies ran while one was open for 3% of the time, Pallas kernels for 9%

profile of v2, /device:TPU:0, one launch (start us, length us, event | category | flops | bytes accessed | tf_op | source)
XLA Modules:
  0.0 131.2 jit_solution(13851629230919841838)
XLA Ops:
  0.6 0.1 pad_add_fusion.place_ref
  0.7 0.7 copy-done.3
  1.4 0.7 copy-done.4
  2.1 0.7 copy-done.5
  2.8 0.7 copy-done.6
  3.5 0.7 copy-done.7
  4.2 1.2 obs.1
  5.4 0.6 collective-permute-start.2
  5.9 0.7 collective-permute-start.3
  6.6 2.5 %fusion.3 = (bf16[4,32,16,256]{3,2,1,0:T(8,128)(2,1)S(1)}, bf16[4,32,16,256]{3,2,1,0:T(8,128)(2,1)S(1)}, bf16[4,32,16,256]{3,2,1,0:T(8,128)(2,1)S(1)}, bf16[4,32,16,256]{3,2,1,0:T(8,128)(2,1)S(1)}) fusion(bf16[4,128,16,256]{3,2,1,0:T(8,128)(2,1)} %p_hbm.3), kind=kLoop, calls=%fused_computation.16 | loop fusion | bytes 8388608 | tf_op jit(solution)/shard_map/slice | solution.py:369
  9.2 0.0 copy-start.8
  9.2 0.3 constant_dynamic-slice_fusion
  9.5 0.0 copy-start.2
  9.5 0.7 collective-permute-start.5
  10.2 5.2 %collective-permute-start.4 = (bf16[4,32,4,256]{3,2,1,0:T(4,128)(2,1)S(1)}, bf16[4,32,4,256]{3,2,1,0:T(4,128)(2,1)S(1)}, u32[]{:S(2)}, u32[]{:S(2)}) collective-permute-start(bf16[4,32,4,256]{3,2,1,0:T(4,128)(2,1)S(1)} %get-tuple-element.91), channel_id=1, source_target_pairs={{0,1},{1,0},{2,3},{3,2},{4,5},{5,4},{6,7},{7,6},{8,9},{9,8},{10,11... | collective-permute-start | bytes 786440 | tf_op jit(solution)/shard_map/ppermute | solution.py:354
  15.3 0.3 constant_dynamic-slice_fusion.4
  15.6 0.7 collective-permute-start.1
  16.3 0.0 collective-permute-done.2
  16.3 4.4 %collective-permute-start = (bf16[4,32,4,256]{3,2,1,0:T(4,128)(2,1)S(1)}, bf16[4,32,4,256]{3,2,1,0:T(4,128)(2,1)S(1)}, u32[]{:S(2)}, u32[]{:S(2)}) collective-permute-start(bf16[4,32,4,256]{3,2,1,0:T(4,128)(2,1)S(1)} %get-tuple-element.95), channel_id=1, source_target_pairs={{0,1},{1,0},{2,3},{3,2},{4,5},{5,4},{6,7},{7,6},{8,9},{9,8},{10,11... | collective-permute-start | bytes 786440 | tf_op jit(solution)/shard_map/ppermute | solution.py:354
  20.7 0.6 constant_dynamic-slice_fusion.2
  21.4 0.1 copy.24.offset_ref
  21.5 0.0 collective-permute-done.4.ha_ref
  21.5 0.0 copy-start
  21.6 2.2 %copy-done = bf16[4,128,16,256]{3,2,1,0:T(8,128)(2,1)S(1)} copy-done((bf16[4,128,16,256]{3,2,1,0:T(8,128)(2,1)S(1)}, bf16[4,128,16,256]{3,2,1,0:T(8,128)(2,1)}, u32[]{:S(2)}) %copy-start) | copy-done | bytes 4194328
  23.7 3.8 %first.4 = (f32[4,24,256]{2,1,0:T(8,128)S(1)}, f32[128,16,256]{2,1,0:T(8,128)S(1)}, bf16[4,128,8,256]{3,2,1,0:T(8,128)(2,1)S(1)}) custom-call(f32[7]{0:T(128)S(1)} %copy-done.2, s32[7,2]{1,0:T(8,128)S(1)} %copy.24.offset_ref, s32[2]{0:T(128)S(1)} %pad_add_fusion.place_ref, bf16[4,128,16,256]{3,2,1,0:T(8,128)(2,1)S(1)} %copy-done, ...), custom_call_target="tpu_custom_call" | custom-call | flops 31457280 | bytes 5242880 | tf_op jit(solution)/shard_map/first/pallas_call | solution.py:436
  27.6 0.1 collective-permute-start.8
  27.7 0.7 collective-permute-start.9
  28.3 0.0 collective-permute-done.1.hb_ref
  28.4 3.8 %first.5 = (f32[4,24,256]{2,1,0:T(8,128)S(1)}, f32[128,16,256]{2,1,0:T(8,128)S(1)}, bf16[4,128,8,256]{3,2,1,0:T(8,128)(2,1)S(1)}) custom-call(f32[7]{0:T(128)S(1)} %copy-done.2, s32[7,2]{1,0:T(8,128)S(1)} %copy.24.offset_ref, s32[2]{0:T(128)S(1)} %pad_add_fusion.place_ref, ...), custom_call_target="tpu_custom_call", output_to_operand_aliasing={{0}: (7, {}), {1}: (8, {}), {2}: (9, {})} | custom-call | flops 31457280 | bytes 5242880 | tf_op jit(solution)/shard_map/first/pallas_call | solution.py:436
  32.2 3.4 %collective-permute-start.6 = (bf16[4,32,4,256]{3,2,1,0:T(4,128)(2,1)S(1)}, bf16[4,32,4,256]{3,2,1,0:T(4,128)(2,1)S(1)}, u32[]{:S(2)}, u32[]{:S(2)}) collective-permute-start(bf16[4,32,4,256]{3,2,1,0:T(4,128)(2,1)S(1)} %get-tuple-element.52), channel_id=1, source_target_pairs={{0,1},{1,0},{2,3},{3,2},{4,5},{5,4},{6,7},{7,6},{8,9},{9,8},{10,11... | collective-permute-start | bytes 786440 | tf_op jit(solution)/shard_map/ppermute | solution.py:354
  35.6 0.7 collective-permute-start.7
  36.3 3.8 %first.6 = (f32[4,24,256]{2,1,0:T(8,128)S(1)}, f32[128,16,256]{2,1,0:T(8,128)S(1)}, bf16[4,128,8,256]{3,2,1,0:T(8,128)(2,1)S(1)}) custom-call(f32[7]{0:T(128)S(1)} %copy-done.2, s32[7,2]{1,0:T(8,128)S(1)} %copy.24.offset_ref, s32[2]{0:T(128)S(1)} %pad_add_fusion.place_ref, ...), custom_call_target="tpu_custom_call", output_to_operand_aliasing={{0}: (7, {}), {1}: (8, {}), {2}: (9, {})} | custom-call | flops 31457280 | bytes 5242880 | tf_op jit(solution)/shard_map/first/pallas_call | solution.py:436
  40.2 0.0 copy-start.1
  40.2 3.8 %first.7 = (f32[4,24,256]{2,1,0:T(8,128)S(1)}, f32[128,16,256]{2,1,0:T(8,128)S(1)}, bf16[4,128,8,256]{3,2,1,0:T(8,128)(2,1)S(1)}) custom-call(f32[7]{0:T(128)S(1)} %copy-done.2, s32[7,2]{1,0:T(8,128)S(1)} %copy.24.offset_ref, s32[2]{0:T(128)S(1)} %pad_add_fusion.place_ref, ...), custom_call_target="tpu_custom_call", output_to_operand_aliasing={{0}: (7, {}), {1}: (8, {}), {2}: (9, {})} | custom-call | flops 31457280 | bytes 5242880 | tf_op jit(solution)/shard_map/first/pallas_call | solution.py:436
  44.1 2.4 %collective-permute-start.10 = (f32[4,24,256]{2,1,0:T(8,128)S(1)}, f32[4,24,256]{2,1,0:T(8,128)S(1)}, u32[]{:S(2)}, u32[]{:S(2)}) collective-permute-start(f32[4,24,256]{2,1,0:T(8,128)S(1)} %get-tuple-element.63.f_ref), channel_id=1, source_target_pairs={{0,16},{16,0},{1,17},{17,1},{2,18},{18,2},{3,19},{19,3},{4,20},{20... | collective-permute-start | bytes 294920 | tf_op jit(solution)/shard_map/ppermute | solution.py:413
  46.4 2.6 %collective-permute-done.10.r_ref = f32[4,24,256]{2,1,0:T(8,128)S(1)} collective-permute-done((f32[4,24,256]{2,1,0:T(8,128)S(1)}, f32[4,24,256]{2,1,0:T(8,128)S(1)}, u32[]{:S(2)}, u32[]{:S(2)}) %collective-permute-start.10) | collective-permute-done | bytes 98336 | tf_op jit(solution)/shard_map/ppermute | solution.py:413
  49.0 0.6 mid.3
  49.6 8.3 %collective-permute-start.11 = (f32[4,8,256]{2,1,0:T(8,128)S(1)}, f32[4,8,256]{2,1,0:T(8,128)S(1)}, u32[]{:S(2)}, u32[]{:S(2)}) collective-permute-start(f32[4,8,256]{2,1,0:T(8,128)S(1)} %get-tuple-element.65), channel_id=1, source_target_pairs={{0,1},{1,0},{2,3},{3,2},{4,5},{5,4},{6,7},{7,6},{8,9},{9,8},{10,11... | collective-permute-start | bytes 98312 | tf_op jit(solution)/shard_map/ppermute | solution.py:354
  57.9 0.7 collective-permute-start.12
  58.5 0.2 collective-permute-done.11.a_ref
  58.8 12.8 %next.2 = (f32[128,16,256]{2,1,0:T(8,128)S(1)}, f32[4,24,256]{2,1,0:T(8,128)S(1)}, f32[4,16,256]{2,1,0:T(8,128)S(1)}, f32[4,24,256]{2,1,0:T(8,128)S(1)}, f32[2,8,128]{2,1,0:T(8,128)S(1)}) custom-call(f32[7]{0:T(128)S(1)} %copy-done.2, s32[7,2]{1,0:T(8,128)S(1)} %copy.24.offset_ref, s32[2]{0:T(128)S(1)} %pad_add_fusion.place_ref, ...), custom_call_target="tpu_custom_call" | custom-call | flops 31457280 | bytes 5242880 | tf_op jit(solution)/shard_map/next/pallas_call | solution.py:456
  71.5 1.6 %collective-permute-start.13 = (f32[4,24,256]{2,1,0:T(8,128)S(1)}, f32[4,24,256]{2,1,0:T(8,128)S(1)}, u32[]{:S(2)}, u32[]{:S(2)}) collective-permute-start(f32[4,24,256]{2,1,0:T(8,128)S(1)} %get-tuple-element.67.f_ref), channel_id=1, source_target_pairs={{0,16},{16,0},{1,17},{17,1},{2,18},{18,2},{3,19},{19,3},{4,20},{20... | collective-permute-start | bytes 294920 | tf_op jit(solution)/shard_map/ppermute | solution.py:413
  73.1 3.1 %collective-permute-done.13.r_ref = f32[4,24,256]{2,1,0:T(8,128)S(1)} collective-permute-done((f32[4,24,256]{2,1,0:T(8,128)S(1)}, f32[4,24,256]{2,1,0:T(8,128)S(1)}, u32[]{:S(2)}, u32[]{:S(2)}) %collective-permute-start.13) | collective-permute-done | bytes 98336 | tf_op jit(solution)/shard_map/ppermute | solution.py:413
  76.2 0.6 mid.4
  76.8 5.2 %collective-permute-start.14 = (f32[4,8,256]{2,1,0:T(8,128)S(1)}, f32[4,8,256]{2,1,0:T(8,128)S(1)}, u32[]{:S(2)}, u32[]{:S(2)}) collective-permute-start(f32[4,8,256]{2,1,0:T(8,128)S(1)} %get-tuple-element.69), channel_id=1, source_target_pairs={{0,1},{1,0},{2,3},{3,2},{4,5},{5,4},{6,7},{7,6},{8,9},{9,8},{10,11... | collective-permute-start | bytes 98312 | tf_op jit(solution)/shard_map/ppermute | solution.py:354
  82.0 0.8 collective-permute-start.15
  82.8 0.0 collective-permute-done.14.a_ref
  82.8 12.8 %next.3 = (f32[128,16,256]{2,1,0:T(8,128)S(1)}, f32[4,24,256]{2,1,0:T(8,128)S(1)}, f32[4,16,256]{2,1,0:T(8,128)S(1)}, f32[4,24,256]{2,1,0:T(8,128)S(1)}, f32[2,8,128]{2,1,0:T(8,128)S(1)}) custom-call(f32[7]{0:T(128)S(1)} %copy-done.2, s32[7,2]{1,0:T(8,128)S(1)} %copy.24.offset_ref, s32[2]{0:T(128)S(1)} %pad_add_fusion.place_ref, ...), custom_call_target="tpu_custom_call" | custom-call | flops 31457280 | bytes 5242880 | tf_op jit(solution)/shard_map/next/pallas_call | solution.py:456
  95.6 1.6 %collective-permute-start.16 = (f32[4,24,256]{2,1,0:T(8,128)S(1)}, f32[4,24,256]{2,1,0:T(8,128)S(1)}, u32[]{:S(2)}, u32[]{:S(2)}) collective-permute-start(f32[4,24,256]{2,1,0:T(8,128)S(1)} %get-tuple-element.72.f_ref), channel_id=1, source_target_pairs={{0,16},{16,0},{1,17},{17,1},{2,18},{18,2},{3,19},{19,3},{4,20},{20... | collective-permute-start | bytes 294920 | tf_op jit(solution)/shard_map/ppermute | solution.py:413
  97.2 3.1 %collective-permute-done.16.r_ref = f32[4,24,256]{2,1,0:T(8,128)S(1)} collective-permute-done((f32[4,24,256]{2,1,0:T(8,128)S(1)}, f32[4,24,256]{2,1,0:T(8,128)S(1)}, u32[]{:S(2)}, u32[]{:S(2)}) %collective-permute-start.16) | collective-permute-done | bytes 98336 | tf_op jit(solution)/shard_map/ppermute | solution.py:413
  100.3 0.6 mid.5
  100.9 5.3 %collective-permute-start.17 = (f32[4,8,256]{2,1,0:T(8,128)S(1)}, f32[4,8,256]{2,1,0:T(8,128)S(1)}, u32[]{:S(2)}, u32[]{:S(2)}) collective-permute-start(f32[4,8,256]{2,1,0:T(8,128)S(1)} %get-tuple-element.74), channel_id=1, source_target_pairs={{0,1},{1,0},{2,3},{3,2},{4,5},{5,4},{6,7},{7,6},{8,9},{9,8},{10,11... | collective-permute-start | bytes 98312 | tf_op jit(solution)/shard_map/ppermute | solution.py:354
  106.1 0.7 collective-permute-start.18
  106.8 0.2 collective-permute-done.17.a_ref
  107.0 0.6 last.1
  107.6 6.5 %collective-permute-start.19 = (f32[8,128]{1,0:T(8,128)S(1)}, f32[8,128]{1,0:T(8,128)S(1)}, u32[]{:S(2)}, u32[]{:S(2)}) collective-permute-start(f32[8,128]{1,0:T(8,128)S(1)} %get-tuple-element.79), channel_id=1, source_target_pairs={{0,1},{1,0},{2,3},{3,2},{4,5},{5,4},{6,7},{7,6},{8,9},{9,8},{10,11... | collective-permute-start | bytes 12296 | tf_op jit(solution)/shard_map/ppermute | solution.py:487
  114.1 0.8 collective-permute-done.19
  115.0 2.9 %collective-permute-start.20 = (f32[8,128]{1,0:T(8,128)S(1)}, f32[8,128]{1,0:T(8,128)S(1)}, u32[]{:S(2)}, u32[]{:S(2)}) collective-permute-start(f32[8,128]{1,0:T(8,128)S(1)} %add.13), channel_id=1, source_target_pairs={{0,2},{1,3},{2,0},{3,1},{4,6},{5,7},{6,4},{7,5},{8,10},{9,11},{10,... | collective-permute-start | bytes 12296 | tf_op jit(solution)/shard_map/ppermute | solution.py:487
  117.9 1.6 %collective-permute-done.20 = f32[8,128]{1,0:T(8,128)S(1)} collective-permute-done((f32[8,128]{1,0:T(8,128)S(1)}, f32[8,128]{1,0:T(8,128)S(1)}, u32[]{:S(2)}, u32[]{:S(2)}) %collective-permute-start.20) | collective-permute-done | bytes 4128 | tf_op jit(solution)/shard_map/ppermute | solution.py:487
  119.5 1.6 %collective-permute-start.21 = (f32[8,128]{1,0:T(8,128)S(1)}, f32[8,128]{1,0:T(8,128)S(1)}, u32[]{:S(2)}, u32[]{:S(2)}) collective-permute-start(f32[8,128]{1,0:T(8,128)S(1)} %add.26), channel_id=1, source_target_pairs={{0,4},{1,5},{2,6},{3,7},{4,0},{5,1},{6,2},{7,3},{8,12},{9,13},{10,... | collective-permute-start | bytes 12296 | tf_op jit(solution)/shard_map/ppermute | solution.py:487
  121.0 2.0 %collective-permute-done.21 = f32[8,128]{1,0:T(8,128)S(1)} collective-permute-done((f32[8,128]{1,0:T(8,128)S(1)}, f32[8,128]{1,0:T(8,128)S(1)}, u32[]{:S(2)}, u32[]{:S(2)}) %collective-permute-start.21) | collective-permute-done | bytes 4128 | tf_op jit(solution)/shard_map/ppermute | solution.py:487
  123.1 2.6 %collective-permute-start.22 = (f32[8,128]{1,0:T(8,128)S(1)}, f32[8,128]{1,0:T(8,128)S(1)}, u32[]{:S(2)}, u32[]{:S(2)}) collective-permute-start(f32[8,128]{1,0:T(8,128)S(1)} %add.27), channel_id=1, source_target_pairs={{0,8},{1,9},{2,10},{3,11},{4,12},{5,13},{6,14},{7,15},{8,0},{9,1},... | collective-permute-start | bytes 12296 | tf_op jit(solution)/shard_map/ppermute | solution.py:487
  125.7 1.9 %collective-permute-done.22 = f32[8,128]{1,0:T(8,128)S(1)} collective-permute-done((f32[8,128]{1,0:T(8,128)S(1)}, f32[8,128]{1,0:T(8,128)S(1)}, u32[]{:S(2)}, u32[]{:S(2)}) %collective-permute-start.22) | collective-permute-done | bytes 4128 | tf_op jit(solution)/shard_map/ppermute | solution.py:487
  127.6 3.6 %final.1 = (f32[128,16,256]{2,1,0:T(8,128)}, f32[4,16,256]{2,1,0:T(8,128)}) custom-call(f32[8,128]{1,0:T(8,128)S(1)} %add.28.moment_ref, f32[128,16,256]{2,1,0:T(8,128)S(1)} %get-tuple-element.80.t0_ref, f32[128,16,256]{2,1,0:T(8,128)S(1)} %get-tuple-element.81.t1_ref, f32[128,16,256]{2,1,0:T(8,128)S(1)} %get-tuple-element.82.t2_ref, ...), custom_call_target="tpu_custom_call" | custom-call | tf_op jit(solution)/shard_map/final/pallas_call | solution.py:489
  (24 shorter events, 0.1 us)
Async XLA Ops:
  0.7 0.7 copy-start.3
  1.4 0.7 copy-start.4
  2.1 0.7 copy-start.5
  2.8 0.7 copy-start.6
  3.5 0.7 copy-start.7
  5.4 10.9 %collective-permute-start.2 = (f32[2,4,4,256]{3,2,1,0:T(4,128)S(1)}, f32[2,4,4,256]{3,2,1,0:T(4,128)S(1)}, u32[]{:S(2)}, u32[]{:S(2)}) collective-permute-start(f32[2,4,4,256]{3,2,1,0:T(4,128)S(1)} %get-tuple-element.45), channel_id=1, source_target_pairs={{0,1},{1,0},{2,3},{3,2},{4,5},{5,4},{6,7},{7,6},{8,9},{9,8},{10,11... | collective-permute-start | bytes 98312 | tf_op jit(solution)/shard_map/ppermute | solution.py:354
  5.9 15.5 %collective-permute-start.3 = (f32[2,4,4,256]{3,2,1,0:T(4,128)S(1)}, f32[2,4,4,256]{3,2,1,0:T(4,128)S(1)}, u32[]{:S(2)}, u32[]{:S(2)}) collective-permute-start(f32[2,4,4,256]{3,2,1,0:T(4,128)S(1)} %get-tuple-element.46), channel_id=1, source_target_pairs={{1,2},{3,4},{5,6},{7,8},{9,10},{11,12},{13,14},{2,1},{4,3},{6,5},{... | collective-permute-start | bytes 98312 | tf_op jit(solution)/shard_map/ppermute | solution.py:354
  9.2 12.2 %copy-start.8 = (s32[7,2]{0,1:T(2,128)S(1)}, s32[7,2]{0,1:T(2,128)}, u32[]{:S(2)}) copy-start(s32[7,2]{0,1:T(2,128)} %param.10) | copy-start | bytes 172
  9.5 12.1 %copy-start.2 = (f32[7]{0:T(128)S(1)}, f32[7]{0:T(128)}, u32[]{:S(2)}) copy-start(f32[7]{0:T(128)} %weight_ref.11) | copy-start | bytes 88
  9.5 12.0 %collective-permute-start.5 = (bf16[4,32,4,256]{3,2,1,0:T(4,128)(2,1)S(1)}, bf16[4,32,4,256]{3,2,1,0:T(4,128)(2,1)S(1)}, u32[]{:S(2)}, u32[]{:S(2)}) collective-permute-start(bf16[4,32,4,256]{3,2,1,0:T(4,128)(2,1)S(1)} %get-tuple-element.90), channel_id=1, source_target_pairs={{1,2},{3,4},{5,6},{7,8},{9,10},{11,12},{13,14},{2,1},{4,3},{6,5},{... | collective-permute-start | bytes 786440 | tf_op jit(solution)/shard_map/ppermute | solution.py:354
  10.2 11.4 %collective-permute-start.4 = (bf16[4,32,4,256]{3,2,1,0:T(4,128)(2,1)S(1)}, bf16[4,32,4,256]{3,2,1,0:T(4,128)(2,1)S(1)}, u32[]{:S(2)}, u32[]{:S(2)}) collective-permute-start(bf16[4,32,4,256]{3,2,1,0:T(4,128)(2,1)S(1)} %get-tuple-element.91), channel_id=1, source_target_pairs={{0,1},{1,0},{2,3},{3,2},{4,5},{5,4},{6,7},{7,6},{8,9},{9,8},{10,11... | collective-permute-start | bytes 786440 | tf_op jit(solution)/shard_map/ppermute | solution.py:354
  15.6 12.7 %collective-permute-start.1 = (bf16[4,32,4,256]{3,2,1,0:T(4,128)(2,1)S(1)}, bf16[4,32,4,256]{3,2,1,0:T(4,128)(2,1)S(1)}, u32[]{:S(2)}, u32[]{:S(2)}) collective-permute-start(bf16[4,32,4,256]{3,2,1,0:T(4,128)(2,1)S(1)} %get-tuple-element.94), channel_id=1, source_target_pairs={{1,2},{3,4},{5,6},{7,8},{9,10},{11,12},{13,14},{2,1},{4,3},{6,5},{... | collective-permute-start | bytes 786440 | tf_op jit(solution)/shard_map/ppermute | solution.py:354
  16.3 12.0 %collective-permute-start = (bf16[4,32,4,256]{3,2,1,0:T(4,128)(2,1)S(1)}, bf16[4,32,4,256]{3,2,1,0:T(4,128)(2,1)S(1)}, u32[]{:S(2)}, u32[]{:S(2)}) collective-permute-start(bf16[4,32,4,256]{3,2,1,0:T(4,128)(2,1)S(1)} %get-tuple-element.95), channel_id=1, source_target_pairs={{0,1},{1,0},{2,3},{3,2},{4,5},{5,4},{6,7},{7,6},{8,9},{9,8},{10,11... | collective-permute-start | bytes 786440 | tf_op jit(solution)/shard_map/ppermute | solution.py:354
  21.5 2.2 %copy-start = (bf16[4,128,16,256]{3,2,1,0:T(8,128)(2,1)S(1)}, bf16[4,128,16,256]{3,2,1,0:T(8,128)(2,1)}, u32[]{:S(2)}) copy-start(bf16[4,128,16,256]{3,2,1,0:T(8,128)(2,1)} %p_hbm.3) | copy-start | bytes 12582916
  27.6 8.7 %collective-permute-start.8 = (bf16[4,32,4,256]{3,2,1,0:T(4,128)(2,1)S(1)}, bf16[4,32,4,256]{3,2,1,0:T(4,128)(2,1)S(1)}, u32[]{:S(2)}, u32[]{:S(2)}) collective-permute-start(bf16[4,32,4,256]{3,2,1,0:T(4,128)(2,1)S(1)} %get-tuple-element.54), channel_id=1, source_target_pairs={{0,1},{1,0},{2,3},{3,2},{4,5},{5,4},{6,7},{7,6},{8,9},{9,8},{10,11... | collective-permute-start | bytes 786440 | tf_op jit(solution)/shard_map/ppermute | solution.py:354
  27.7 8.7 %collective-permute-start.9 = (bf16[4,32,4,256]{3,2,1,0:T(4,128)(2,1)S(1)}, bf16[4,32,4,256]{3,2,1,0:T(4,128)(2,1)S(1)}, u32[]{:S(2)}, u32[]{:S(2)}) collective-permute-start(bf16[4,32,4,256]{3,2,1,0:T(4,128)(2,1)S(1)} %get-tuple-element.55), channel_id=1, source_target_pairs={{1,2},{3,4},{5,6},{7,8},{9,10},{11,12},{13,14},{2,1},{4,3},{6,5},{... | collective-permute-start | bytes 786440 | tf_op jit(solution)/shard_map/ppermute | solution.py:354
  32.2 8.0 %collective-permute-start.6 = (bf16[4,32,4,256]{3,2,1,0:T(4,128)(2,1)S(1)}, bf16[4,32,4,256]{3,2,1,0:T(4,128)(2,1)S(1)}, u32[]{:S(2)}, u32[]{:S(2)}) collective-permute-start(bf16[4,32,4,256]{3,2,1,0:T(4,128)(2,1)S(1)} %get-tuple-element.52), channel_id=1, source_target_pairs={{0,1},{1,0},{2,3},{3,2},{4,5},{5,4},{6,7},{7,6},{8,9},{9,8},{10,11... | collective-permute-start | bytes 786440 | tf_op jit(solution)/shard_map/ppermute | solution.py:354
  35.6 4.6 %collective-permute-start.7 = (bf16[4,32,4,256]{3,2,1,0:T(4,128)(2,1)S(1)}, bf16[4,32,4,256]{3,2,1,0:T(4,128)(2,1)S(1)}, u32[]{:S(2)}, u32[]{:S(2)}) collective-permute-start(bf16[4,32,4,256]{3,2,1,0:T(4,128)(2,1)S(1)} %get-tuple-element.53), channel_id=1, source_target_pairs={{1,2},{3,4},{5,6},{7,8},{9,10},{11,12},{13,14},{2,1},{4,3},{6,5},{... | collective-permute-start | bytes 786440 | tf_op jit(solution)/shard_map/ppermute | solution.py:354
  40.2 18.6 %copy-start.1 = (bf16[4,128,16,256]{3,2,1,0:T(8,128)(2,1)S(1)}, bf16[4,128,16,256]{3,2,1,0:T(8,128)(2,1)}, u32[]{:S(2)}) copy-start(bf16[4,128,16,256]{3,2,1,0:T(8,128)(2,1)} %p_hbm.3) | copy-start | bytes 12582916
  44.1 5.0 %collective-permute-start.10 = (f32[4,24,256]{2,1,0:T(8,128)S(1)}, f32[4,24,256]{2,1,0:T(8,128)S(1)}, u32[]{:S(2)}, u32[]{:S(2)}) collective-permute-start(f32[4,24,256]{2,1,0:T(8,128)S(1)} %get-tuple-element.63.f_ref), channel_id=1, source_target_pairs={{0,16},{16,0},{1,17},{17,1},{2,18},{18,2},{3,19},{19,3},{4,20},{20... | collective-permute-start | bytes 294920 | tf_op jit(solution)/shard_map/ppermute | solution.py:413
  49.6 9.1 %collective-permute-start.11 = (f32[4,8,256]{2,1,0:T(8,128)S(1)}, f32[4,8,256]{2,1,0:T(8,128)S(1)}, u32[]{:S(2)}, u32[]{:S(2)}) collective-permute-start(f32[4,8,256]{2,1,0:T(8,128)S(1)} %get-tuple-element.65), channel_id=1, source_target_pairs={{0,1},{1,0},{2,3},{3,2},{4,5},{5,4},{6,7},{7,6},{8,9},{9,8},{10,11... | collective-permute-start | bytes 98312 | tf_op jit(solution)/shard_map/ppermute | solution.py:354
  57.9 0.9 collective-permute-start.12
  71.5 4.7 %collective-permute-start.13 = (f32[4,24,256]{2,1,0:T(8,128)S(1)}, f32[4,24,256]{2,1,0:T(8,128)S(1)}, u32[]{:S(2)}, u32[]{:S(2)}) collective-permute-start(f32[4,24,256]{2,1,0:T(8,128)S(1)} %get-tuple-element.67.f_ref), channel_id=1, source_target_pairs={{0,16},{16,0},{1,17},{17,1},{2,18},{18,2},{3,19},{19,3},{4,20},{20... | collective-permute-start | bytes 294920 | tf_op jit(solution)/shard_map/ppermute | solution.py:413
  76.8 6.1 %collective-permute-start.14 = (f32[4,8,256]{2,1,0:T(8,128)S(1)}, f32[4,8,256]{2,1,0:T(8,128)S(1)}, u32[]{:S(2)}, u32[]{:S(2)}) collective-permute-start(f32[4,8,256]{2,1,0:T(8,128)S(1)} %get-tuple-element.69), channel_id=1, source_target_pairs={{0,1},{1,0},{2,3},{3,2},{4,5},{5,4},{6,7},{7,6},{8,9},{9,8},{10,11... | collective-permute-start | bytes 98312 | tf_op jit(solution)/shard_map/ppermute | solution.py:354
  82.0 0.9 collective-permute-start.15
  95.6 4.7 %collective-permute-start.16 = (f32[4,24,256]{2,1,0:T(8,128)S(1)}, f32[4,24,256]{2,1,0:T(8,128)S(1)}, u32[]{:S(2)}, u32[]{:S(2)}) collective-permute-start(f32[4,24,256]{2,1,0:T(8,128)S(1)} %get-tuple-element.72.f_ref), channel_id=1, source_target_pairs={{0,16},{16,0},{1,17},{17,1},{2,18},{18,2},{3,19},{19,3},{4,20},{20... | collective-permute-start | bytes 294920 | tf_op jit(solution)/shard_map/ppermute | solution.py:413
  100.9 6.2 %collective-permute-start.17 = (f32[4,8,256]{2,1,0:T(8,128)S(1)}, f32[4,8,256]{2,1,0:T(8,128)S(1)}, u32[]{:S(2)}, u32[]{:S(2)}) collective-permute-start(f32[4,8,256]{2,1,0:T(8,128)S(1)} %get-tuple-element.74), channel_id=1, source_target_pairs={{0,1},{1,0},{2,3},{3,2},{4,5},{5,4},{6,7},{7,6},{8,9},{9,8},{10,11... | collective-permute-start | bytes 98312 | tf_op jit(solution)/shard_map/ppermute | solution.py:354
  106.1 0.9 collective-permute-start.18
  107.6 7.4 %collective-permute-start.19 = (f32[8,128]{1,0:T(8,128)S(1)}, f32[8,128]{1,0:T(8,128)S(1)}, u32[]{:S(2)}, u32[]{:S(2)}) collective-permute-start(f32[8,128]{1,0:T(8,128)S(1)} %get-tuple-element.79), channel_id=1, source_target_pairs={{0,1},{1,0},{2,3},{3,2},{4,5},{5,4},{6,7},{7,6},{8,9},{9,8},{10,11... | collective-permute-start | bytes 12296 | tf_op jit(solution)/shard_map/ppermute | solution.py:487
  115.0 4.5 %collective-permute-start.20 = (f32[8,128]{1,0:T(8,128)S(1)}, f32[8,128]{1,0:T(8,128)S(1)}, u32[]{:S(2)}, u32[]{:S(2)}) collective-permute-start(f32[8,128]{1,0:T(8,128)S(1)} %add.13), channel_id=1, source_target_pairs={{0,2},{1,3},{2,0},{3,1},{4,6},{5,7},{6,4},{7,5},{8,10},{9,11},{10,... | collective-permute-start | bytes 12296 | tf_op jit(solution)/shard_map/ppermute | solution.py:487
  119.5 3.6 %collective-permute-start.21 = (f32[8,128]{1,0:T(8,128)S(1)}, f32[8,128]{1,0:T(8,128)S(1)}, u32[]{:S(2)}, u32[]{:S(2)}) collective-permute-start(f32[8,128]{1,0:T(8,128)S(1)} %add.26), channel_id=1, source_target_pairs={{0,4},{1,5},{2,6},{3,7},{4,0},{5,1},{6,2},{7,3},{8,12},{9,13},{10,... | collective-permute-start | bytes 12296 | tf_op jit(solution)/shard_map/ppermute | solution.py:487
  123.1 4.5 %collective-permute-start.22 = (f32[8,128]{1,0:T(8,128)S(1)}, f32[8,128]{1,0:T(8,128)S(1)}, u32[]{:S(2)}, u32[]{:S(2)}) collective-permute-start(f32[8,128]{1,0:T(8,128)S(1)} %add.27), channel_id=1, source_target_pairs={{0,8},{1,9},{2,10},{3,11},{4,12},{5,13},{6,14},{7,15},{8,0},{9,1},... | collective-permute-start | bytes 12296 | tf_op jit(solution)/shard_map/ppermute | solution.py:487

commit v3 on v2

--- a/solution.py
+++ b/solution.py
@@ -7,12 +7,17 @@
 from jax.experimental.pallas import tpu as pltpu
 from jax.sharding import PartitionSpec as P
 
+
 RADIUS = 4
 SCALE = 2.0**-12
 TINY = 3e-8
 GROUP = 4
 LIMIT = 20 << 20
-AHEAD = 2
+FIRST_LIMIT = 20 << 20
+PACK_LIMIT = 20 << 20
+FULL_LIMIT = 67043328
+PARTS = 4
+AHEAD = 3
 LANES = 128
 SMEM = pltpu.MemorySpace.SMEM
 VMEM = pltpu.MemorySpace.VMEM
@@ -26,7 +31,43 @@
     return hi, mid, low
 
 
-def obs_kernel(place_ref, ox_ref, oy_ref, ot_ref, inno_ref, rinv_ref, field_ref, a_ref, b_ref):
+def pack_kernel(place_ref, p_hbm, *refs):
+    *sends, p_ref, sem = refs
+    even = place_ref[1] == 0
+    levels, part, radius, _ = sends[0].shape
+    width = p_ref.shape[2]
+    parts = len(sends) // 2
+    copies = [
+        pltpu.make_async_copy(
+            p_hbm.at[:, pl.ds(index * part, part)], p_ref.at[:, pl.ds(index * part, part)], sem.at[index]
+        )
+        for index in range(parts)
+    ]
+    for copy in copies:
+        copy.start()
+    for index in range(parts):
+        copies[index].wait()
+        to_a, to_b = sends[2 * index], sends[2 * index + 1]
+
+        def cut(k, carry, index=index, to_a=to_a, to_b=to_b):
+            for l in range(levels):
+                value = p_ref[l, index * part + k].astype(jnp.float32)
+                low, high = value[:radius], value[width - radius :]
+                to_a[l, k] = jnp.where(even, high, low).astype(to_a.dtype)
+                to_b[l, k] = jnp.where(even, low, high).astype(to_b.dtype)
+            return carry
+
+        lax.fori_loop(0, part, cut, 0, unroll=4)
+
+
+def obs_kernel(place_ref, *refs):
+    sources, (field_ref, a_ref, b_ref), targets, sem = refs[:5], refs[5:8], refs[8:13], refs[13]
+    copies = [pltpu.make_async_copy(*pair, sem.at[n]) for n, pair in enumerate(zip(sources, targets))]
+    for copy in copies:
+        copy.start()
+    for copy in copies:
+        copy.wait()
+    ox_ref, oy_ref, ot_ref, inno_ref, rinv_ref = targets
     _, levels, width, depth = field_ref.shape
     cells = levels * width
     count = ox_ref.shape[1]
@@ -55,6 +96,16 @@
     b_ref[...] = jnp.where(even, low, high)
 
 
+def sides_kernel(place_ref, field_ref, a_ref, b_ref, d_ref, w_ref):
+    even = place_ref[1] == 0
+    width = field_ref.shape[2]
+    for field, out_ref in enumerate((d_ref, w_ref)):
+        from_a, from_b = a_ref[field], b_ref[field]
+        both = jnp.concatenate([jnp.where(even, from_a, from_b), jnp.where(even, from_b, from_a)], axis=1)
+        out_ref[:, :width, :] = field_ref[field]
+        out_ref[:, width:, :] = both
+
+
 def mid_kernel(place_ref, f_ref, r_ref, m_ref, a_ref, b_ref):
     even = place_ref[1] == 0
     width = f_ref.shape[1] - 2 * RADIUS
@@ -86,7 +137,7 @@
 
 def apply_core(weight_ref, offset_ref, p_ref, h_ref, w_ref, t_ref, f_ref, work, chunk, enter, leave):
     prod_refs, mid_refs, roll_refs = split(work)
-    levels, block, width, depth = p_ref.shape
+    levels, block, width, _ = p_ref.shape
     taps = weight_ref.shape[0]
     halves = [slice(i * LANES, (i + 1) * LANES) for i in range(2)]
     ext = width + 2 * RADIUS
@@ -109,9 +160,9 @@
     def transposed(k, prod_ref, mid_ref):
         total = None
         for s in range(taps):
-            across = offset_ref[s, 1]
+            across = offset_ref[1, s]
             swap = (across < 0).astype(jnp.int32)
-            start = pl.ds(8 - offset_ref[s, 0], width)
+            start = pl.ds(8 - offset_ref[0, s], width)
             got = shifted(prod_ref[swap, start, :], prod_ref[1 - swap, start, :], across & (LANES - 1))
             got = [weight_ref[s] * new for new in got]
             total = got if total is None else [old + new for old, new in zip(total, got)]
@@ -121,7 +172,7 @@
 
     def rolled(mid_ref, roll_ref):
         for s in range(taps):
-            across = -offset_ref[s, 1]
+            across = -offset_ref[1, s]
             swap = (across < 0).astype(jnp.int32)
             got = shifted(mid_ref[swap], mid_ref[1 - swap], across & (LANES - 1))
             for i in range(2):
@@ -130,7 +181,7 @@
                 roll_ref[s, i, 16 + width : 24 + width, :] = new[0:8]
 
     def gather(base):
-        starts = [8 + offset_ref[s, 0] for s in range(taps)]
+        starts = [8 + offset_ref[0, s] for s in range(taps)]
         for i, half in enumerate(halves):
             for row in range(0, ext, 8):
                 moved = [
@@ -200,9 +251,13 @@
 
 
 def ordered_kernel(
-    started, weight_ref, offset_ref, place_ref, p_ref, ha_ref, hb_ref, w_ref, *rest
+    index, weight_ref, offset_ref, place_ref, p_hbm, ha_ref, hb_ref, w_ref, *rest
 ):
-    levels, block, width, depth = p_ref.shape
+    *rest, p_ref, p_sem = rest
+    started = index > 0
+    levels, block, _, _ = p_ref.shape
+    fetch = pltpu.make_async_copy(p_hbm.at[:, pl.ds(index * block, block)], p_ref, p_sem)
+    fetch.start()
     before_ref = rest[0]
     f_ref, t_ref, h_ref, *work = rest[3:] if started else rest
     f_ref[...] = before_ref[...] if started else jnp.zeros_like(f_ref)
@@ -217,6 +272,7 @@
         return carry
 
     lax.fori_loop(0, block, join, 0)
+    fetch.wait()
     nothing = lambda index: None
     apply_core(weight_ref, offset_ref, p_ref, h_ref, w_ref, t_ref, f_ref, work, block, nothing, nothing)
 
@@ -337,7 +393,7 @@
     columns = lax.axis_size("col")
     halves = lax.axis_size("mem")
     ext = width + 2 * RADIUS
-    parts = 4
+    parts = PARTS
     part = members // parts
     block = min(16, members)
     grid = members // block
@@ -345,52 +401,64 @@
     me = lax.axis_index("col")
     parity = me % 2
     place = jnp.stack([me * width, parity]).astype(jnp.int32)
-    even = parity == 0
+    taps = offsets.T
     pair_a = [(i, i ^ 1) for i in range(columns)]
     pair_b = [(i, i + 1) for i in range(1, columns - 1, 2)]
     pair_b = pair_b + [(target, source) for source, target in pair_b]
 
     def swap(a, b):
-        return lax.ppermute(b, "col", pair_b), lax.ppermute(a, "col", pair_a)
-
-    def edges(a, b, dim):
-        return jnp.where(even, jnp.concatenate([a, b], axis=dim), jnp.concatenate([b, a], axis=dim))
+        from_b = lax.ppermute(b, "col", pair_b)
+        return from_b, lax.ppermute(a, "col", pair_a)
 
     smem = pl.BlockSpec(memory_space=SMEM)
     vmem = pl.BlockSpec(memory_space=VMEM)
-    hbm = pl.BlockSpec(memory_space=pl.ANY)
+    anywhere = pl.BlockSpec(memory_space=pl.ANY)
+    hbm = pl.BlockSpec(memory_space=pltpu.HBM)
 
     def shape(*dims, dtype=jnp.float32):
         return jax.ShapeDtypeStruct(dims, dtype)
 
-    high = width - RADIUS
+    row = lambda v: v.reshape(1, -1)
+    call = pl.pallas_call(
+        obs_kernel,
+        out_shape=(shape(2, levels, width, depth), shape(2, levels, RADIUS, depth), shape(2, levels, RADIUS, depth)),
+        in_specs=[smem] + [hbm] * 5,
+        out_specs=(vmem, vmem, vmem),
+        scratch_shapes=[pltpu.VMEM((1, obs_x.shape[0]), dtype) for dtype in [jnp.int32] * 3 + [jnp.float32] * 2]
+        + [pltpu.SemaphoreType.DMA((5,))],
+        name="obs",
+        compiler_params=pltpu.CompilerParams(vmem_limit_bytes=FULL_LIMIT),
+    )
+    fields, obs_a, obs_b = call(place, row(obs_x), row(obs_y), row(obs_t), row(innovations), row(obs_rinv))
+    side_b, side_a = swap(obs_a, obs_b)
+    pack_place, _ = lax.optimization_barrier((place, obs_a))
+    call = pl.pallas_call(
+        pack_kernel,
+        out_shape=[jax.ShapeDtypeStruct((levels, part, RADIUS, depth), perturbations.dtype)] * (2 * parts),
+        in_specs=[smem, hbm],
+        out_specs=[vmem] * (2 * parts),
+        scratch_shapes=[pltpu.VMEM(perturbations.shape, perturbations.dtype), pltpu.SemaphoreType.DMA((parts,))],
+        name="pack",
+        compiler_params=pltpu.CompilerParams(vmem_limit_bytes=PACK_LIMIT),
+    )
+    packed = call(pack_place, perturbations)
 
     def send(index, after=None):
-        own = lax.slice_in_dim(perturbations, index * part, (index + 1) * part, axis=1)
-        send_a = lax.dynamic_slice_in_dim(own, jnp.where(even, high, 0), RADIUS, 2)
-        send_b = lax.dynamic_slice_in_dim(own, jnp.where(even, 0, high), RADIUS, 2)
+        sends = tuple(packed[2 * index : 2 * index + 2])
         if after is not None:
-            send_a, send_b, after = lax.optimization_barrier((send_a, send_b, after))
-        return swap(send_a, send_b), after
+            sends, after = lax.optimization_barrier((sends, after))
+        return swap(*sends), after
 
     pieces = [send(index)[0] for index in range(min(AHEAD, parts))]
 
-    row = lambda v: v.reshape(1, -1)
-    fields, obs_a, obs_b = pl.pallas_call(
-        obs_kernel,
-        out_shape=(
-            shape(2, levels, width, depth),
-            shape(2, levels, RADIUS, depth),
-            shape(2, levels, RADIUS, depth),
-        ),
-        in_specs=[smem] + [vmem] * 5,
-        out_specs=(vmem, vmem, vmem),
-        name="obs",
+    diagonal, weighted = pl.pallas_call(
+        sides_kernel,
+        out_shape=(shape(levels, ext, depth), shape(levels, ext, depth)),
+        in_specs=[smem, vmem, vmem, vmem],
+        out_specs=(vmem, vmem),
+        name="sides",
         compiler_params=pltpu.CompilerParams(vmem_limit_bytes=LIMIT),
-    )(place, row(obs_x), row(obs_y), row(obs_t), row(innovations), row(obs_rinv))
-    side_b, side_a = swap(obs_a, obs_b)
-    fields = jnp.concatenate([fields, edges(side_a, side_b, 2)], axis=2)
-    diagonal, weighted = fields[0], fields[1]
+    )(place, fields, side_a, side_b)
 
     t_spec = pl.BlockSpec((block, width, depth), lambda i: (i, 0, 0))
     t_shape = shape(members, width, depth)
@@ -433,20 +501,24 @@
 
         side = pl.BlockSpec((levels, part, RADIUS, depth), lambda i: (0, 0, 0, 0))
         from_b, from_a = pieces[index]
-        f0, t0, halo = earlier = pl.pallas_call(
-            functools.partial(ordered_kernel, index > 0),
+        call = pl.pallas_call(
+            functools.partial(ordered_kernel, index),
             out_shape=(f_shape, t_shape, h_shape),
             grid=(1,),
             in_specs=[smem] * 3
-            + [at(levels, part, width, depth, axis=1), side, side, f_spec]
-            + [f_spec, hbm, hbm][: len(earlier)],
+            + [hbm, side, side, f_spec]
+            + [f_spec, anywhere, anywhere][: len(earlier)],
             out_specs=(f_spec, at(part, width, depth, axis=0), at(levels, part, 2 * RADIUS, depth, axis=1)),
-            scratch_shapes=scratch,
+            scratch_shapes=scratch
+            + [pltpu.VMEM((levels, part, width, depth), perturbations.dtype), pltpu.SemaphoreType.DMA],
             input_output_aliases={7: 0, 8: 1, 9: 2} if earlier else {},
             cost_estimate=cost,
             name="first",
-            compiler_params=pltpu.CompilerParams(vmem_limit_bytes=LIMIT),
-        )(loc_weights, offsets, place, perturbations, from_a, from_b, weighted, *earlier)
+            compiler_params=pltpu.CompilerParams(vmem_limit_bytes=FIRST_LIMIT),
+        )
+        f0, t0, halo = earlier = call(
+            loc_weights, taps, place, perturbations, from_a, from_b, weighted, *earlier
+        )
         if index + AHEAD < parts:
             piece, f0 = send(index + AHEAD, f0)
             pieces.append(piece)
@@ -457,7 +529,7 @@
             next_kernel,
             out_shape=(t_shape, f_shape, own_shape, f_shape, m_shape),
             in_specs=[smem] * 3 + [hbm] * 2 + [vmem] * 5,
-            out_specs=(hbm, vmem, vmem, vmem, vmem),
+            out_specs=(anywhere, vmem, vmem, vmem, vmem),
             scratch_shapes=[
                 pltpu.VMEM(perturbations.shape, perturbations.dtype),
                 pltpu.VMEM(halo.shape, halo.dtype),
@@ -470,7 +542,7 @@
             cost_estimate=cost,
             name="next",
             compiler_params=pltpu.CompilerParams(vmem_limit_bytes=LIMIT),
-        )(loc_weights, offsets, place, perturbations, halo, *pieces, diagonal, old)
+        )(loc_weights, taps, place, perturbations, halo, *pieces, diagonal, old)
 
     t1, f1, e0, w1, moment0 = following(exchange(f0), weighted)
     t2, f2, e1, w2, moment1 = following(exchange(f1), w1)

time: 132 us -> 128 us (0.970)
  local copies, waits for them, and re-layouts: 9.5 us -> 3.73 us
  Pallas kernels: 47.9 us -> 52.6 us
  starting transfers between devices: 57 us -> 52.9 us
    ppermute x16, starting transfers between devices: 37.9 us -> 32.8 us  [the longest x8 27.4 us: swap(): return (from_b, lax.ppermute(a, 'col', pair_a))]
    pallas_call x5 -> x7, Pallas kernels: 16.5 us -> 21.2 us  [the longest x4 15.8 us: per_device(): call(loc_weights, taps, place, perturbations, from_a, from_b, weighted, *...]
    slice x1 -> x0, local copies, waits for them, and re-layouts: 2.55 us -> none  [send(): lax.slice_in_dim(perturbations, index * part, (index + 1) * part, axis=1)]
    unnamed x19 -> x12, local copies, waits for them, and re-layouts: 5.78 us -> 3.73 us
    ppermute x4, starting transfers between devices: 13.6 us -> 15.3 us  [per_device(): lax.ppermute(moments, 'col', [(i, i ^ step) for i in range(columns)])]
  transfers between devices with their start and end apart: 23 -> 23, of which waited for: 9 -> 10; matrix products, arithmetic and copies ran while one was open for 3% -> 0% of each run, Pallas kernels for 9% -> 10%
where the time goes in v3:
time: 128 us; the launch traced here: 127 us
  starting transfers between devices  52.9 us (41%)
  Pallas kernels  52.6 us (41%)
  waiting for transfers between devices  16.3 us (13%)
  local copies, waits for them, and re-layouts  3.73 us (3%)
    ppermute x8, starting transfers between devices, swap(): return (from_b, lax.ppermute(a, 'col', pair_a))  27.4 us
    pallas_call x2, Pallas kernels, following(): pl.pallas_call(next_kernel, out_shape=(t_shape, f_shape, own_shape, f_sha...  25.6 us
    pallas_call x4, Pallas kernels, per_device(): call(loc_weights, taps, place, perturbations, from_a, from_b, weighted, *...  15.8 us
    ppermute x4, starting transfers between devices, per_device(): lax.ppermute(moments, 'col', [(i, i ^ step) for i in range(columns)])  15.3 us
    ppermute x3, waiting for transfers between devices, exchange(): partner = lax.ppermute(field, 'mem', [(0, 1), (1, 0)])  9.29 us
    ppermute x4, waiting for transfers between devices, per_device(): lax.ppermute(moments, 'col', [(i, i ^ step) for i in range(columns)])  6.14 us
    ppermute x8, starting transfers between devices, swap(): from_b = lax.ppermute(b, 'col', pair_b)  5.46 us
    ppermute x3, starting transfers between devices, exchange(): partner = lax.ppermute(field, 'mem', [(0, 1), (1, 0)])  4.75 us
  transfers between devices with their start and end apart: 23, of which 10 were waited for; matrix products, arithmetic and copies ran while one was open for 0% of the time, Pallas kernels for 10%

profile of v3, /device:TPU:0, one launch (start us, length us, event | category | flops | bytes accessed | tf_op | source)
XLA Modules:
  0.0 127.1 jit_solution(11461207743987449913)
XLA Ops:
  0.6 0.6 pad_add_fusion.place_ref
  1.3 2.8 %obs.1 = (f32[2,4,16,256]{3,2,1,0:T(8,128)}, f32[2,4,4,256]{3,2,1,0:T(4,128)}, f32[2,4,4,256]{3,2,1,0:T(4,128)}) custom-call(s32[2]{0:T(128)} %pad_add_fusion.place_ref, s32[1,2048]{1,0:T(1,128)} %bitcast.14, s32[1,2048]{1,0:T(1,128)} %bitcast.15, s32[1,2048]{1,0:T(1,128)} %bitcast.16, f32[1,2048]{1,0:T(1,128)} %bitcast.17, f32[1,2048]{1,0:T(1,128)} %bitcast.18), custom_call_target="tpu_custom_call" | custom-call | tf_op jit(solution)/shard_map/obs/pallas_call | solution.py:432
  4.0 0.0 copy-start
  4.0 2.2 %copy-done = bf16[4,128,16,256]{3,2,1,0:T(8,128)(2,1)S(1)} copy-done((bf16[4,128,16,256]{3,2,1,0:T(8,128)(2,1)S(1)}, bf16[4,128,16,256]{3,2,1,0:T(8,128)(2,1)}, u32[]{:S(2)}) %copy-start) | copy-done | bytes 4194328
  6.2 0.6 copy-done.3
  6.9 2.1 %pack.1 = (bf16[4,32,4,256]{3,2,1,0:T(4,128)(2,1)S(1)}, bf16[4,32,4,256]{3,2,1,0:T(4,128)(2,1)S(1)}, bf16[4,32,4,256]{3,2,1,0:T(4,128)(2,1)S(1)}, bf16[4,32,4,25...) custom-call(s32[2]{0:T(128)S(1)} %copy-done.3, ...), custom_call_target="tpu_custom_call" | custom-call | tf_op jit(solution)/shard_map/pack/pallas_call | solution.py:444
  9.0 0.6 collective-permute-start
  9.5 0.7 collective-permute-start.1
  10.2 3.9 %collective-permute-start.8 = (bf16[4,32,4,256]{3,2,1,0:T(4,128)(2,1)S(1)}, bf16[4,32,4,256]{3,2,1,0:T(4,128)(2,1)S(1)}, u32[]{:S(2)}, u32[]{:S(2)}) collective-permute-start(bf16[4,32,4,256]{3,2,1,0:T(4,128)(2,1)S(1)} %get-tuple-element.66), channel_id=1, source_target_pairs={{0,1},{1,0},{2,3},{3,2},{4,5},{5,4},{6,7},{7,6},{8,9},{9,8},{10,11... | collective-permute-start | bytes 786440 | tf_op jit(solution)/shard_map/ppermute | solution.py:411
  14.1 0.7 collective-permute-start.3
  14.8 3.0 %collective-permute-start.2 = (f32[2,4,4,256]{3,2,1,0:T(4,128)}, f32[2,4,4,256]{3,2,1,0:T(4,128)S(1)}, u32[]{:S(2)}, u32[]{:S(2)}) collective-permute-start(f32[2,4,4,256]{3,2,1,0:T(4,128)} %get-tuple-element.52), channel_id=1, source_target_pairs={{0,1},{1,0},{2,3},{3,2},{4,5},{5,4},{6,7},{7,6},{8,9},{9,8},{10,11... | collective-permute-start | bytes 98312 | tf_op jit(solution)/shard_map/ppermute | solution.py:411
  17.8 0.0 collective-permute-done.3.b_ref
  17.8 0.7 collective-permute-start.9
  18.4 0.4 collective-permute-done.2.a_ref
  18.8 6.5 %collective-permute-start.6 = (bf16[4,32,4,256]{3,2,1,0:T(4,128)(2,1)S(1)}, bf16[4,32,4,256]{3,2,1,0:T(4,128)(2,1)S(1)}, u32[]{:S(2)}, u32[]{:S(2)}) collective-permute-start(bf16[4,32,4,256]{3,2,1,0:T(4,128)(2,1)S(1)} %get-tuple-element.64), channel_id=1, source_target_pairs={{0,1},{1,0},{2,3},{3,2},{4,5},{5,4},{6,7},{7,6},{8,9},{9,8},{10,11... | collective-permute-start | bytes 786440 | tf_op jit(solution)/shard_map/ppermute | solution.py:411
  25.3 0.9 copy-done.2
  26.2 0.6 sides.1
  26.8 0.0 collective-permute-done.ha_ref
  26.8 0.7 collective-permute-start.7
  27.5 0.0 collective-permute-done.1.hb_ref
  27.5 3.9 %first.4 = (f32[4,24,256]{2,1,0:T(8,128)S(1)}, f32[128,16,256]{2,1,0:T(8,128)S(1)}, bf16[4,128,8,256]{3,2,1,0:T(8,128)(2,1)S(1)}) custom-call(f32[7]{0:T(128)S(1)} %copy-done.5, s32[2,7]{1,0:T(2,128)S(1)} %bitcast.8, s32[2]{0:T(128)S(1)} %copy-done.3, bf16[4,128,16,256]{3,2,1,0:T(8,128)(2,1)S(1)} %copy-done.1, ...), custom_call_target="tpu_custom_call" | custom-call | flops 31457280 | bytes 5242880 | tf_op jit(solution)/shard_map/first/pallas_call | solution.py:519
  31.5 1.8 %collective-permute-start.4 = (bf16[4,32,4,256]{3,2,1,0:T(4,128)(2,1)S(1)}, bf16[4,32,4,256]{3,2,1,0:T(4,128)(2,1)S(1)}, u32[]{:S(2)}, u32[]{:S(2)}) collective-permute-start(bf16[4,32,4,256]{3,2,1,0:T(4,128)(2,1)S(1)} %get-tuple-element.62), channel_id=1, source_target_pairs={{0,1},{1,0},{2,3},{3,2},{4,5},{5,4},{6,7},{7,6},{8,9},{9,8},{10,11... | collective-permute-start | bytes 786440 | tf_op jit(solution)/shard_map/ppermute | solution.py:411
  33.2 0.0 collective-permute-done.8.ha_ref
  33.3 0.7 collective-permute-start.5
  33.9 0.0 collective-permute-done.9.hb_ref
  33.9 3.9 %first.5 = (f32[4,24,256]{2,1,0:T(8,128)S(1)}, f32[128,16,256]{2,1,0:T(8,128)S(1)}, bf16[4,128,8,256]{3,2,1,0:T(8,128)(2,1)S(1)}) custom-call(f32[7]{0:T(128)S(1)} %copy-done.5, s32[2,7]{1,0:T(2,128)S(1)} %bitcast.9, s32[2]{0:T(128)S(1)} %copy-done.3, ...), custom_call_target="tpu_custom_call", output_to_operand_aliasing={{0}: (7, {}), {1}: (8, {}), {2}: (9, {})} | custom-call | flops 31457280 | bytes 5242880 | tf_op jit(solution)/shard_map/first/pallas_call | solution.py:519
  37.9 0.0 collective-permute-done.6.ha_ref
  37.9 0.0 collective-permute-done.7.hb_ref
  37.9 3.9 %first.6 = (f32[4,24,256]{2,1,0:T(8,128)S(1)}, f32[128,16,256]{2,1,0:T(8,128)S(1)}, bf16[4,128,8,256]{3,2,1,0:T(8,128)(2,1)S(1)}) custom-call(f32[7]{0:T(128)S(1)} %copy-done.5, s32[2,7]{1,0:T(2,128)S(1)} %bitcast.10, s32[2]{0:T(128)S(1)} %copy-done.3, ...), custom_call_target="tpu_custom_call", output_to_operand_aliasing={{0}: (7, {}), {1}: (8, {}), {2}: (9, {})} | custom-call | flops 31457280 | bytes 5242880 | tf_op jit(solution)/shard_map/first/pallas_call | solution.py:519
  41.9 0.0 collective-permute-done.4.ha_ref
  41.9 0.0 collective-permute-done.5.hb_ref
  41.9 3.9 %first.7 = (f32[4,24,256]{2,1,0:T(8,128)S(1)}, f32[128,16,256]{2,1,0:T(8,128)S(1)}, bf16[4,128,8,256]{3,2,1,0:T(8,128)(2,1)S(1)}) custom-call(f32[7]{0:T(128)S(1)} %copy-done.5, s32[2,7]{1,0:T(2,128)S(1)} %bitcast.11, s32[2]{0:T(128)S(1)} %copy-done.3, ...), custom_call_target="tpu_custom_call", output_to_operand_aliasing={{0}: (7, {}), {1}: (8, {}), {2}: (9, {})} | custom-call | flops 31457280 | bytes 5242880 | tf_op jit(solution)/shard_map/first/pallas_call | solution.py:519
  45.8 1.6 %collective-permute-start.10 = (f32[4,24,256]{2,1,0:T(8,128)S(1)}, f32[4,24,256]{2,1,0:T(8,128)S(1)}, u32[]{:S(2)}, u32[]{:S(2)}) collective-permute-start(f32[4,24,256]{2,1,0:T(8,128)S(1)} %get-tuple-element.78.f_ref), channel_id=1, source_target_pairs={{0,16},{16,0},{1,17},{17,1},{2,18},{18,2},{3,19},{19,3},{4,20},{20... | collective-permute-start | bytes 294920 | tf_op jit(solution)/shard_map/ppermute | solution.py:481
  47.4 3.1 %collective-permute-done.10.r_ref = f32[4,24,256]{2,1,0:T(8,128)S(1)} collective-permute-done((f32[4,24,256]{2,1,0:T(8,128)S(1)}, f32[4,24,256]{2,1,0:T(8,128)S(1)}, u32[]{:S(2)}, u32[]{:S(2)}) %collective-permute-start.10) | collective-permute-done | bytes 98336 | tf_op jit(solution)/shard_map/ppermute | solution.py:481
  50.5 0.6 mid.3
  51.1 2.9 %collective-permute-start.11 = (f32[4,8,256]{2,1,0:T(8,128)S(1)}, f32[4,8,256]{2,1,0:T(8,128)S(1)}, u32[]{:S(2)}, u32[]{:S(2)}) collective-permute-start(f32[4,8,256]{2,1,0:T(8,128)S(1)} %get-tuple-element.80), channel_id=1, source_target_pairs={{0,1},{1,0},{2,3},{3,2},{4,5},{5,4},{6,7},{7,6},{8,9},{9,8},{10,11... | collective-permute-start | bytes 98312 | tf_op jit(solution)/shard_map/ppermute | solution.py:411
  54.0 0.7 collective-permute-start.12
  54.7 0.2 collective-permute-done.11.a_ref
  54.9 12.8 %next.2 = (f32[128,16,256]{2,1,0:T(8,128)S(1)}, f32[4,24,256]{2,1,0:T(8,128)S(1)}, f32[4,16,256]{2,1,0:T(8,128)S(1)}, f32[4,24,256]{2,1,0:T(8,128)S(1)}, f32[2,8,128]{2,1,0:T(8,128)S(1)}) custom-call(f32[7]{0:T(128)S(1)} %copy-done.5, s32[2,7]{1,0:T(2,128)S(1)} %bitcast.12, s32[2]{0:T(128)S(1)} %copy-done.3, bf16[4,128,16,256]{3,2,1,0:T(8,128)(2,1)S(1)} %copy-done.1, ...), custom_call_target="tpu_custom_call" | custom-call | flops 31457280 | bytes 5242880 | tf_op jit(solution)/shard_map/next/pallas_call | solution.py:528
  67.6 1.6 %collective-permute-start.13 = (f32[4,24,256]{2,1,0:T(8,128)S(1)}, f32[4,24,256]{2,1,0:T(8,128)S(1)}, u32[]{:S(2)}, u32[]{:S(2)}) collective-permute-start(f32[4,24,256]{2,1,0:T(8,128)S(1)} %get-tuple-element.83.f_ref), channel_id=1, source_target_pairs={{0,16},{16,0},{1,17},{17,1},{2,18},{18,2},{3,19},{19,3},{4,20},{20... | collective-permute-start | bytes 294920 | tf_op jit(solution)/shard_map/ppermute | solution.py:481
  69.2 3.1 %collective-permute-done.13.r_ref = f32[4,24,256]{2,1,0:T(8,128)S(1)} collective-permute-done((f32[4,24,256]{2,1,0:T(8,128)S(1)}, f32[4,24,256]{2,1,0:T(8,128)S(1)}, u32[]{:S(2)}, u32[]{:S(2)}) %collective-permute-start.13) | collective-permute-done | bytes 98336 | tf_op jit(solution)/shard_map/ppermute | solution.py:481
  72.3 0.6 mid.4
  72.9 3.4 %collective-permute-start.14 = (f32[4,8,256]{2,1,0:T(8,128)S(1)}, f32[4,8,256]{2,1,0:T(8,128)S(1)}, u32[]{:S(2)}, u32[]{:S(2)}) collective-permute-start(f32[4,8,256]{2,1,0:T(8,128)S(1)} %get-tuple-element.85), channel_id=1, source_target_pairs={{0,1},{1,0},{2,3},{3,2},{4,5},{5,4},{6,7},{7,6},{8,9},{9,8},{10,11... | collective-permute-start | bytes 98312 | tf_op jit(solution)/shard_map/ppermute | solution.py:411
  76.3 0.8 collective-permute-start.15
  77.2 0.0 collective-permute-done.14.a_ref
  77.2 0.0 collective-permute-done.15.b_ref
  77.2 12.8 %next.3 = (f32[128,16,256]{2,1,0:T(8,128)S(1)}, f32[4,24,256]{2,1,0:T(8,128)S(1)}, f32[4,16,256]{2,1,0:T(8,128)S(1)}, f32[4,24,256]{2,1,0:T(8,128)S(1)}, f32[2,8,128]{2,1,0:T(8,128)S(1)}) custom-call(f32[7]{0:T(128)S(1)} %copy-done.5, s32[2,7]{1,0:T(2,128)S(1)} %bitcast.13, s32[2]{0:T(128)S(1)} %copy-done.3, bf16[4,128,16,256]{3,2,1,0:T(8,128)(2,1)S(1)} %copy-done.1, ...), custom_call_target="tpu_custom_call" | custom-call | flops 31457280 | bytes 5242880 | tf_op jit(solution)/shard_map/next/pallas_call | solution.py:528
  90.0 1.6 %collective-permute-start.16 = (f32[4,24,256]{2,1,0:T(8,128)S(1)}, f32[4,24,256]{2,1,0:T(8,128)S(1)}, u32[]{:S(2)}, u32[]{:S(2)}) collective-permute-start(f32[4,24,256]{2,1,0:T(8,128)S(1)} %get-tuple-element.88.f_ref), channel_id=1, source_target_pairs={{0,16},{16,0},{1,17},{17,1},{2,18},{18,2},{3,19},{19,3},{4,20},{20... | collective-permute-start | bytes 294920 | tf_op jit(solution)/shard_map/ppermute | solution.py:481
  91.6 3.1 %collective-permute-done.16.r_ref = f32[4,24,256]{2,1,0:T(8,128)S(1)} collective-permute-done((f32[4,24,256]{2,1,0:T(8,128)S(1)}, f32[4,24,256]{2,1,0:T(8,128)S(1)}, u32[]{:S(2)}, u32[]{:S(2)}) %collective-permute-start.16) | collective-permute-done | bytes 98336 | tf_op jit(solution)/shard_map/ppermute | solution.py:481
  94.7 0.6 mid.5
  95.3 5.3 %collective-permute-start.17 = (f32[4,8,256]{2,1,0:T(8,128)S(1)}, f32[4,8,256]{2,1,0:T(8,128)S(1)}, u32[]{:S(2)}, u32[]{:S(2)}) collective-permute-start(f32[4,8,256]{2,1,0:T(8,128)S(1)} %get-tuple-element.90), channel_id=1, source_target_pairs={{0,1},{1,0},{2,3},{3,2},{4,5},{5,4},{6,7},{7,6},{8,9},{9,8},{10,11... | collective-permute-start | bytes 98312 | tf_op jit(solution)/shard_map/ppermute | solution.py:411
  100.6 0.7 collective-permute-start.18
  101.3 0.2 collective-permute-done.17.a_ref
  101.5 0.0 collective-permute-done.18.b_ref
  101.5 0.6 last.1
  102.0 6.5 %collective-permute-start.19 = (f32[8,128]{1,0:T(8,128)S(1)}, f32[8,128]{1,0:T(8,128)S(1)}, u32[]{:S(2)}, u32[]{:S(2)}) collective-permute-start(f32[8,128]{1,0:T(8,128)S(1)} %get-tuple-element.95), channel_id=1, source_target_pairs={{0,1},{1,0},{2,3},{3,2},{4,5},{5,4},{6,7},{7,6},{8,9},{9,8},{10,11... | collective-permute-start | bytes 12296 | tf_op jit(solution)/shard_map/ppermute | solution.py:559
  108.6 0.8 collective-permute-done.19
  109.4 2.9 %collective-permute-start.20 = (f32[8,128]{1,0:T(8,128)S(1)}, f32[8,128]{1,0:T(8,128)S(1)}, u32[]{:S(2)}, u32[]{:S(2)}) collective-permute-start(f32[8,128]{1,0:T(8,128)S(1)} %add.17), channel_id=1, source_target_pairs={{0,2},{1,3},{2,0},{3,1},{4,6},{5,7},{6,4},{7,5},{8,10},{9,11},{10,... | collective-permute-start | bytes 12296 | tf_op jit(solution)/shard_map/ppermute | solution.py:559
  112.3 1.6 %collective-permute-done.20 = f32[8,128]{1,0:T(8,128)S(1)} collective-permute-done((f32[8,128]{1,0:T(8,128)S(1)}, f32[8,128]{1,0:T(8,128)S(1)}, u32[]{:S(2)}, u32[]{:S(2)}) %collective-permute-start.20) | collective-permute-done | bytes 4128 | tf_op jit(solution)/shard_map/ppermute | solution.py:559
  113.9 3.5 %collective-permute-start.21 = (f32[8,128]{1,0:T(8,128)S(1)}, f32[8,128]{1,0:T(8,128)S(1)}, u32[]{:S(2)}, u32[]{:S(2)}) collective-permute-start(f32[8,128]{1,0:T(8,128)S(1)} %add.18), channel_id=1, source_target_pairs={{0,4},{1,5},{2,6},{3,7},{4,0},{5,1},{6,2},{7,3},{8,12},{9,13},{10,... | collective-permute-start | bytes 12296 | tf_op jit(solution)/shard_map/ppermute | solution.py:559
  117.4 1.6 %collective-permute-done.21 = f32[8,128]{1,0:T(8,128)S(1)} collective-permute-done((f32[8,128]{1,0:T(8,128)S(1)}, f32[8,128]{1,0:T(8,128)S(1)}, u32[]{:S(2)}, u32[]{:S(2)}) %collective-permute-start.21) | collective-permute-done | bytes 4128 | tf_op jit(solution)/shard_map/ppermute | solution.py:559
  119.0 2.4 %collective-permute-start.22 = (f32[8,128]{1,0:T(8,128)S(1)}, f32[8,128]{1,0:T(8,128)S(1)}, u32[]{:S(2)}, u32[]{:S(2)}) collective-permute-start(f32[8,128]{1,0:T(8,128)S(1)} %add.19), channel_id=1, source_target_pairs={{0,8},{1,9},{2,10},{3,11},{4,12},{5,13},{6,14},{7,15},{8,0},{9,1},... | collective-permute-start | bytes 12296 | tf_op jit(solution)/shard_map/ppermute | solution.py:559
  121.4 2.1 %collective-permute-done.22 = f32[8,128]{1,0:T(8,128)S(1)} collective-permute-done((f32[8,128]{1,0:T(8,128)S(1)}, f32[8,128]{1,0:T(8,128)S(1)}, u32[]{:S(2)}, u32[]{:S(2)}) %collective-permute-start.22) | collective-permute-done | bytes 4128 | tf_op jit(solution)/shard_map/ppermute | solution.py:559
  123.5 3.6 %final.1 = (f32[128,16,256]{2,1,0:T(8,128)}, f32[4,16,256]{2,1,0:T(8,128)}) custom-call(f32[8,128]{1,0:T(8,128)S(1)} %add.20.moment_ref, f32[128,16,256]{2,1,0:T(8,128)S(1)} %get-tuple-element.96.t0_ref, f32[128,16,256]{2,1,0:T(8,128)S(1)} %get-tuple-element.97.t1_ref, f32[128,16,256]{2,1,0:T(8,128)S(1)} %get-tuple-element.98.t2_ref, ...), custom_call_target="tpu_custom_call" | custom-call | tf_op jit(solution)/shard_map/final/pallas_call | solution.py:561
  (13 shorter events, 0.0 us)
Async XLA Ops:
  4.0 2.2 %copy-start = (bf16[4,128,16,256]{3,2,1,0:T(8,128)(2,1)S(1)}, bf16[4,128,16,256]{3,2,1,0:T(8,128)(2,1)}, u32[]{:S(2)}) copy-start(bf16[4,128,16,256]{3,2,1,0:T(8,128)(2,1)} %p_hbm.13) | copy-start | bytes 12582916
  6.2 0.6 copy-start.3
  6.9 20.6 %copy-start.1 = (bf16[4,128,16,256]{3,2,1,0:T(8,128)(2,1)S(1)}, bf16[4,128,16,256]{3,2,1,0:T(8,128)(2,1)}, u32[]{:S(2)}) copy-start(bf16[4,128,16,256]{3,2,1,0:T(8,128)(2,1)} %p_hbm.13) | copy-start | bytes 12582916
  6.9 20.6 %copy-start.4 = (s32[7,2]{0,1:T(2,128)S(1)}, s32[7,2]{0,1:T(2,128)}, u32[]{:S(2)}) copy-start(s32[7,2]{0,1:T(2,128)} %param.10) | copy-start | bytes 172
  6.9 20.7 %copy-start.5 = (f32[7]{0:T(128)S(1)}, f32[7]{0:T(128)}, u32[]{:S(2)}) copy-start(f32[7]{0:T(128)} %weight_ref.11) | copy-start | bytes 88
  9.0 17.8 %collective-permute-start = (bf16[4,32,4,256]{3,2,1,0:T(4,128)(2,1)S(1)}, bf16[4,32,4,256]{3,2,1,0:T(4,128)(2,1)S(1)}, u32[]{:S(2)}, u32[]{:S(2)}) collective-permute-start(bf16[4,32,4,256]{3,2,1,0:T(4,128)(2,1)S(1)} %get-tuple-element.56), channel_id=1, source_target_pairs={{0,1},{1,0},{2,3},{3,2},{4,5},{5,4},{6,7},{7,6},{8,9},{9,8},{10,11... | collective-permute-start | bytes 786440 | tf_op jit(solution)/shard_map/ppermute | solution.py:411
  9.5 18.0 %collective-permute-start.1 = (bf16[4,32,4,256]{3,2,1,0:T(4,128)(2,1)S(1)}, bf16[4,32,4,256]{3,2,1,0:T(4,128)(2,1)S(1)}, u32[]{:S(2)}, u32[]{:S(2)}) collective-permute-start(bf16[4,32,4,256]{3,2,1,0:T(4,128)(2,1)S(1)} %get-tuple-element.57), channel_id=1, source_target_pairs={{1,2},{3,4},{5,6},{7,8},{9,10},{11,12},{13,14},{2,1},{4,3},{6,5},{... | collective-permute-start | bytes 786440 | tf_op jit(solution)/shard_map/ppermute | solution.py:410
  10.2 23.0 %collective-permute-start.8 = (bf16[4,32,4,256]{3,2,1,0:T(4,128)(2,1)S(1)}, bf16[4,32,4,256]{3,2,1,0:T(4,128)(2,1)S(1)}, u32[]{:S(2)}, u32[]{:S(2)}) collective-permute-start(bf16[4,32,4,256]{3,2,1,0:T(4,128)(2,1)S(1)} %get-tuple-element.66), channel_id=1, source_target_pairs={{0,1},{1,0},{2,3},{3,2},{4,5},{5,4},{6,7},{7,6},{8,9},{9,8},{10,11... | collective-permute-start | bytes 786440 | tf_op jit(solution)/shard_map/ppermute | solution.py:411
  14.1 3.6 %collective-permute-start.3 = (f32[2,4,4,256]{3,2,1,0:T(4,128)}, f32[2,4,4,256]{3,2,1,0:T(4,128)S(1)}, u32[]{:S(2)}, u32[]{:S(2)}) collective-permute-start(f32[2,4,4,256]{3,2,1,0:T(4,128)} %get-tuple-element.59), channel_id=1, source_target_pairs={{1,2},{3,4},{5,6},{7,8},{9,10},{11,12},{13,14},{2,1},{4,3},{6,5},{... | collective-permute-start | bytes 98312 | tf_op jit(solution)/shard_map/ppermute | solution.py:410
  14.8 4.0 %collective-permute-start.2 = (f32[2,4,4,256]{3,2,1,0:T(4,128)}, f32[2,4,4,256]{3,2,1,0:T(4,128)S(1)}, u32[]{:S(2)}, u32[]{:S(2)}) collective-permute-start(f32[2,4,4,256]{3,2,1,0:T(4,128)} %get-tuple-element.52), channel_id=1, source_target_pairs={{0,1},{1,0},{2,3},{3,2},{4,5},{5,4},{6,7},{7,6},{8,9},{9,8},{10,11... | collective-permute-start | bytes 98312 | tf_op jit(solution)/shard_map/ppermute | solution.py:411
  17.8 16.2 %collective-permute-start.9 = (bf16[4,32,4,256]{3,2,1,0:T(4,128)(2,1)S(1)}, bf16[4,32,4,256]{3,2,1,0:T(4,128)(2,1)S(1)}, u32[]{:S(2)}, u32[]{:S(2)}) collective-permute-start(bf16[4,32,4,256]{3,2,1,0:T(4,128)(2,1)S(1)} %get-tuple-element.67), channel_id=1, source_target_pairs={{1,2},{3,4},{5,6},{7,8},{9,10},{11,12},{13,14},{2,1},{4,3},{6,5},{... | collective-permute-start | bytes 786440 | tf_op jit(solution)/shard_map/ppermute | solution.py:410
  18.8 19.1 %collective-permute-start.6 = (bf16[4,32,4,256]{3,2,1,0:T(4,128)(2,1)S(1)}, bf16[4,32,4,256]{3,2,1,0:T(4,128)(2,1)S(1)}, u32[]{:S(2)}, u32[]{:S(2)}) collective-permute-start(bf16[4,32,4,256]{3,2,1,0:T(4,128)(2,1)S(1)} %get-tuple-element.64), channel_id=1, source_target_pairs={{0,1},{1,0},{2,3},{3,2},{4,5},{5,4},{6,7},{7,6},{8,9},{9,8},{10,11... | collective-permute-start | bytes 786440 | tf_op jit(solution)/shard_map/ppermute | solution.py:411
  25.3 0.9 copy-start.2
  26.8 11.1 %collective-permute-start.7 = (bf16[4,32,4,256]{3,2,1,0:T(4,128)(2,1)S(1)}, bf16[4,32,4,256]{3,2,1,0:T(4,128)(2,1)S(1)}, u32[]{:S(2)}, u32[]{:S(2)}) collective-permute-start(bf16[4,32,4,256]{3,2,1,0:T(4,128)(2,1)S(1)} %get-tuple-element.65), channel_id=1, source_target_pairs={{1,2},{3,4},{5,6},{7,8},{9,10},{11,12},{13,14},{2,1},{4,3},{6,5},{... | collective-permute-start | bytes 786440 | tf_op jit(solution)/shard_map/ppermute | solution.py:410
  31.5 10.4 %collective-permute-start.4 = (bf16[4,32,4,256]{3,2,1,0:T(4,128)(2,1)S(1)}, bf16[4,32,4,256]{3,2,1,0:T(4,128)(2,1)S(1)}, u32[]{:S(2)}, u32[]{:S(2)}) collective-permute-start(bf16[4,32,4,256]{3,2,1,0:T(4,128)(2,1)S(1)} %get-tuple-element.62), channel_id=1, source_target_pairs={{0,1},{1,0},{2,3},{3,2},{4,5},{5,4},{6,7},{7,6},{8,9},{9,8},{10,11... | collective-permute-start | bytes 786440 | tf_op jit(solution)/shard_map/ppermute | solution.py:411
  33.3 8.6 %collective-permute-start.5 = (bf16[4,32,4,256]{3,2,1,0:T(4,128)(2,1)S(1)}, bf16[4,32,4,256]{3,2,1,0:T(4,128)(2,1)S(1)}, u32[]{:S(2)}, u32[]{:S(2)}) collective-permute-start(bf16[4,32,4,256]{3,2,1,0:T(4,128)(2,1)S(1)} %get-tuple-element.63), channel_id=1, source_target_pairs={{1,2},{3,4},{5,6},{7,8},{9,10},{11,12},{13,14},{2,1},{4,3},{6,5},{... | collective-permute-start | bytes 786440 | tf_op jit(solution)/shard_map/ppermute | solution.py:410
  45.8 4.7 %collective-permute-start.10 = (f32[4,24,256]{2,1,0:T(8,128)S(1)}, f32[4,24,256]{2,1,0:T(8,128)S(1)}, u32[]{:S(2)}, u32[]{:S(2)}) collective-permute-start(f32[4,24,256]{2,1,0:T(8,128)S(1)} %get-tuple-element.78.f_ref), channel_id=1, source_target_pairs={{0,16},{16,0},{1,17},{17,1},{2,18},{18,2},{3,19},{19,3},{4,20},{20... | collective-permute-start | bytes 294920 | tf_op jit(solution)/shard_map/ppermute | solution.py:481
  51.1 3.8 %collective-permute-start.11 = (f32[4,8,256]{2,1,0:T(8,128)S(1)}, f32[4,8,256]{2,1,0:T(8,128)S(1)}, u32[]{:S(2)}, u32[]{:S(2)}) collective-permute-start(f32[4,8,256]{2,1,0:T(8,128)S(1)} %get-tuple-element.80), channel_id=1, source_target_pairs={{0,1},{1,0},{2,3},{3,2},{4,5},{5,4},{6,7},{7,6},{8,9},{9,8},{10,11... | collective-permute-start | bytes 98312 | tf_op jit(solution)/shard_map/ppermute | solution.py:411
  54.0 0.9 collective-permute-start.12
  67.6 4.7 %collective-permute-start.13 = (f32[4,24,256]{2,1,0:T(8,128)S(1)}, f32[4,24,256]{2,1,0:T(8,128)S(1)}, u32[]{:S(2)}, u32[]{:S(2)}) collective-permute-start(f32[4,24,256]{2,1,0:T(8,128)S(1)} %get-tuple-element.83.f_ref), channel_id=1, source_target_pairs={{0,16},{16,0},{1,17},{17,1},{2,18},{18,2},{3,19},{19,3},{4,20},{20... | collective-permute-start | bytes 294920 | tf_op jit(solution)/shard_map/ppermute | solution.py:481
  72.9 4.3 %collective-permute-start.14 = (f32[4,8,256]{2,1,0:T(8,128)S(1)}, f32[4,8,256]{2,1,0:T(8,128)S(1)}, u32[]{:S(2)}, u32[]{:S(2)}) collective-permute-start(f32[4,8,256]{2,1,0:T(8,128)S(1)} %get-tuple-element.85), channel_id=1, source_target_pairs={{0,1},{1,0},{2,3},{3,2},{4,5},{5,4},{6,7},{7,6},{8,9},{9,8},{10,11... | collective-permute-start | bytes 98312 | tf_op jit(solution)/shard_map/ppermute | solution.py:411
  76.3 0.9 collective-permute-start.15
  90.0 4.7 %collective-permute-start.16 = (f32[4,24,256]{2,1,0:T(8,128)S(1)}, f32[4,24,256]{2,1,0:T(8,128)S(1)}, u32[]{:S(2)}, u32[]{:S(2)}) collective-permute-start(f32[4,24,256]{2,1,0:T(8,128)S(1)} %get-tuple-element.88.f_ref), channel_id=1, source_target_pairs={{0,16},{16,0},{1,17},{17,1},{2,18},{18,2},{3,19},{19,3},{4,20},{20... | collective-permute-start | bytes 294920 | tf_op jit(solution)/shard_map/ppermute | solution.py:481
  95.3 6.2 %collective-permute-start.17 = (f32[4,8,256]{2,1,0:T(8,128)S(1)}, f32[4,8,256]{2,1,0:T(8,128)S(1)}, u32[]{:S(2)}, u32[]{:S(2)}) collective-permute-start(f32[4,8,256]{2,1,0:T(8,128)S(1)} %get-tuple-element.90), channel_id=1, source_target_pairs={{0,1},{1,0},{2,3},{3,2},{4,5},{5,4},{6,7},{7,6},{8,9},{9,8},{10,11... | collective-permute-start | bytes 98312 | tf_op jit(solution)/shard_map/ppermute | solution.py:411
  100.6 0.9 collective-permute-start.18
  102.0 7.4 %collective-permute-start.19 = (f32[8,128]{1,0:T(8,128)S(1)}, f32[8,128]{1,0:T(8,128)S(1)}, u32[]{:S(2)}, u32[]{:S(2)}) collective-permute-start(f32[8,128]{1,0:T(8,128)S(1)} %get-tuple-element.95), channel_id=1, source_target_pairs={{0,1},{1,0},{2,3},{3,2},{4,5},{5,4},{6,7},{7,6},{8,9},{9,8},{10,11... | collective-permute-start | bytes 12296 | tf_op jit(solution)/shard_map/ppermute | solution.py:559
  109.4 4.5 %collective-permute-start.20 = (f32[8,128]{1,0:T(8,128)S(1)}, f32[8,128]{1,0:T(8,128)S(1)}, u32[]{:S(2)}, u32[]{:S(2)}) collective-permute-start(f32[8,128]{1,0:T(8,128)S(1)} %add.17), channel_id=1, source_target_pairs={{0,2},{1,3},{2,0},{3,1},{4,6},{5,7},{6,4},{7,5},{8,10},{9,11},{10,... | collective-permute-start | bytes 12296 | tf_op jit(solution)/shard_map/ppermute | solution.py:559
  113.9 5.1 %collective-permute-start.21 = (f32[8,128]{1,0:T(8,128)S(1)}, f32[8,128]{1,0:T(8,128)S(1)}, u32[]{:S(2)}, u32[]{:S(2)}) collective-permute-start(f32[8,128]{1,0:T(8,128)S(1)} %add.18), channel_id=1, source_target_pairs={{0,4},{1,5},{2,6},{3,7},{4,0},{5,1},{6,2},{7,3},{8,12},{9,13},{10,... | collective-permute-start | bytes 12296 | tf_op jit(solution)/shard_map/ppermute | solution.py:559
  119.0 4.5 %collective-permute-start.22 = (f32[8,128]{1,0:T(8,128)S(1)}, f32[8,128]{1,0:T(8,128)S(1)}, u32[]{:S(2)}, u32[]{:S(2)}) collective-permute-start(f32[8,128]{1,0:T(8,128)S(1)} %add.19), channel_id=1, source_target_pairs={{0,8},{1,9},{2,10},{3,11},{4,12},{5,13},{6,14},{7,15},{8,0},{9,1},... | collective-permute-start | bytes 12296 | tf_op jit(solution)/shard_map/ppermute | solution.py:559

commit v4 on v3

--- a/solution.py
+++ b/solution.py
@@ -396,7 +396,6 @@
     parts = PARTS
     part = members // parts
     block = min(16, members)
-    grid = members // block
     chunks = members // block
     me = lax.axis_index("col")
     parity = me % 2
@@ -558,12 +557,14 @@
     while step < columns:
         moments = moments + lax.ppermute(moments, "col", [(i, i ^ step) for i in range(columns)])
         step *= 2
+    wide = min(32, members)
+    wide_spec = pl.BlockSpec((wide, width, depth), lambda i: (i, 0, 0))
     control, increment = pl.pallas_call(
         final_kernel,
         out_shape=(t_shape, own_shape),
-        grid=(grid,),
-        in_specs=[whole(8, LANES)] + [t_spec] * 3 + [own_spec] * 3,
-        out_specs=(t_spec, own_spec),
+        grid=(members // wide,),
+        in_specs=[whole(8, LANES)] + [wide_spec] * 3 + [own_spec] * 3,
+        out_specs=(wide_spec, own_spec),
         scratch_shapes=[pltpu.VMEM((3, 8, LANES), jnp.float32)],
         name="final",
         compiler_params=pltpu.CompilerParams(vmem_limit_bytes=LIMIT),

time: 128 us -> 126 us (0.984)
  no operation moved by 1% of the time
where the time goes in v4:
time: 126 us
  starting transfers between devices  52.9 us (42%)
  Pallas kernels  51.5 us (41%)
  waiting for transfers between devices  16.3 us (13%)
  local copies, waits for them, and re-layouts  3.73 us (3%)
    ppermute x8, starting transfers between devices, swap(): return (from_b, lax.ppermute(a, 'col', pair_a))  27.4 us
    pallas_call x2, Pallas kernels, following(): pl.pallas_call(next_kernel, out_shape=(t_shape, f_shape, own_shape, f_sha...  25.6 us
    pallas_call x4, Pallas kernels, per_device(): call(loc_weights, taps, place, perturbations, from_a, from_b, weighted, *...  15.8 us
    ppermute x4, starting transfers between devices, per_device(): lax.ppermute(moments, 'col', [(i, i ^ step) for i in range(columns)])  15.3 us
    ppermute x3, waiting for transfers between devices, exchange(): partner = lax.ppermute(field, 'mem', [(0, 1), (1, 0)])  9.29 us
    ppermute x4, waiting for transfers between devices, per_device(): lax.ppermute(moments, 'col', [(i, i ^ step) for i in range(columns)])  6.14 us
    ppermute x8, starting transfers between devices, swap(): from_b = lax.ppermute(b, 'col', pair_b)  5.46 us
    ppermute x3, starting transfers between devices, exchange(): partner = lax.ppermute(field, 'mem', [(0, 1), (1, 0)])  4.75 us
  transfers between devices with their start and end apart: 23, of which 10 were waited for; matrix products, arithmetic and copies ran while one was open for 0% of the time, Pallas kernels for 10%

profile of v4, /device:TPU:0, one launch (start us, length us, event | category | flops | bytes accessed | tf_op | source)
XLA Modules:
  0.0 126.0 jit_solution(11519975467507142643)
XLA Ops:
  0.6 0.6 pad_add_fusion.place_ref
  1.3 2.8 %obs.1 = (f32[2,4,16,256]{3,2,1,0:T(8,128)}, f32[2,4,4,256]{3,2,1,0:T(4,128)}, f32[2,4,4,256]{3,2,1,0:T(4,128)}) custom-call(s32[2]{0:T(128)} %pad_add_fusion.place_ref, s32[1,2048]{1,0:T(1,128)} %bitcast.14, s32[1,2048]{1,0:T(1,128)} %bitcast.15, s32[1,2048]{1,0:T(1,128)} %bitcast.16, f32[1,2048]{1,0:T(1,128)} %bitcast.17, f32[1,2048]{1,0:T(1,128)} %bitcast.18), custom_call_target="tpu_custom_call" | custom-call | tf_op jit(solution)/shard_map/obs/pallas_call | solution.py:431
  4.0 0.0 copy-start
  4.0 2.2 %copy-done = bf16[4,128,16,256]{3,2,1,0:T(8,128)(2,1)S(1)} copy-done((bf16[4,128,16,256]{3,2,1,0:T(8,128)(2,1)S(1)}, bf16[4,128,16,256]{3,2,1,0:T(8,128)(2,1)}, u32[]{:S(2)}) %copy-start) | copy-done | bytes 4194328
  6.2 0.6 copy-done.3
  6.9 2.1 %pack.1 = (bf16[4,32,4,256]{3,2,1,0:T(4,128)(2,1)S(1)}, bf16[4,32,4,256]{3,2,1,0:T(4,128)(2,1)S(1)}, bf16[4,32,4,256]{3,2,1,0:T(4,128)(2,1)S(1)}, bf16[4,32,4,25...) custom-call(s32[2]{0:T(128)S(1)} %copy-done.3, ...), custom_call_target="tpu_custom_call" | custom-call | tf_op jit(solution)/shard_map/pack/pallas_call | solution.py:443
  9.0 0.6 collective-permute-start
  9.5 0.7 collective-permute-start.1
  10.2 3.9 %collective-permute-start.8 = (bf16[4,32,4,256]{3,2,1,0:T(4,128)(2,1)S(1)}, bf16[4,32,4,256]{3,2,1,0:T(4,128)(2,1)S(1)}, u32[]{:S(2)}, u32[]{:S(2)}) collective-permute-start(bf16[4,32,4,256]{3,2,1,0:T(4,128)(2,1)S(1)} %get-tuple-element.66), channel_id=1, source_target_pairs={{0,1},{1,0},{2,3},{3,2},{4,5},{5,4},{6,7},{7,6},{8,9},{9,8},{10,11... | collective-permute-start | bytes 786440 | tf_op jit(solution)/shard_map/ppermute | solution.py:410
  14.1 0.7 collective-permute-start.3
  14.8 3.0 %collective-permute-start.2 = (f32[2,4,4,256]{3,2,1,0:T(4,128)}, f32[2,4,4,256]{3,2,1,0:T(4,128)S(1)}, u32[]{:S(2)}, u32[]{:S(2)}) collective-permute-start(f32[2,4,4,256]{3,2,1,0:T(4,128)} %get-tuple-element.52), channel_id=1, source_target_pairs={{0,1},{1,0},{2,3},{3,2},{4,5},{5,4},{6,7},{7,6},{8,9},{9,8},{10,11... | collective-permute-start | bytes 98312 | tf_op jit(solution)/shard_map/ppermute | solution.py:410
  17.8 0.0 collective-permute-done.3.b_ref
  17.8 0.7 collective-permute-start.9
  18.4 0.4 collective-permute-done.2.a_ref
  18.8 6.5 %collective-permute-start.6 = (bf16[4,32,4,256]{3,2,1,0:T(4,128)(2,1)S(1)}, bf16[4,32,4,256]{3,2,1,0:T(4,128)(2,1)S(1)}, u32[]{:S(2)}, u32[]{:S(2)}) collective-permute-start(bf16[4,32,4,256]{3,2,1,0:T(4,128)(2,1)S(1)} %get-tuple-element.64), channel_id=1, source_target_pairs={{0,1},{1,0},{2,3},{3,2},{4,5},{5,4},{6,7},{7,6},{8,9},{9,8},{10,11... | collective-permute-start | bytes 786440 | tf_op jit(solution)/shard_map/ppermute | solution.py:410
  25.3 0.9 copy-done.2
  26.2 0.6 sides.1
  26.8 0.0 collective-permute-done.ha_ref
  26.8 0.7 collective-permute-start.7
  27.5 0.0 collective-permute-done.1.hb_ref
  27.5 3.9 %first.4 = (f32[4,24,256]{2,1,0:T(8,128)S(1)}, f32[128,16,256]{2,1,0:T(8,128)S(1)}, bf16[4,128,8,256]{3,2,1,0:T(8,128)(2,1)S(1)}) custom-call(f32[7]{0:T(128)S(1)} %copy-done.5, s32[2,7]{1,0:T(2,128)S(1)} %bitcast.8, s32[2]{0:T(128)S(1)} %copy-done.3, bf16[4,128,16,256]{3,2,1,0:T(8,128)(2,1)S(1)} %copy-done.1, ...), custom_call_target="tpu_custom_call" | custom-call | flops 31457280 | bytes 5242880 | tf_op jit(solution)/shard_map/first/pallas_call | solution.py:518
  31.5 1.8 %collective-permute-start.4 = (bf16[4,32,4,256]{3,2,1,0:T(4,128)(2,1)S(1)}, bf16[4,32,4,256]{3,2,1,0:T(4,128)(2,1)S(1)}, u32[]{:S(2)}, u32[]{:S(2)}) collective-permute-start(bf16[4,32,4,256]{3,2,1,0:T(4,128)(2,1)S(1)} %get-tuple-element.62), channel_id=1, source_target_pairs={{0,1},{1,0},{2,3},{3,2},{4,5},{5,4},{6,7},{7,6},{8,9},{9,8},{10,11... | collective-permute-start | bytes 786440 | tf_op jit(solution)/shard_map/ppermute | solution.py:410
  33.2 0.0 collective-permute-done.8.ha_ref
  33.3 0.7 collective-permute-start.5
  33.9 0.0 collective-permute-done.9.hb_ref
  33.9 3.9 %first.5 = (f32[4,24,256]{2,1,0:T(8,128)S(1)}, f32[128,16,256]{2,1,0:T(8,128)S(1)}, bf16[4,128,8,256]{3,2,1,0:T(8,128)(2,1)S(1)}) custom-call(f32[7]{0:T(128)S(1)} %copy-done.5, s32[2,7]{1,0:T(2,128)S(1)} %bitcast.9, s32[2]{0:T(128)S(1)} %copy-done.3, ...), custom_call_target="tpu_custom_call", output_to_operand_aliasing={{0}: (7, {}), {1}: (8, {}), {2}: (9, {})} | custom-call | flops 31457280 | bytes 5242880 | tf_op jit(solution)/shard_map/first/pallas_call | solution.py:518
  37.9 0.0 collective-permute-done.6.ha_ref
  37.9 0.0 collective-permute-done.7.hb_ref
  37.9 3.9 %first.6 = (f32[4,24,256]{2,1,0:T(8,128)S(1)}, f32[128,16,256]{2,1,0:T(8,128)S(1)}, bf16[4,128,8,256]{3,2,1,0:T(8,128)(2,1)S(1)}) custom-call(f32[7]{0:T(128)S(1)} %copy-done.5, s32[2,7]{1,0:T(2,128)S(1)} %bitcast.10, s32[2]{0:T(128)S(1)} %copy-done.3, ...), custom_call_target="tpu_custom_call", output_to_operand_aliasing={{0}: (7, {}), {1}: (8, {}), {2}: (9, {})} | custom-call | flops 31457280 | bytes 5242880 | tf_op jit(solution)/shard_map/first/pallas_call | solution.py:518
  41.9 0.0 collective-permute-done.4.ha_ref
  41.9 0.0 collective-permute-done.5.hb_ref
  41.9 3.9 %first.7 = (f32[4,24,256]{2,1,0:T(8,128)S(1)}, f32[128,16,256]{2,1,0:T(8,128)S(1)}, bf16[4,128,8,256]{3,2,1,0:T(8,128)(2,1)S(1)}) custom-call(f32[7]{0:T(128)S(1)} %copy-done.5, s32[2,7]{1,0:T(2,128)S(1)} %bitcast.11, s32[2]{0:T(128)S(1)} %copy-done.3, ...), custom_call_target="tpu_custom_call", output_to_operand_aliasing={{0}: (7, {}), {1}: (8, {}), {2}: (9, {})} | custom-call | flops 31457280 | bytes 5242880 | tf_op jit(solution)/shard_map/first/pallas_call | solution.py:518
  45.8 1.6 %collective-permute-start.10 = (f32[4,24,256]{2,1,0:T(8,128)S(1)}, f32[4,24,256]{2,1,0:T(8,128)S(1)}, u32[]{:S(2)}, u32[]{:S(2)}) collective-permute-start(f32[4,24,256]{2,1,0:T(8,128)S(1)} %get-tuple-element.78.f_ref), channel_id=1, source_target_pairs={{0,16},{16,0},{1,17},{17,1},{2,18},{18,2},{3,19},{19,3},{4,20},{20... | collective-permute-start | bytes 294920 | tf_op jit(solution)/shard_map/ppermute | solution.py:480
  47.4 3.1 %collective-permute-done.10.r_ref = f32[4,24,256]{2,1,0:T(8,128)S(1)} collective-permute-done((f32[4,24,256]{2,1,0:T(8,128)S(1)}, f32[4,24,256]{2,1,0:T(8,128)S(1)}, u32[]{:S(2)}, u32[]{:S(2)}) %collective-permute-start.10) | collective-permute-done | bytes 98336 | tf_op jit(solution)/shard_map/ppermute | solution.py:480
  50.5 0.6 mid.3
  51.1 2.9 %collective-permute-start.11 = (f32[4,8,256]{2,1,0:T(8,128)S(1)}, f32[4,8,256]{2,1,0:T(8,128)S(1)}, u32[]{:S(2)}, u32[]{:S(2)}) collective-permute-start(f32[4,8,256]{2,1,0:T(8,128)S(1)} %get-tuple-element.80), channel_id=1, source_target_pairs={{0,1},{1,0},{2,3},{3,2},{4,5},{5,4},{6,7},{7,6},{8,9},{9,8},{10,11... | collective-permute-start | bytes 98312 | tf_op jit(solution)/shard_map/ppermute | solution.py:410
  54.0 0.7 collective-permute-start.12
  54.7 0.2 collective-permute-done.11.a_ref
  54.9 12.8 %next.2 = (f32[128,16,256]{2,1,0:T(8,128)S(1)}, f32[4,24,256]{2,1,0:T(8,128)S(1)}, f32[4,16,256]{2,1,0:T(8,128)S(1)}, f32[4,24,256]{2,1,0:T(8,128)S(1)}, f32[2,8,128]{2,1,0:T(8,128)S(1)}) custom-call(f32[7]{0:T(128)S(1)} %copy-done.5, s32[2,7]{1,0:T(2,128)S(1)} %bitcast.12, s32[2]{0:T(128)S(1)} %copy-done.3, bf16[4,128,16,256]{3,2,1,0:T(8,128)(2,1)S(1)} %copy-done.1, ...), custom_call_target="tpu_custom_call" | custom-call | flops 31457280 | bytes 5242880 | tf_op jit(solution)/shard_map/next/pallas_call | solution.py:527
  67.6 1.6 %collective-permute-start.13 = (f32[4,24,256]{2,1,0:T(8,128)S(1)}, f32[4,24,256]{2,1,0:T(8,128)S(1)}, u32[]{:S(2)}, u32[]{:S(2)}) collective-permute-start(f32[4,24,256]{2,1,0:T(8,128)S(1)} %get-tuple-element.83.f_ref), channel_id=1, source_target_pairs={{0,16},{16,0},{1,17},{17,1},{2,18},{18,2},{3,19},{19,3},{4,20},{20... | collective-permute-start | bytes 294920 | tf_op jit(solution)/shard_map/ppermute | solution.py:480
  69.2 3.1 %collective-permute-done.13.r_ref = f32[4,24,256]{2,1,0:T(8,128)S(1)} collective-permute-done((f32[4,24,256]{2,1,0:T(8,128)S(1)}, f32[4,24,256]{2,1,0:T(8,128)S(1)}, u32[]{:S(2)}, u32[]{:S(2)}) %collective-permute-start.13) | collective-permute-done | bytes 98336 | tf_op jit(solution)/shard_map/ppermute | solution.py:480
  72.3 0.6 mid.4
  72.9 3.4 %collective-permute-start.14 = (f32[4,8,256]{2,1,0:T(8,128)S(1)}, f32[4,8,256]{2,1,0:T(8,128)S(1)}, u32[]{:S(2)}, u32[]{:S(2)}) collective-permute-start(f32[4,8,256]{2,1,0:T(8,128)S(1)} %get-tuple-element.85), channel_id=1, source_target_pairs={{0,1},{1,0},{2,3},{3,2},{4,5},{5,4},{6,7},{7,6},{8,9},{9,8},{10,11... | collective-permute-start | bytes 98312 | tf_op jit(solution)/shard_map/ppermute | solution.py:410
  76.3 0.8 collective-permute-start.15
  77.2 0.0 collective-permute-done.14.a_ref
  77.2 0.0 collective-permute-done.15.b_ref
  77.2 12.8 %next.3 = (f32[128,16,256]{2,1,0:T(8,128)S(1)}, f32[4,24,256]{2,1,0:T(8,128)S(1)}, f32[4,16,256]{2,1,0:T(8,128)S(1)}, f32[4,24,256]{2,1,0:T(8,128)S(1)}, f32[2,8,128]{2,1,0:T(8,128)S(1)}) custom-call(f32[7]{0:T(128)S(1)} %copy-done.5, s32[2,7]{1,0:T(2,128)S(1)} %bitcast.13, s32[2]{0:T(128)S(1)} %copy-done.3, bf16[4,128,16,256]{3,2,1,0:T(8,128)(2,1)S(1)} %copy-done.1, ...), custom_call_target="tpu_custom_call" | custom-call | flops 31457280 | bytes 5242880 | tf_op jit(solution)/shard_map/next/pallas_call | solution.py:527
  90.0 1.6 %collective-permute-start.16 = (f32[4,24,256]{2,1,0:T(8,128)S(1)}, f32[4,24,256]{2,1,0:T(8,128)S(1)}, u32[]{:S(2)}, u32[]{:S(2)}) collective-permute-start(f32[4,24,256]{2,1,0:T(8,128)S(1)} %get-tuple-element.88.f_ref), channel_id=1, source_target_pairs={{0,16},{16,0},{1,17},{17,1},{2,18},{18,2},{3,19},{19,3},{4,20},{20... | collective-permute-start | bytes 294920 | tf_op jit(solution)/shard_map/ppermute | solution.py:480
  91.6 3.1 %collective-permute-done.16.r_ref = f32[4,24,256]{2,1,0:T(8,128)S(1)} collective-permute-done((f32[4,24,256]{2,1,0:T(8,128)S(1)}, f32[4,24,256]{2,1,0:T(8,128)S(1)}, u32[]{:S(2)}, u32[]{:S(2)}) %collective-permute-start.16) | collective-permute-done | bytes 98336 | tf_op jit(solution)/shard_map/ppermute | solution.py:480
  94.7 0.6 mid.5
  95.3 5.3 %collective-permute-start.17 = (f32[4,8,256]{2,1,0:T(8,128)S(1)}, f32[4,8,256]{2,1,0:T(8,128)S(1)}, u32[]{:S(2)}, u32[]{:S(2)}) collective-permute-start(f32[4,8,256]{2,1,0:T(8,128)S(1)} %get-tuple-element.90), channel_id=1, source_target_pairs={{0,1},{1,0},{2,3},{3,2},{4,5},{5,4},{6,7},{7,6},{8,9},{9,8},{10,11... | collective-permute-start | bytes 98312 | tf_op jit(solution)/shard_map/ppermute | solution.py:410
  100.6 0.7 collective-permute-start.18
  101.3 0.2 collective-permute-done.17.a_ref
  101.5 0.0 collective-permute-done.18.b_ref
  101.5 0.6 last.1
  102.0 6.5 %collective-permute-start.19 = (f32[8,128]{1,0:T(8,128)S(1)}, f32[8,128]{1,0:T(8,128)S(1)}, u32[]{:S(2)}, u32[]{:S(2)}) collective-permute-start(f32[8,128]{1,0:T(8,128)S(1)} %get-tuple-element.95), channel_id=1, source_target_pairs={{0,1},{1,0},{2,3},{3,2},{4,5},{5,4},{6,7},{7,6},{8,9},{9,8},{10,11... | collective-permute-start | bytes 12296 | tf_op jit(solution)/shard_map/ppermute | solution.py:558
  108.6 0.8 collective-permute-done.19
  109.4 2.9 %collective-permute-start.20 = (f32[8,128]{1,0:T(8,128)S(1)}, f32[8,128]{1,0:T(8,128)S(1)}, u32[]{:S(2)}, u32[]{:S(2)}) collective-permute-start(f32[8,128]{1,0:T(8,128)S(1)} %add.17), channel_id=1, source_target_pairs={{0,2},{1,3},{2,0},{3,1},{4,6},{5,7},{6,4},{7,5},{8,10},{9,11},{10,... | collective-permute-start | bytes 12296 | tf_op jit(solution)/shard_map/ppermute | solution.py:558
  112.3 1.6 %collective-permute-done.20 = f32[8,128]{1,0:T(8,128)S(1)} collective-permute-done((f32[8,128]{1,0:T(8,128)S(1)}, f32[8,128]{1,0:T(8,128)S(1)}, u32[]{:S(2)}, u32[]{:S(2)}) %collective-permute-start.20) | collective-permute-done | bytes 4128 | tf_op jit(solution)/shard_map/ppermute | solution.py:558
  113.9 3.5 %collective-permute-start.21 = (f32[8,128]{1,0:T(8,128)S(1)}, f32[8,128]{1,0:T(8,128)S(1)}, u32[]{:S(2)}, u32[]{:S(2)}) collective-permute-start(f32[8,128]{1,0:T(8,128)S(1)} %add.18), channel_id=1, source_target_pairs={{0,4},{1,5},{2,6},{3,7},{4,0},{5,1},{6,2},{7,3},{8,12},{9,13},{10,... | collective-permute-start | bytes 12296 | tf_op jit(solution)/shard_map/ppermute | solution.py:558
  117.4 1.6 %collective-permute-done.21 = f32[8,128]{1,0:T(8,128)S(1)} collective-permute-done((f32[8,128]{1,0:T(8,128)S(1)}, f32[8,128]{1,0:T(8,128)S(1)}, u32[]{:S(2)}, u32[]{:S(2)}) %collective-permute-start.21) | collective-permute-done | bytes 4128 | tf_op jit(solution)/shard_map/ppermute | solution.py:558
  119.0 2.4 %collective-permute-start.22 = (f32[8,128]{1,0:T(8,128)S(1)}, f32[8,128]{1,0:T(8,128)S(1)}, u32[]{:S(2)}, u32[]{:S(2)}) collective-permute-start(f32[8,128]{1,0:T(8,128)S(1)} %add.19), channel_id=1, source_target_pairs={{0,8},{1,9},{2,10},{3,11},{4,12},{5,13},{6,14},{7,15},{8,0},{9,1},... | collective-permute-start | bytes 12296 | tf_op jit(solution)/shard_map/ppermute | solution.py:558
  121.4 2.1 %collective-permute-done.22 = f32[8,128]{1,0:T(8,128)S(1)} collective-permute-done((f32[8,128]{1,0:T(8,128)S(1)}, f32[8,128]{1,0:T(8,128)S(1)}, u32[]{:S(2)}, u32[]{:S(2)}) %collective-permute-start.22) | collective-permute-done | bytes 4128 | tf_op jit(solution)/shard_map/ppermute | solution.py:558
  123.5 2.4 %final.1 = (f32[128,16,256]{2,1,0:T(8,128)}, f32[4,16,256]{2,1,0:T(8,128)}) custom-call(f32[8,128]{1,0:T(8,128)S(1)} %add.20.moment_ref, f32[128,16,256]{2,1,0:T(8,128)S(1)} %get-tuple-element.96.t0_ref, f32[128,16,256]{2,1,0:T(8,128)S(1)} %get-tuple-element.97.t1_ref, f32[128,16,256]{2,1,0:T(8,128)S(1)} %get-tuple-element.98.t2_ref, ...), custom_call_target="tpu_custom_call" | custom-call | tf_op jit(solution)/shard_map/final/pallas_call | solution.py:562
  (13 shorter events, 0.0 us)
Async XLA Ops:
  4.0 2.2 %copy-start = (bf16[4,128,16,256]{3,2,1,0:T(8,128)(2,1)S(1)}, bf16[4,128,16,256]{3,2,1,0:T(8,128)(2,1)}, u32[]{:S(2)}) copy-start(bf16[4,128,16,256]{3,2,1,0:T(8,128)(2,1)} %p_hbm.13) | copy-start | bytes 12582916
  6.2 0.6 copy-start.3
  6.9 20.6 %copy-start.1 = (bf16[4,128,16,256]{3,2,1,0:T(8,128)(2,1)S(1)}, bf16[4,128,16,256]{3,2,1,0:T(8,128)(2,1)}, u32[]{:S(2)}) copy-start(bf16[4,128,16,256]{3,2,1,0:T(8,128)(2,1)} %p_hbm.13) | copy-start | bytes 12582916
  6.9 20.6 %copy-start.4 = (s32[7,2]{0,1:T(2,128)S(1)}, s32[7,2]{0,1:T(2,128)}, u32[]{:S(2)}) copy-start(s32[7,2]{0,1:T(2,128)} %param.10) | copy-start | bytes 172
  6.9 20.7 %copy-start.5 = (f32[7]{0:T(128)S(1)}, f32[7]{0:T(128)}, u32[]{:S(2)}) copy-start(f32[7]{0:T(128)} %weight_ref.11) | copy-start | bytes 88
  9.0 17.8 %collective-permute-start = (bf16[4,32,4,256]{3,2,1,0:T(4,128)(2,1)S(1)}, bf16[4,32,4,256]{3,2,1,0:T(4,128)(2,1)S(1)}, u32[]{:S(2)}, u32[]{:S(2)}) collective-permute-start(bf16[4,32,4,256]{3,2,1,0:T(4,128)(2,1)S(1)} %get-tuple-element.56), channel_id=1, source_target_pairs={{0,1},{1,0},{2,3},{3,2},{4,5},{5,4},{6,7},{7,6},{8,9},{9,8},{10,11... | collective-permute-start | bytes 786440 | tf_op jit(solution)/shard_map/ppermute | solution.py:410
  9.5 18.0 %collective-permute-start.1 = (bf16[4,32,4,256]{3,2,1,0:T(4,128)(2,1)S(1)}, bf16[4,32,4,256]{3,2,1,0:T(4,128)(2,1)S(1)}, u32[]{:S(2)}, u32[]{:S(2)}) collective-permute-start(bf16[4,32,4,256]{3,2,1,0:T(4,128)(2,1)S(1)} %get-tuple-element.57), channel_id=1, source_target_pairs={{1,2},{3,4},{5,6},{7,8},{9,10},{11,12},{13,14},{2,1},{4,3},{6,5},{... | collective-permute-start | bytes 786440 | tf_op jit(solution)/shard_map/ppermute | solution.py:409
  10.2 23.0 %collective-permute-start.8 = (bf16[4,32,4,256]{3,2,1,0:T(4,128)(2,1)S(1)}, bf16[4,32,4,256]{3,2,1,0:T(4,128)(2,1)S(1)}, u32[]{:S(2)}, u32[]{:S(2)}) collective-permute-start(bf16[4,32,4,256]{3,2,1,0:T(4,128)(2,1)S(1)} %get-tuple-element.66), channel_id=1, source_target_pairs={{0,1},{1,0},{2,3},{3,2},{4,5},{5,4},{6,7},{7,6},{8,9},{9,8},{10,11... | collective-permute-start | bytes 786440 | tf_op jit(solution)/shard_map/ppermute | solution.py:410
  14.1 3.6 %collective-permute-start.3 = (f32[2,4,4,256]{3,2,1,0:T(4,128)}, f32[2,4,4,256]{3,2,1,0:T(4,128)S(1)}, u32[]{:S(2)}, u32[]{:S(2)}) collective-permute-start(f32[2,4,4,256]{3,2,1,0:T(4,128)} %get-tuple-element.59), channel_id=1, source_target_pairs={{1,2},{3,4},{5,6},{7,8},{9,10},{11,12},{13,14},{2,1},{4,3},{6,5},{... | collective-permute-start | bytes 98312 | tf_op jit(solution)/shard_map/ppermute | solution.py:409
  14.8 4.0 %collective-permute-start.2 = (f32[2,4,4,256]{3,2,1,0:T(4,128)}, f32[2,4,4,256]{3,2,1,0:T(4,128)S(1)}, u32[]{:S(2)}, u32[]{:S(2)}) collective-permute-start(f32[2,4,4,256]{3,2,1,0:T(4,128)} %get-tuple-element.52), channel_id=1, source_target_pairs={{0,1},{1,0},{2,3},{3,2},{4,5},{5,4},{6,7},{7,6},{8,9},{9,8},{10,11... | collective-permute-start | bytes 98312 | tf_op jit(solution)/shard_map/ppermute | solution.py:410
  17.8 16.2 %collective-permute-start.9 = (bf16[4,32,4,256]{3,2,1,0:T(4,128)(2,1)S(1)}, bf16[4,32,4,256]{3,2,1,0:T(4,128)(2,1)S(1)}, u32[]{:S(2)}, u32[]{:S(2)}) collective-permute-start(bf16[4,32,4,256]{3,2,1,0:T(4,128)(2,1)S(1)} %get-tuple-element.67), channel_id=1, source_target_pairs={{1,2},{3,4},{5,6},{7,8},{9,10},{11,12},{13,14},{2,1},{4,3},{6,5},{... | collective-permute-start | bytes 786440 | tf_op jit(solution)/shard_map/ppermute | solution.py:409
  18.8 19.1 %collective-permute-start.6 = (bf16[4,32,4,256]{3,2,1,0:T(4,128)(2,1)S(1)}, bf16[4,32,4,256]{3,2,1,0:T(4,128)(2,1)S(1)}, u32[]{:S(2)}, u32[]{:S(2)}) collective-permute-start(bf16[4,32,4,256]{3,2,1,0:T(4,128)(2,1)S(1)} %get-tuple-element.64), channel_id=1, source_target_pairs={{0,1},{1,0},{2,3},{3,2},{4,5},{5,4},{6,7},{7,6},{8,9},{9,8},{10,11... | collective-permute-start | bytes 786440 | tf_op jit(solution)/shard_map/ppermute | solution.py:410
  25.3 0.9 copy-start.2
  26.8 11.1 %collective-permute-start.7 = (bf16[4,32,4,256]{3,2,1,0:T(4,128)(2,1)S(1)}, bf16[4,32,4,256]{3,2,1,0:T(4,128)(2,1)S(1)}, u32[]{:S(2)}, u32[]{:S(2)}) collective-permute-start(bf16[4,32,4,256]{3,2,1,0:T(4,128)(2,1)S(1)} %get-tuple-element.65), channel_id=1, source_target_pairs={{1,2},{3,4},{5,6},{7,8},{9,10},{11,12},{13,14},{2,1},{4,3},{6,5},{... | collective-permute-start | bytes 786440 | tf_op jit(solution)/shard_map/ppermute | solution.py:409
  31.5 10.4 %collective-permute-start.4 = (bf16[4,32,4,256]{3,2,1,0:T(4,128)(2,1)S(1)}, bf16[4,32,4,256]{3,2,1,0:T(4,128)(2,1)S(1)}, u32[]{:S(2)}, u32[]{:S(2)}) collective-permute-start(bf16[4,32,4,256]{3,2,1,0:T(4,128)(2,1)S(1)} %get-tuple-element.62), channel_id=1, source_target_pairs={{0,1},{1,0},{2,3},{3,2},{4,5},{5,4},{6,7},{7,6},{8,9},{9,8},{10,11... | collective-permute-start | bytes 786440 | tf_op jit(solution)/shard_map/ppermute | solution.py:410
  33.3 8.6 %collective-permute-start.5 = (bf16[4,32,4,256]{3,2,1,0:T(4,128)(2,1)S(1)}, bf16[4,32,4,256]{3,2,1,0:T(4,128)(2,1)S(1)}, u32[]{:S(2)}, u32[]{:S(2)}) collective-permute-start(bf16[4,32,4,256]{3,2,1,0:T(4,128)(2,1)S(1)} %get-tuple-element.63), channel_id=1, source_target_pairs={{1,2},{3,4},{5,6},{7,8},{9,10},{11,12},{13,14},{2,1},{4,3},{6,5},{... | collective-permute-start | bytes 786440 | tf_op jit(solution)/shard_map/ppermute | solution.py:409
  45.8 4.7 %collective-permute-start.10 = (f32[4,24,256]{2,1,0:T(8,128)S(1)}, f32[4,24,256]{2,1,0:T(8,128)S(1)}, u32[]{:S(2)}, u32[]{:S(2)}) collective-permute-start(f32[4,24,256]{2,1,0:T(8,128)S(1)} %get-tuple-element.78.f_ref), channel_id=1, source_target_pairs={{0,16},{16,0},{1,17},{17,1},{2,18},{18,2},{3,19},{19,3},{4,20},{20... | collective-permute-start | bytes 294920 | tf_op jit(solution)/shard_map/ppermute | solution.py:480
  51.1 3.8 %collective-permute-start.11 = (f32[4,8,256]{2,1,0:T(8,128)S(1)}, f32[4,8,256]{2,1,0:T(8,128)S(1)}, u32[]{:S(2)}, u32[]{:S(2)}) collective-permute-start(f32[4,8,256]{2,1,0:T(8,128)S(1)} %get-tuple-element.80), channel_id=1, source_target_pairs={{0,1},{1,0},{2,3},{3,2},{4,5},{5,4},{6,7},{7,6},{8,9},{9,8},{10,11... | collective-permute-start | bytes 98312 | tf_op jit(solution)/shard_map/ppermute | solution.py:410
  54.0 0.9 collective-permute-start.12
  67.6 4.7 %collective-permute-start.13 = (f32[4,24,256]{2,1,0:T(8,128)S(1)}, f32[4,24,256]{2,1,0:T(8,128)S(1)}, u32[]{:S(2)}, u32[]{:S(2)}) collective-permute-start(f32[4,24,256]{2,1,0:T(8,128)S(1)} %get-tuple-element.83.f_ref), channel_id=1, source_target_pairs={{0,16},{16,0},{1,17},{17,1},{2,18},{18,2},{3,19},{19,3},{4,20},{20... | collective-permute-start | bytes 294920 | tf_op jit(solution)/shard_map/ppermute | solution.py:480
  72.9 4.3 %collective-permute-start.14 = (f32[4,8,256]{2,1,0:T(8,128)S(1)}, f32[4,8,256]{2,1,0:T(8,128)S(1)}, u32[]{:S(2)}, u32[]{:S(2)}) collective-permute-start(f32[4,8,256]{2,1,0:T(8,128)S(1)} %get-tuple-element.85), channel_id=1, source_target_pairs={{0,1},{1,0},{2,3},{3,2},{4,5},{5,4},{6,7},{7,6},{8,9},{9,8},{10,11... | collective-permute-start | bytes 98312 | tf_op jit(solution)/shard_map/ppermute | solution.py:410
  76.3 0.9 collective-permute-start.15
  90.0 4.7 %collective-permute-start.16 = (f32[4,24,256]{2,1,0:T(8,128)S(1)}, f32[4,24,256]{2,1,0:T(8,128)S(1)}, u32[]{:S(2)}, u32[]{:S(2)}) collective-permute-start(f32[4,24,256]{2,1,0:T(8,128)S(1)} %get-tuple-element.88.f_ref), channel_id=1, source_target_pairs={{0,16},{16,0},{1,17},{17,1},{2,18},{18,2},{3,19},{19,3},{4,20},{20... | collective-permute-start | bytes 294920 | tf_op jit(solution)/shard_map/ppermute | solution.py:480
  95.3 6.2 %collective-permute-start.17 = (f32[4,8,256]{2,1,0:T(8,128)S(1)}, f32[4,8,256]{2,1,0:T(8,128)S(1)}, u32[]{:S(2)}, u32[]{:S(2)}) collective-permute-start(f32[4,8,256]{2,1,0:T(8,128)S(1)} %get-tuple-element.90), channel_id=1, source_target_pairs={{0,1},{1,0},{2,3},{3,2},{4,5},{5,4},{6,7},{7,6},{8,9},{9,8},{10,11... | collective-permute-start | bytes 98312 | tf_op jit(solution)/shard_map/ppermute | solution.py:410
  100.6 0.9 collective-permute-start.18
  102.0 7.4 %collective-permute-start.19 = (f32[8,128]{1,0:T(8,128)S(1)}, f32[8,128]{1,0:T(8,128)S(1)}, u32[]{:S(2)}, u32[]{:S(2)}) collective-permute-start(f32[8,128]{1,0:T(8,128)S(1)} %get-tuple-element.95), channel_id=1, source_target_pairs={{0,1},{1,0},{2,3},{3,2},{4,5},{5,4},{6,7},{7,6},{8,9},{9,8},{10,11... | collective-permute-start | bytes 12296 | tf_op jit(solution)/shard_map/ppermute | solution.py:558
  109.4 4.5 %collective-permute-start.20 = (f32[8,128]{1,0:T(8,128)S(1)}, f32[8,128]{1,0:T(8,128)S(1)}, u32[]{:S(2)}, u32[]{:S(2)}) collective-permute-start(f32[8,128]{1,0:T(8,128)S(1)} %add.17), channel_id=1, source_target_pairs={{0,2},{1,3},{2,0},{3,1},{4,6},{5,7},{6,4},{7,5},{8,10},{9,11},{10,... | collective-permute-start | bytes 12296 | tf_op jit(solution)/shard_map/ppermute | solution.py:558
  113.9 5.1 %collective-permute-start.21 = (f32[8,128]{1,0:T(8,128)S(1)}, f32[8,128]{1,0:T(8,128)S(1)}, u32[]{:S(2)}, u32[]{:S(2)}) collective-permute-start(f32[8,128]{1,0:T(8,128)S(1)} %add.18), channel_id=1, source_target_pairs={{0,4},{1,5},{2,6},{3,7},{4,0},{5,1},{6,2},{7,3},{8,12},{9,13},{10,... | collective-permute-start | bytes 12296 | tf_op jit(solution)/shard_map/ppermute | solution.py:558
  119.0 4.5 %collective-permute-start.22 = (f32[8,128]{1,0:T(8,128)S(1)}, f32[8,128]{1,0:T(8,128)S(1)}, u32[]{:S(2)}, u32[]{:S(2)}) collective-permute-start(f32[8,128]{1,0:T(8,128)S(1)} %add.19), channel_id=1, source_target_pairs={{0,8},{1,9},{2,10},{3,11},{4,12},{5,13},{6,14},{7,15},{8,0},{9,1},... | collective-permute-start | bytes 12296 | tf_op jit(solution)/shard_map/ppermute | solution.py:558
